TPU v7x, 32 devices: a whole 2x2x4 slice. The times are simulated.
32 devices in a mesh: blk: 8 (over z, x), rep: 4 (over y, core).
Axes of the slice: x: 2, y: 2, z: 4, core: 2. Of those that a mesh axis runs over, the one named last changes fastest.
Arguments:
- points: bfloat16 [6144, 1024], P('blk'), may hold values from -6 to 6
- w_in: bfloat16 [1024, 512], replicated, may hold values from -0.1875 to 0.1875
- b_in: float32 [512], replicated, may hold values from -3 to 3
- w_out: bfloat16 [512, 64], replicated, may hold values from -0.25 to 0.25
- inv_scale: float32 [64], replicated, may hold values from 0.05 to 0.5
- solves: bfloat16 [64, 6144], P(None, 'blk'), may hold values from -1.6875 to 1.6875
- probes: bfloat16 [64, 6144], P(None, 'blk'), may hold values from -1.6875 to 1.6875
Outputs:
- feat_grad: float32 [64, 6144], P(None, ('blk', 'rep'))
- grad_w_in: float32 [1024, 512], replicated
- grad_b_in: float32 [512], replicated
- grad_w_out: float32 [512, 64], replicated
All inputs are finite; a program needn't handle non-finite values.
Results may differ from a plain program's by a relative error of at most 0.034.
Values may be sent and summed in bfloat16 or wider, within the bound.
No kernel may reach another device: no remote copies, remote signals or barrier semaphores. Data moves between devices by JAX's collectives and lax.ppermute only.
A program may use at most 64 MiB of HBM per device.

v0:
```python
import math

import jax
import jax.numpy as jnp
from jax import lax
from jax.sharding import PartitionSpec as P


def shifted(block, axis, distance):
    devices = range(lax.axis_size(axis))
    route = [((i - distance) % len(devices), i) for i in devices]
    return lax.ppermute(block, axis, route)


def couple(own_y, own_pair, own_sq, visitor, feat):
    vis_y = visitor[:feat]
    vis_pair = visitor[feat:]
    vis_sq = jnp.sum(jnp.square(vis_y.astype(jnp.float32)), axis=0)
    cross = lax.dot_general(
        own_y, vis_y, (((0,), (0,)), ((), ())), preferred_element_type=jnp.float32
    )
    kernel = jnp.exp(-0.5 * (own_sq[:, None] + vis_sq[None, :] - 2.0 * cross))
    coupling = lax.dot_general(
        own_pair, vis_pair, (((0,), (0,)), ((), ())), preferred_element_type=jnp.float32
    )
    weight_b = (coupling * kernel).astype(jnp.bfloat16)
    totals = jnp.sum(weight_b.astype(jnp.float32), axis=1)
    pull = lax.dot_general(
        vis_y, weight_b, (((1,), (1,)), ((), ())), preferred_element_type=jnp.float32
    )
    return (totals, pull)


def on_device(points, w_in, b_in, w_out, inv_scale, solves, probes):
    feat = w_out.shape[1]
    reps = lax.axis_size("rep")
    blocks = lax.axis_size("blk")
    rep_index = lax.axis_index("rep")
    rows = points.shape[0]
    quarter = rows // reps
    first = rep_index * quarter
    npts = rows * blocks
    levels = reps.bit_length() - 1
    own_points = lax.dynamic_slice_in_dim(points, first, quarter, 0)
    hidden = jnp.tanh(jnp.dot(points, w_in, preferred_element_type=jnp.float32) + b_in).astype(
        jnp.bfloat16
    )
    pre = lax.dot_general(
        w_out, hidden, (((0,), (1,)), ((), ())), preferred_element_type=jnp.float32
    )
    hidden, scaled = (hidden, (pre * inv_scale[:, None]).astype(jnp.bfloat16))
    own_hidden = lax.dynamic_slice_in_dim(hidden, first, quarter, 0)
    own_pair = jnp.concatenate([solves, probes], axis=0)
    own_sq = jnp.sum(jnp.square(scaled.astype(jnp.float32)), axis=0)
    scaled32 = scaled.astype(jnp.float32)
    visitor = jnp.concatenate([scaled, probes, solves], axis=0)
    for bit in range(levels):
        moved = shifted(visitor, "blk", -(1 << bit))
        visitor = jnp.where(rep_index // (1 << bit) % 2 == 1, moved, visitor)

    def accumulate(state, vis):
        totals, pull = couple(scaled, own_pair, own_sq, vis, feat)
        return (state[0] + totals, state[1] + pull)

    init = (jnp.zeros((rows,), jnp.float32), jnp.zeros((feat, rows), jnp.float32))
    steps = blocks // reps

    def advance(index, carry):
        state, vis = carry
        state = accumulate(state, vis)
        return (state, shifted(vis, "blk", -reps))

    state, last_vis = lax.fori_loop(0, steps - 1, advance, (init, visitor))
    state = accumulate(state, last_vis)
    totals, pull = state
    drift = pull - scaled32 * totals[None, :]
    summed = lax.psum_scatter(drift, "rep", scatter_dimension=1, tiled=True)
    feat_grad = summed * inv_scale[:, None]
    grad_b16 = feat_grad.astype(jnp.bfloat16)
    back = lax.dot_general(
        grad_b16, w_out, (((0,), (1,)), ((), ())), preferred_element_type=jnp.float32
    )
    hid32 = own_hidden.astype(jnp.float32)
    pre_grad = back * (1.0 - hid32 * hid32)
    norm = 1.0 / math.sqrt(npts)
    term_w_in = (
        lax.dot_general(
            own_points,
            pre_grad.astype(jnp.bfloat16),
            (((0,), (0,)), ((), ())),
            preferred_element_type=jnp.float32,
        )
        * norm
    )
    term_b_in = jnp.sum(pre_grad, axis=0) * norm
    term_w_out = (
        lax.dot_general(
            own_hidden, grad_b16, (((0,), (1,)), ((), ())), preferred_element_type=jnp.float32
        )
        * norm
    )
    grad_w_in, grad_b_in, grad_w_out = lax.psum((term_w_in, term_b_in, term_w_out), ("blk", "rep"))
    return (feat_grad, grad_w_in, grad_b_in, grad_w_out)


def solution(mesh):
    in_specs = (P("blk", None), P(), P(), P(), P(), P(None, "blk"), P(None, "blk"))
    out_specs = (P(None, ("blk", "rep")), P(), P(), P())
    return jax.shard_map(
        on_device, mesh=mesh, in_specs=in_specs, out_specs=out_specs, check_vma=False
    )
```

profile of v0, /device:TPU:0, one launch (start us, length us, event | category | flops | bytes accessed | tf_op | source)
XLA Modules:
  0.0 224.5 jit_solution(10279714449616067677)
XLA Ops:
  7.2 0.0 copy-start
  7.2 0.0 copy-start.6
  7.2 0.0 copy-start.5
  7.2 0.0 copy-start.1
  7.2 0.0 copy-start.2
  7.2 0.0 reduce-scatter.4.cloned.1.call-start
  7.3 1.3 copy-done
  8.6 2.2 tanh_convert_fusion
  10.8 0.0 copy-done.6
  10.8 0.0 copy-done.5
  10.8 0.4 fusion.3
  11.2 0.0 copy-done.1
  11.2 0.0 copy-done.2
  11.2 6.1 %collective-permute-start = (bf16[192,768]{1,0:T(8,128)(2,1)S(1)}, bf16[192,768]{1,0:T(8,128)(2,1)S(1)}, u32[]{:S(2)}, u32[]{:S(2)}) collective-permute-start(bf16[192,768]{1,0:T(8,128)(2,1)S(1)} %pad_maximum_fusion), channel_id=1, source_target_pairs={{4,0},{8,4},{12,8},{16,12},{20,16},{24,20},{28,24},{0,28},{5,1},{9... | collective-permute-start | bytes 884744 | tf_op jit(solution)/shard_map/ppermute | solution.py:12
  17.3 6.3 %collective-permute-done = bf16[192,768]{1,0:T(8,128)(2,1)S(1)} collective-permute-done((bf16[192,768]{1,0:T(8,128)(2,1)S(1)}, bf16[192,768]{1,0:T(8,128)(2,1)S(1)}, u32[]{:S(2)}, u32[]{:S(2)}) %collective-permute-start) | collective-permute-done | bytes 294944 | tf_op jit(solution)/shard_map/ppermute | solution.py:12
  23.6 0.1 broadcast_select_fusion
  23.6 1.6 collective-permute-start.1
  25.3 6.3 %collective-permute-done.1 = bf16[192,768]{1,0:T(8,128)(2,1)S(1)} collective-permute-done((bf16[192,768]{1,0:T(8,128)(2,1)S(1)}, bf16[192,768]{1,0:T(8,128)(2,1)S(1)}, u32[]{:S(2)}, u32[]{:S(2)}) %collective-permute-start.1) | collective-permute-done | bytes 294944 | tf_op jit(solution)/shard_map/ppermute | solution.py:12
  31.6 0.6 collective-permute-start.2
  32.3 0.5 fusion.13
  32.8 0.9 convert_reduce_fusion.1
  33.7 12.2 %collective-permute-done.2 = bf16[192,768]{1,0:T(8,128)(2,1)S(1)} collective-permute-done((bf16[192,768]{1,0:T(8,128)(2,1)S(1)}, bf16[192,768]{1,0:T(8,128)(2,1)S(1)}, u32[]{:S(2)}, u32[]{:S(2)}) %collective-permute-start.2) | collective-permute-done | bytes 294944 | tf_op jit(solution)/shard_map/while/body/eval_jaxpr/ppermute | solution.py:12
  46.0 0.5 fusion.10
  46.5 0.9 convert_reduce_fusion
  47.4 0.3 fusion.8
  47.8 0.3 fusion
  48.1 0.9 copy.11
  49.0 0.0 reduce-scatter.4.cloned.1.call-update
  49.1 0.0 all-reduce.3.cloned.1.call-start
  49.1 22.9 %reduce-scatter.4.cloned.1.call-done = f32[192,64]{1,0:T(8,128)} async-done(((f32[768,64]{1,0:T(8,128)}), f32[192,64]{1,0:T(8,128)}) %reduce-scatter.4.cloned.1.call-update) | async-done | bytes 49168
  72.0 1.0 copy.12
  73.0 0.1 broadcast_multiply_fusion
  73.0 0.0 copy-start.3
  73.0 0.3 fusion.19
  73.3 0.8 convolution_multiply_fusion.3
  74.1 1.8 convolution_multiply_fusion
  75.9 0.0 all-reduce.3.cloned.1.call-update
  75.9 0.0 copy-done.3
  76.0 39.6 %psum.22 = f32[512]{0:T(512)} all-reduce(f32[512]{0:T(512)S(1)} %broadcast_multiply_fusion.1), channel_id=1, replica_groups=mesh['blk'=8,'rep'=4] {'blk','rep'}, use_global_device_ids=true, to_apply=%region_8.9 | all-reduce | flops 512 | bytes 4096 | tf_op jit(solution)/shard_map/psum | solution.py:102
  115.6 98.3 %all-reduce.3.cloned.1.call-done = (f32[1024,512]{1,0:T(8,128)}, f32[512,64]{0,1:T(8,128)}) async-done(((f32[1024,512]{1,0:T(8,128)}, f32[512,64]{0,1:T(8,128)}), (f32[1024,512]{1,0:T(8,128)}, f32[512,64]{0,1:T(8,128)})) %all-reduce.3.cloned.1.call-update) | async-done | bytes 2228240 | tf_op jit(solution)/shard_map/psum | solution.py:102
  213.9 0.0 copy-start.4
  213.9 3.1 %copy.16 = f32[1024,512]{1,0:T(8,128)} copy(f32[1024,512]{1,0:T(8,128)} %get-tuple-element.38) | data formatting | bytes 4194304
  217.0 0.0 copy-done.4
  217.0 0.7 copy.17
  (8 shorter events, 0.1 us)
Async XLA Ops:
  7.2 1.4 copy-start
  7.2 3.6 %copy-start.6 = (f32[64]{0:T(128)S(1)}, f32[64]{0:T(128)}, u32[]{:S(2)}) copy-start(f32[64]{0:T(128)} %param.11) | copy-start | bytes 772
  7.2 3.6 %copy-start.5 = (bf16[512,64]{0,1:T(8,128)(2,1)S(1)}, bf16[512,64]{0,1:T(8,128)(2,1)}, u32[]{:S(2)}) copy-start(bf16[512,64]{0,1:T(8,128)(2,1)} %param.10) | copy-start | bytes 196612
  7.2 4.0 %copy-start.1 = (bf16[64,768]{1,0:T(8,128)(2,1)S(1)}, bf16[64,768]{1,0:T(8,128)(2,1)}, u32[]{:S(2)}) copy-start(bf16[64,768]{1,0:T(8,128)(2,1)} %param.12) | copy-start | bytes 294916
  7.2 4.0 %copy-start.2 = (bf16[64,768]{1,0:T(8,128)(2,1)S(1)}, bf16[64,768]{1,0:T(8,128)(2,1)}, u32[]{:S(2)}) copy-start(bf16[64,768]{1,0:T(8,128)(2,1)} %param.13) | copy-start | bytes 294916
  7.2 64.8 %reduce-scatter.4.cloned.1.call-start = ((), (), s32[]{:S(2)}) async-start(), calls=%async_computation.1 | async-start | bytes 491520
  11.2 12.3 %collective-permute-start = (bf16[192,768]{1,0:T(8,128)(2,1)S(1)}, bf16[192,768]{1,0:T(8,128)(2,1)S(1)}, u32[]{:S(2)}, u32[]{:S(2)}) collective-permute-start(bf16[192,768]{1,0:T(8,128)(2,1)S(1)} %pad_maximum_fusion), channel_id=1, source_target_pairs={{4,0},{8,4},{12,8},{16,12},{20,16},{24,20},{28,24},{0,28},{5,1},{9... | collective-permute-start | bytes 884744 | tf_op jit(solution)/shard_map/ppermute | solution.py:12
  23.6 7.9 %collective-permute-start.1 = (bf16[192,768]{1,0:T(8,128)(2,1)S(1)}, bf16[192,768]{1,0:T(8,128)(2,1)S(1)}, u32[]{:S(2)}, u32[]{:S(2)}) collective-permute-start(bf16[192,768]{1,0:T(8,128)(2,1)S(1)} %broadcast_select_fusion), channel_id=1, source_target_pairs={{8,0},{12,4},{16,8},{20,12},{24,16},{28,20},{0,24},{4,28},{9,1},{1... | collective-permute-start | bytes 884744 | tf_op jit(solution)/shard_map/ppermute | solution.py:12
  31.6 14.3 %collective-permute-start.2 = (bf16[192,768]{1,0:T(8,128)(2,1)S(1)}, bf16[192,768]{1,0:T(8,128)(2,1)S(1)}, u32[]{:S(2)}, u32[]{:S(2)}) collective-permute-start(bf16[192,768]{1,0:T(8,128)(2,1)S(1)} %broadcast_select_fusion.1), channel_id=1, source_target_pairs={{16,0},{20,4},{24,8},{28,12},{0,16},{4,20},{8,24},{12,28},{17,1},{... | collective-permute-start | bytes 884744 | tf_op jit(solution)/shard_map/while/body/eval_jaxpr/ppermute | solution.py:12
  49.1 164.8 %all-reduce.3.cloned.1.call-start = ((), (), s32[]{:S(2)}) async-start(), calls=%async_computation.2 | async-start | bytes 4456448 | tf_op jit(solution)/shard_map/psum | solution.py:102
  73.0 2.9 %copy-start.3 = (f32[64,192]{1,0:T(8,128)}, f32[64,192]{1,0:T(8,128)S(1)}, u32[]{:S(2)}) copy-start(f32[64,192]{1,0:T(8,128)S(1)} %broadcast_multiply_fusion) | copy-start | bytes 147460
  213.9 3.1 %copy-start.4 = (f32[512,64]{0,1:T(8,128)S(1)}, f32[512,64]{0,1:T(8,128)}, u32[]{:S(2)}) copy-start(f32[512,64]{0,1:T(8,128)} %get-tuple-element.40) | copy-start | bytes 393220
Sparse Core Ops, SparseCore 0:
  49.2 22.7 reduce-scatter.3
  78.1 135.7 all-reduce.2
where the time goes:
time: 225 us; the launch traced here: 224 us
  waiting for transfers between devices  146 us (65%)
  blocking collectives  39.6 us (18%)
  between operations  14.2 us (6%)
  matrix products  8.95 us (4%)
  starting transfers between devices  8.36 us (4%)
  local copies, waits for them, and re-layouts  7.02 us (3%)
    psum x1, waiting for transfers between devices, on_device(): lax.psum((term_w_in, term_b_in, term_w_out), ('blk', 'rep'))  98.3 us
    psum x1, blocking collectives, on_device(): lax.psum((term_w_in, term_b_in, term_w_out), ('blk', 'rep'))  39.6 us
    ppermute x3, waiting for transfers between devices, shifted(): return lax.ppermute(block, axis, route)  24.8 us
    unnamed x3, waiting for transfers between devices  22.9 us
    ppermute x3, starting transfers between devices, shifted(): return lax.ppermute(block, axis, route)  8.29 us
    unnamed x19, local copies, waits for them, and re-layouts  7.01 us
  transfers between devices with their start and end apart: 5, of which 5 were waited for; matrix products, arithmetic and copies ran while one was open for 1% of the time, Pallas kernels for 0%

commit v1 on v0

v1 whole, which is shorter than its diff:
```python
import math

import jax
import jax.numpy as jnp
from jax import lax
from jax.sharding import PartitionSpec as P

AXES = ("blk", "rep")
BF16 = jnp.bfloat16
F32 = jnp.float32


def bits_of(count):
    return count.bit_length() - 1


def visit_mask(step, rep, blocks, reps):
    low = (bits_of(reps) + 1) // 2
    high = bits_of(reps) - low
    near, far = divmod(rep, 1 << high)
    return far * (blocks >> high) + step * (1 << low) + near


def fetch(array, masks, blocks, reps):
    route = [((b ^ masks[r]) * reps + r, b * reps + r) for b in range(blocks) for r in range(reps)]
    return lax.ppermute(array, AXES, route)


def swap(array, blk_mask, rep_mask, blocks, reps):
    route = [
        (b * reps + r, (b ^ blk_mask) * reps + (r ^ rep_mask))
        for b in range(blocks)
        for r in range(reps)
    ]
    return lax.ppermute(array, AXES, route)


def couple(own_y, own_pair, own_sq, visitor, feat):
    vis_y = visitor[:feat]
    vis_pair = visitor[feat:]
    vis_sq = jnp.sum(jnp.square(vis_y.astype(F32)), axis=0)
    cross = lax.dot_general(own_y, vis_y, (((0,), (0,)), ((), ())), preferred_element_type=F32)
    kernel = jnp.exp(-0.5 * (own_sq[:, None] + vis_sq[None, :] - 2.0 * cross))
    coupling = lax.dot_general(
        own_pair, vis_pair, (((0,), (0,)), ((), ())), preferred_element_type=F32
    )
    weight_b = (coupling * kernel).astype(BF16)
    totals = jnp.sum(weight_b.astype(F32), axis=1)
    pull = lax.dot_general(vis_y, weight_b, (((1,), (1,)), ((), ())), preferred_element_type=F32)
    return (totals, pull)


def on_device(points, w_in, b_in, w_out, inv_scale, solves, probes):
    feat = w_out.shape[1]
    reps = lax.axis_size("rep")
    blocks = lax.axis_size("blk")
    rep_index = lax.axis_index("rep")
    blk_index = lax.axis_index("blk")
    rows, din = points.shape
    hid = w_in.shape[1]
    npts = rows * blocks
    quarter = rows // reps
    cols = hid // reps

    hidden = jnp.tanh(jnp.dot(points, w_in, preferred_element_type=F32) + b_in).astype(BF16)
    pre = lax.dot_general(w_out, hidden, (((0,), (1,)), ((), ())), preferred_element_type=F32)
    scaled = (pre * inv_scale[:, None]).astype(BF16)
    own_sq = jnp.sum(jnp.square(scaled.astype(F32)), axis=0)
    own_pair = jnp.concatenate([solves, probes], axis=0)
    visitor = jnp.concatenate([scaled, probes, solves], axis=0)

    visitors = []
    for step in range(blocks // reps):
        masks = [visit_mask(step, r, blocks, reps) for r in range(reps)]
        visitors.append(fetch(visitor, masks, blocks, reps))
    totals = jnp.zeros((rows,), F32)
    pull = jnp.zeros((feat, rows), F32)
    for vis in visitors:
        more_totals, more_pull = couple(scaled, own_pair, own_sq, vis, feat)
        totals = totals + more_totals
        pull = pull + more_pull
    drift = pull - scaled.astype(F32) * totals[None, :]

    drift = drift + swap(drift, 0, 1, blocks, reps)
    for bit in range(1, bits_of(reps)):
        sent = drift.astype(BF16)
        got = swap(sent, 0, 1 << bit, blocks, reps)
        drift = sent.astype(F32) + got.astype(F32)
    full_grad = drift * inv_scale[:, None]
    feat_grad = lax.dynamic_slice_in_dim(full_grad, rep_index * quarter, quarter, 1)
    grad_b16 = full_grad.astype(BF16)

    first = rep_index * cols
    own_hidden = lax.dynamic_slice_in_dim(hidden, first, cols, 1)
    own_w_out = lax.dynamic_slice_in_dim(w_out, first, cols, 0)
    back = lax.dot_general(
        grad_b16, own_w_out, (((0,), (1,)), ((), ())), preferred_element_type=F32
    )
    hid32 = own_hidden.astype(F32)
    pre_grad = back * (1.0 - hid32 * hid32)
    norm = 1.0 / math.sqrt(npts)
    term_w_in = lax.dot_general(
        points, pre_grad.astype(BF16), (((0,), (0,)), ((), ())), preferred_element_type=F32
    )
    term_b_in = jnp.sum(pre_grad, axis=0)
    term_w_out = lax.dot_general(
        grad_b16, own_hidden, (((1,), (0,)), ((), ())), preferred_element_type=F32
    )
    bias = jnp.broadcast_to(term_b_in[None, None], (2, 16, cols))
    halves = jnp.concatenate(
        [term_w_in.reshape(2, din // 2, cols), term_w_out.reshape(2, feat // 2, cols), bias], axis=1
    )
    halves = (halves * norm).astype(BF16)

    side = blk_index % 2
    kept = lax.dynamic_index_in_dim(halves, side, 0, keepdims=False)
    sent = lax.dynamic_index_in_dim(halves, 1 - side, 0, keepdims=False)
    got = swap(sent, 1, 0, blocks, reps)
    part = (kept.astype(F32) + got.astype(F32)).astype(BF16)
    for bit in range(1, bits_of(blocks)):
        got = swap(part, (2 << bit) - 2, 0, blocks, reps)
        part = (part.astype(F32) + got.astype(F32)).astype(BF16)

    masks = [(h, r << 1) for r in range(reps // 2) for h in range(2)]
    pieces = [part] + [swap(part, h, r, blocks, reps) for h, r in masks[1:]]
    near = jnp.stack(pieces)
    other = swap(near, 0, 1, blocks, reps)
    table = jnp.stack([near, other])
    table = table.reshape(2, reps // 2, 2, *part.shape)

    def piece(half, rep):
        index = (
            (rep ^ rep_index) & 1,
            (rep ^ rep_index) >> 1,
            half ^ side,
            0,
            0,
        )
        return lax.dynamic_slice(table, index, (1, 1, 1, *part.shape)).reshape(part.shape)

    whole = jnp.concatenate(
        [jnp.concatenate([piece(h, r) for r in range(reps)], axis=1)[None] for h in range(2)]
    ).astype(F32)
    grad_w_in = whole[:, : din // 2].reshape(din, hid)
    grad_w_out = whole[:, din // 2 : din // 2 + feat // 2].reshape(feat, hid).T
    grad_b_in = whole[0, din // 2 + feat // 2]
    return (feat_grad, grad_w_in, grad_b_in, grad_w_out)


def solution(mesh):
    in_specs = (P("blk", None), P(), P(), P(), P(), P(None, "blk"), P(None, "blk"))
    out_specs = (P(None, ("blk", "rep")), P(), P(), P())
    return jax.shard_map(
        on_device, mesh=mesh, in_specs=in_specs, out_specs=out_specs, check_vma=False
    )
```

time: 225 us -> 65.5 us (0.29)
  waiting for transfers between devices: 146 us -> 28.9 us
  blocking collectives: 39.6 us -> 0 us
  starting transfers between devices: 8.36 us -> 22.2 us
  between operations: 14.2 us -> 0.95 us
  local copies, waits for them, and re-layouts: 7.02 us -> 3.83 us
    psum x1 -> x0, waiting for transfers between devices: 98.3 us -> none  [on_device(): lax.psum((term_w_in, term_b_in, term_w_out), ('blk', 'rep'))]
    psum x1 -> x0, blocking collectives: 39.6 us -> none  [on_device(): lax.psum((term_w_in, term_b_in, term_w_out), ('blk', 'rep'))]
    unnamed x3 -> x0, waiting for transfers between devices: 22.9 us -> none
    ppermute x3 -> x11, starting transfers between devices: 8.29 us -> 22.2 us  [the longest x9 18.4 us: swap(): return lax.ppermute(array, AXES, route)]
    unnamed x19 -> x11, local copies, waits for them, and re-layouts: 7.01 us -> 1.4 us
    ppermute x3 -> x11, waiting for transfers between devices: 24.8 us -> 28.9 us  [the longest x9 21.7 us: swap(): return lax.ppermute(array, AXES, route)]
  transfers between devices with their start and end apart: 5 -> 11, of which waited for: 5 -> 10; matrix products, arithmetic and copies ran while one was open for 1% -> 2% of each run, Pallas kernels for 0% -> 0%
where the time goes in v1:
time: 65.5 us; the launch traced here: 65.3 us
  waiting for transfers between devices  28.9 us (44%)
  starting transfers between devices  22.2 us (34%)
  matrix products  6.95 us (11%)
  local copies, waits for them, and re-layouts  3.83 us (6%)
  other arithmetic  2.49 us (4%)
  between operations  0.95 us (1%)
    ppermute x9, waiting for transfers between devices, swap(): return lax.ppermute(array, AXES, route)  21.7 us
    ppermute x9, starting transfers between devices, swap(): return lax.ppermute(array, AXES, route)  18.4 us
    ppermute x2, waiting for transfers between devices, fetch(): return lax.ppermute(array, AXES, route)  7.16 us
    ppermute x2, starting transfers between devices, fetch(): return lax.ppermute(array, AXES, route)  3.78 us
    dot_general x1, matrix products, on_device(): jnp.dot(points, w_in, preferred_element_type=F32) + b_in  2.24 us
    dot_general x2, matrix products, couple(): lax.dot_general(own_pair, vis_pair, (((0,), (0,)), ((), ())), preferred_e...  1.79 us
    slice x1, local copies, waits for them, and re-layouts, on_device(): grad_w_in = whole[:, :din // 2].reshape(din, hid)  1.49 us
    unnamed x11, local copies, waits for them, and re-layouts  1.4 us
  transfers between devices with their start and end apart: 11, of which 10 were waited for; matrix products, arithmetic and copies ran while one was open for 2% of the time, Pallas kernels for 0%

profile of v1, /device:TPU:0, one launch (start us, length us, event | category | flops | bytes accessed | tf_op | source)
XLA Modules:
  0.0 65.3 jit_solution(14893733361673541576)
XLA Ops:
  0.6 0.0 copy-start
  0.6 0.0 copy-start.4
  0.7 0.0 copy-start.3
  0.7 0.0 copy-start.1
  0.7 1.4 %copy-done = bf16[768,1024]{1,0:T(8,128)(2,1)S(1)} copy-done((bf16[768,1024]{1,0:T(8,128)(2,1)S(1)}, bf16[768,1024]{1,0:T(8,128)(2,1)}, u32[]{:S(2)}) %copy-start) | copy-done | bytes 1572888
  2.0 0.0 copy-start.2
  2.0 2.2 %tanh_convert_fusion = bf16[768,512]{1,0:T(8,128)(2,1)S(1)} fusion(bf16[768,1024]{1,0:T(8,128)(2,1)S(1)} %copy-done, bf16[1024,512]{1,0:T(8,128)(2,1)} %param.8, f32[512]{0:T(512)} %param.9), kind=kOutput, calls=%fused_computation.20 | convolution fusion | flops 806092800 | bytes 3409920 | tf_op jit(solution)/shard_map/dot_general | solution.py:65
  4.3 0.0 copy-done.4
  4.3 0.0 copy-done.3
  4.3 0.4 fusion.4
  4.7 0.0 copy-done.1
  4.7 0.0 copy-done.2
  4.7 3.1 %collective-permute-start.1 = (bf16[192,768]{1,0:T(8,128)(2,1)S(1)}, bf16[192,768]{1,0:T(8,128)(2,1)S(1)}, u32[]{:S(2)}, u32[]{:S(2)}) collective-permute-start(bf16[192,768]{1,0:T(8,128)(2,1)S(1)} %pad_maximum_fusion.1), channel_id=1, source_target_pairs={{8,0},{25,1},{14,2},{31,3},{12,4},{29,5},{10,6},{27,7},{0,8},{17,9... | collective-permute-start | bytes 884744 | tf_op jit(solution)/shard_map/ppermute | solution.py:26
  7.9 0.7 %collective-permute-start = (bf16[192,768]{1,0:T(8,128)(2,1)S(1)}, bf16[192,768]{1,0:T(8,128)(2,1)S(1)}, u32[]{:S(2)}, u32[]{:S(2)}) collective-permute-start(bf16[192,768]{1,0:T(8,128)(2,1)S(1)} %pad_maximum_fusion.1), channel_id=1, source_target_pairs={{0,0},{17,1},{6,2},{23,3},{4,4},{21,5},{2,6},{19,7},{8,8},{25,9},{... | collective-permute-start | bytes 884744 | tf_op jit(solution)/shard_map/ppermute | solution.py:26
  8.6 7.2 %collective-permute-done.1 = bf16[192,768]{1,0:T(8,128)(2,1)S(1)} collective-permute-done((bf16[192,768]{1,0:T(8,128)(2,1)S(1)}, bf16[192,768]{1,0:T(8,128)(2,1)S(1)}, u32[]{:S(2)}, u32[]{:S(2)}) %collective-permute-start.1) | collective-permute-done | bytes 294944 | tf_op jit(solution)/shard_map/ppermute | solution.py:26
  15.8 0.5 fusion.28
  16.3 0.0 collective-permute-done
  16.3 0.5 fusion.31
  16.8 0.9 %convert_reduce_fusion = (f32[768]{0:T(1024)S(1)}, bf16[768,768]{0,1:T(8,128)(2,1)S(1)}) fusion(f32[768,768]{0,1:T(8,128)S(1)} %fusion.28, f32[768]{0:T(1024)S(1)} %multiply_reduce_fusion, f32[768]{0:T(1024)S(1)} %get-tuple-element.12, bf16[128,768]{1,0:T(8,128)(2,1)S(1)} %constant_dynamic-update-slice_fusion, bf16[192,768]{1,0:T(8,128)(2,1)S(1)} %collective-permute-done.1), kind=kOutput, calls=%fused_computation | convolution fusion | flops 155712768 | bytes 3943424 | tf_op jit(solution)/shard_map/dot_general | solution.py:44
  17.7 0.9 %convert_reduce_fusion.1 = (f32[768]{0:T(1024)S(1)}, bf16[768,768]{0,1:T(8,128)(2,1)S(1)}) fusion(f32[768,768]{0,1:T(8,128)S(1)} %fusion.31, f32[768]{0:T(1024)S(1)} %multiply_reduce_fusion.1, f32[768]{0:T(1024)S(1)} %get-tuple-element.12, bf16[128,768]{1,0:T(8,128)(2,1)S(1)} %constant_dynamic-update-slice_fusion, bf16[192,768]{1,0:T(8,128)(2,1)S(1)} %collective-permute-done), kind=kOutput, calls=%fused_computation.1 | convolution fusion | flops 155712768 | bytes 3943424 | tf_op jit(solution)/shard_map/dot_general | solution.py:44
  18.6 0.3 fusion.26
  19.0 0.3 fusion
  19.3 6.0 %collective-permute-start.2 = (f32[64,768]{1,0:T(8,128)S(1)}, f32[64,768]{1,0:T(8,128)S(1)}, u32[]{:S(2)}, u32[]{:S(2)}) collective-permute-start(f32[64,768]{1,0:T(8,128)S(1)} %fusion), channel_id=1, source_target_pairs={{0,1},{1,0},{2,3},{3,2},{4,5},{5,4},{6,7},{7,6},{8,9},{9,8},{10,11... | collective-permute-start | bytes 589832 | tf_op jit(solution)/shard_map/ppermute | solution.py:35
  25.3 1.1 %collective-permute-done.2 = f32[64,768]{1,0:T(8,128)S(1)} collective-permute-done((f32[64,768]{1,0:T(8,128)S(1)}, f32[64,768]{1,0:T(8,128)S(1)}, u32[]{:S(2)}, u32[]{:S(2)}) %collective-permute-start.2) | collective-permute-done | bytes 196640 | tf_op jit(solution)/shard_map/ppermute | solution.py:35
  26.4 3.2 %collective-permute-start.3 = (bf16[64,768]{1,0:T(8,128)(2,1)S(1)}, bf16[64,768]{1,0:T(8,128)(2,1)S(1)}, u32[]{:S(2)}, u32[]{:S(2)}) collective-permute-start(bf16[64,768]{1,0:T(8,128)(2,1)S(1)} %add_convert_fusion.2), channel_id=1, source_target_pairs={{0,2},{1,3},{2,0},{3,1},{4,6},{5,7},{6,4},{7,5},{8,10},{9,11},{10,... | collective-permute-start | bytes 294920 | tf_op jit(solution)/shard_map/ppermute | solution.py:35
  29.6 3.1 %collective-permute-done.3 = bf16[64,768]{1,0:T(8,128)(2,1)S(1)} collective-permute-done((bf16[64,768]{1,0:T(8,128)(2,1)S(1)}, bf16[64,768]{1,0:T(8,128)(2,1)S(1)}, u32[]{:S(2)}, u32[]{:S(2)}) %collective-permute-start.3) | collective-permute-done | bytes 98336 | tf_op jit(solution)/shard_map/ppermute | solution.py:35
  32.7 0.1 add_multiply_fusion
  32.7 0.3 fusion.38
  33.1 0.2 fusion.8
  33.2 0.4 convolution_bitcast_fusion
  33.6 0.2 copy.21
  33.9 0.1 fusion.2
  34.0 1.2 %collective-permute-start.4 = (bf16[560,128]{1,0:T(8,128)(2,1)S(1)}, bf16[560,128]{1,0:T(8,128)(2,1)S(1)}, u32[]{:S(2)}, u32[]{:S(2)}) collective-permute-start(bf16[560,128]{1,0:T(8,128)(2,1)S(1)} %dynamic-slice_bitcast_fusion), channel_id=1, source_target_pairs={{0,4},{1,5},{2,6},{3,7},{4,0},{5,1},{6,2},{7,3},{8,12},{9,13},{10,... | collective-permute-start | bytes 430088 | tf_op jit(solution)/shard_map/ppermute | solution.py:35
  35.2 4.1 %collective-permute-done.4 = bf16[560,128]{1,0:T(8,128)(2,1)S(1)} collective-permute-done((bf16[560,128]{1,0:T(8,128)(2,1)S(1)}, bf16[560,128]{1,0:T(8,128)(2,1)S(1)}, u32[]{:S(2)}, u32[]{:S(2)}) %collective-permute-start.4) | collective-permute-done | bytes 143392 | tf_op jit(solution)/shard_map/ppermute | solution.py:35
  39.3 0.8 %collective-permute-start.5 = (bf16[560,128]{1,0:T(8,128)(2,1)S(1)}, bf16[560,128]{1,0:T(8,128)(2,1)S(1)}, u32[]{:S(2)}, u32[]{:S(2)}) collective-permute-start(bf16[560,128]{1,0:T(8,128)(2,1)S(1)} %fusion.3), channel_id=1, source_target_pairs={{0,8},{1,9},{2,10},{3,11},{4,12},{5,13},{6,14},{7,15},{8,0},{9,1},... | collective-permute-start | bytes 430088 | tf_op jit(solution)/shard_map/ppermute | solution.py:35
  40.1 4.4 %collective-permute-done.5 = bf16[560,128]{1,0:T(8,128)(2,1)S(1)} collective-permute-done((bf16[560,128]{1,0:T(8,128)(2,1)S(1)}, bf16[560,128]{1,0:T(8,128)(2,1)S(1)}, u32[]{:S(2)}, u32[]{:S(2)}) %collective-permute-start.5) | collective-permute-done | bytes 143392 | tf_op jit(solution)/shard_map/ppermute | solution.py:35
  44.5 3.7 %collective-permute-start.6 = (bf16[560,128]{1,0:T(8,128)(2,1)S(1)}, bf16[560,128]{1,0:T(8,128)(2,1)S(1)}, u32[]{:S(2)}, u32[]{:S(2)}) collective-permute-start(bf16[560,128]{1,0:T(8,128)(2,1)S(1)} %add_convert_fusion.1), channel_id=1, source_target_pairs={{0,24},{1,25},{2,26},{3,27},{4,28},{5,29},{6,30},{7,31},{8,16},{9,... | collective-permute-start | bytes 430088 | tf_op jit(solution)/shard_map/ppermute | solution.py:35
  48.2 3.4 %collective-permute-done.6 = bf16[560,128]{1,0:T(8,128)(2,1)S(1)} collective-permute-done((bf16[560,128]{1,0:T(8,128)(2,1)S(1)}, bf16[560,128]{1,0:T(8,128)(2,1)S(1)}, u32[]{:S(2)}, u32[]{:S(2)}) %collective-permute-start.6) | collective-permute-done | bytes 143392 | tf_op jit(solution)/shard_map/ppermute | solution.py:35
  51.6 2.4 %collective-permute-start.9 = (bf16[560,128]{1,0:T(8,128)(2,1)S(1)}, bf16[560,128]{1,0:T(8,128)(2,1)S(1)}, u32[]{:S(2)}, u32[]{:S(2)}) collective-permute-start(bf16[560,128]{1,0:T(8,128)(2,1)S(1)} %add_convert_fusion), channel_id=1, source_target_pairs={{0,6},{1,7},{2,4},{3,5},{4,2},{5,3},{6,0},{7,1},{8,14},{9,15},{10,... | collective-permute-start | bytes 430088 | tf_op jit(solution)/shard_map/ppermute | solution.py:35
  54.0 0.5 collective-permute-start.8
  54.5 0.6 collective-permute-start.7
  55.1 2.5 %collective-permute-done.9 = bf16[560,128]{1,0:T(8,128)(2,1)S(1)} collective-permute-done((bf16[560,128]{1,0:T(8,128)(2,1)S(1)}, bf16[560,128]{1,0:T(8,128)(2,1)S(1)}, u32[]{:S(2)}, u32[]{:S(2)}) %collective-permute-start.9) | collective-permute-done | bytes 143392 | tf_op jit(solution)/shard_map/ppermute | solution.py:35
  57.7 1.5 %collective-permute-done.8 = bf16[560,128]{1,0:T(8,128)(2,1)S(1)} collective-permute-done((bf16[560,128]{1,0:T(8,128)(2,1)S(1)}, bf16[560,128]{1,0:T(8,128)(2,1)S(1)}, u32[]{:S(2)}, u32[]{:S(2)}) %collective-permute-start.8) | collective-permute-done | bytes 143392 | tf_op jit(solution)/shard_map/ppermute | solution.py:35
  59.2 0.5 collective-permute-done.7
  59.6 0.1 pad_maximum_fusion
  59.7 0.1 collective-permute-start.10
  59.8 0.7 %constant_dynamic-slice_fusion = f32[64,192]{1,0:T(8,128)} fusion(f32[64,768]{1,0:T(8,128)S(1)} %add_multiply_fusion, s32[]{:T(128)S(6)} %select_n.63), kind=kLoop, calls=%fused_computation.82 | loop fusion | bytes 98308 | tf_op jit(solution)/shard_map/dynamic_slice | solution.py:90
  60.5 1.2 %collective-permute-done.10 = bf16[4,560,128]{2,1,0:T(8,128)(2,1)S(1)} collective-permute-done((bf16[4,560,128]{2,1,0:T(8,128)(2,1)S(1)}, bf16[4,560,128]{2,1,0:T(8,128)(2,1)S(1)}, u32[]{:S(2)}, u32[]{:S(2)}) %collective-permute-start.10) | collective-permute-done | bytes 573472 | tf_op jit(solution)/shard_map/ppermute | solution.py:35
  61.8 0.2 fusion.23
  62.0 0.3 fusion.24
  62.3 0.1 maximum_bitcast_fusion
  62.4 0.2 maximum_convert_fusion
  62.6 0.6 maximum_convert_fusion.2
  63.1 0.7 %maximum_convert_fusion.1 = f32[2,32,512]{2,1,0:T(8,128)} fusion(bf16[1,560,512]{2,1,0:T(8,128)(2,1)S(1)} %get-tuple-element.21, bf16[1,560,512]{2,1,0:T(8,128)(2,1)S(1)} %get-tuple-element.20), kind=kLoop, calls=%fused_computation.74 | loop fusion | flops 131072 | bytes 1277952 | tf_op jit(solution)/shard_map/slice | solution.py:145
  63.8 1.5 %slice.32 = f32[2,512,512]{2,1,0:T(8,128)} slice(f32[2,560,512]{2,1,0:T(8,128)S(1)} %maximum_convert_fusion), slice={[0:2], [0:512], [0:512]} | slice | bytes 4194304 | tf_op jit(solution)/shard_map/slice | solution.py:144
  (12 shorter events, 0.3 us)
Async XLA Ops:
  0.6 1.4 %copy-start = (bf16[768,1024]{1,0:T(8,128)(2,1)S(1)}, bf16[768,1024]{1,0:T(8,128)(2,1)}, u32[]{:S(2)}) copy-start(bf16[768,1024]{1,0:T(8,128)(2,1)} %param.7) | copy-start | bytes 4718596
  0.6 3.6 %copy-start.4 = (f32[64]{0:T(128)S(1)}, f32[64]{0:T(128)}, u32[]{:S(2)}) copy-start(f32[64]{0:T(128)} %param.11) | copy-start | bytes 772
  0.7 3.6 %copy-start.3 = (bf16[512,64]{0,1:T(8,128)(2,1)S(1)}, bf16[512,64]{0,1:T(8,128)(2,1)}, u32[]{:S(2)}) copy-start(bf16[512,64]{0,1:T(8,128)(2,1)} %param.10) | copy-start | bytes 196612
  0.7 4.0 %copy-start.1 = (bf16[64,768]{1,0:T(8,128)(2,1)S(1)}, bf16[64,768]{1,0:T(8,128)(2,1)}, u32[]{:S(2)}) copy-start(bf16[64,768]{1,0:T(8,128)(2,1)} %param.12) | copy-start | bytes 294916
  2.0 2.7 %copy-start.2 = (bf16[64,768]{1,0:T(8,128)(2,1)S(1)}, bf16[64,768]{1,0:T(8,128)(2,1)}, u32[]{:S(2)}) copy-start(bf16[64,768]{1,0:T(8,128)(2,1)} %param.13) | copy-start | bytes 294916
  4.7 11.0 %collective-permute-start.1 = (bf16[192,768]{1,0:T(8,128)(2,1)S(1)}, bf16[192,768]{1,0:T(8,128)(2,1)S(1)}, u32[]{:S(2)}, u32[]{:S(2)}) collective-permute-start(bf16[192,768]{1,0:T(8,128)(2,1)S(1)} %pad_maximum_fusion.1), channel_id=1, source_target_pairs={{8,0},{25,1},{14,2},{31,3},{12,4},{29,5},{10,6},{27,7},{0,8},{17,9... | collective-permute-start | bytes 884744 | tf_op jit(solution)/shard_map/ppermute | solution.py:26
  7.9 8.4 %collective-permute-start = (bf16[192,768]{1,0:T(8,128)(2,1)S(1)}, bf16[192,768]{1,0:T(8,128)(2,1)S(1)}, u32[]{:S(2)}, u32[]{:S(2)}) collective-permute-start(bf16[192,768]{1,0:T(8,128)(2,1)S(1)} %pad_maximum_fusion.1), channel_id=1, source_target_pairs={{0,0},{17,1},{6,2},{23,3},{4,4},{21,5},{2,6},{19,7},{8,8},{25,9},{... | collective-permute-start | bytes 884744 | tf_op jit(solution)/shard_map/ppermute | solution.py:26
  19.3 7.0 %collective-permute-start.2 = (f32[64,768]{1,0:T(8,128)S(1)}, f32[64,768]{1,0:T(8,128)S(1)}, u32[]{:S(2)}, u32[]{:S(2)}) collective-permute-start(f32[64,768]{1,0:T(8,128)S(1)} %fusion), channel_id=1, source_target_pairs={{0,1},{1,0},{2,3},{3,2},{4,5},{5,4},{6,7},{7,6},{8,9},{9,8},{10,11... | collective-permute-start | bytes 589832 | tf_op jit(solution)/shard_map/ppermute | solution.py:35
  26.4 6.3 %collective-permute-start.3 = (bf16[64,768]{1,0:T(8,128)(2,1)S(1)}, bf16[64,768]{1,0:T(8,128)(2,1)S(1)}, u32[]{:S(2)}, u32[]{:S(2)}) collective-permute-start(bf16[64,768]{1,0:T(8,128)(2,1)S(1)} %add_convert_fusion.2), channel_id=1, source_target_pairs={{0,2},{1,3},{2,0},{3,1},{4,6},{5,7},{6,4},{7,5},{8,10},{9,11},{10,... | collective-permute-start | bytes 294920 | tf_op jit(solution)/shard_map/ppermute | solution.py:35
  34.0 5.3 %collective-permute-start.4 = (bf16[560,128]{1,0:T(8,128)(2,1)S(1)}, bf16[560,128]{1,0:T(8,128)(2,1)S(1)}, u32[]{:S(2)}, u32[]{:S(2)}) collective-permute-start(bf16[560,128]{1,0:T(8,128)(2,1)S(1)} %dynamic-slice_bitcast_fusion), channel_id=1, source_target_pairs={{0,4},{1,5},{2,6},{3,7},{4,0},{5,1},{6,2},{7,3},{8,12},{9,13},{10,... | collective-permute-start | bytes 430088 | tf_op jit(solution)/shard_map/ppermute | solution.py:35
  39.3 5.2 %collective-permute-start.5 = (bf16[560,128]{1,0:T(8,128)(2,1)S(1)}, bf16[560,128]{1,0:T(8,128)(2,1)S(1)}, u32[]{:S(2)}, u32[]{:S(2)}) collective-permute-start(bf16[560,128]{1,0:T(8,128)(2,1)S(1)} %fusion.3), channel_id=1, source_target_pairs={{0,8},{1,9},{2,10},{3,11},{4,12},{5,13},{6,14},{7,15},{8,0},{9,1},... | collective-permute-start | bytes 430088 | tf_op jit(solution)/shard_map/ppermute | solution.py:35
  44.5 7.0 %collective-permute-start.6 = (bf16[560,128]{1,0:T(8,128)(2,1)S(1)}, bf16[560,128]{1,0:T(8,128)(2,1)S(1)}, u32[]{:S(2)}, u32[]{:S(2)}) collective-permute-start(bf16[560,128]{1,0:T(8,128)(2,1)S(1)} %add_convert_fusion.1), channel_id=1, source_target_pairs={{0,24},{1,25},{2,26},{3,27},{4,28},{5,29},{6,30},{7,31},{8,16},{9,... | collective-permute-start | bytes 430088 | tf_op jit(solution)/shard_map/ppermute | solution.py:35
  51.6 6.1 %collective-permute-start.9 = (bf16[560,128]{1,0:T(8,128)(2,1)S(1)}, bf16[560,128]{1,0:T(8,128)(2,1)S(1)}, u32[]{:S(2)}, u32[]{:S(2)}) collective-permute-start(bf16[560,128]{1,0:T(8,128)(2,1)S(1)} %add_convert_fusion), channel_id=1, source_target_pairs={{0,6},{1,7},{2,4},{3,5},{4,2},{5,3},{6,0},{7,1},{8,14},{9,15},{10,... | collective-permute-start | bytes 430088 | tf_op jit(solution)/shard_map/ppermute | solution.py:35
  54.0 5.2 %collective-permute-start.8 = (bf16[560,128]{1,0:T(8,128)(2,1)S(1)}, bf16[560,128]{1,0:T(8,128)(2,1)S(1)}, u32[]{:S(2)}, u32[]{:S(2)}) collective-permute-start(bf16[560,128]{1,0:T(8,128)(2,1)S(1)} %add_convert_fusion), channel_id=1, source_target_pairs={{0,2},{1,3},{2,0},{3,1},{4,6},{5,7},{6,4},{7,5},{8,10},{9,11},{10,... | collective-permute-start | bytes 430088 | tf_op jit(solution)/shard_map/ppermute | solution.py:35
  54.5 5.1 %collective-permute-start.7 = (bf16[560,128]{1,0:T(8,128)(2,1)S(1)}, bf16[560,128]{1,0:T(8,128)(2,1)S(1)}, u32[]{:S(2)}, u32[]{:S(2)}) collective-permute-start(bf16[560,128]{1,0:T(8,128)(2,1)S(1)} %add_convert_fusion), channel_id=1, source_target_pairs={{0,4},{1,5},{2,6},{3,7},{4,0},{5,1},{6,2},{7,3},{8,12},{9,13},{10,... | collective-permute-start | bytes 430088 | tf_op jit(solution)/shard_map/ppermute | solution.py:35
  59.7 2.0 %collective-permute-start.10 = (bf16[4,560,128]{2,1,0:T(8,128)(2,1)S(1)}, bf16[4,560,128]{2,1,0:T(8,128)(2,1)S(1)}, u32[]{:S(2)}, u32[]{:S(2)}) collective-permute-start(bf16[4,560,128]{2,1,0:T(8,128)(2,1)S(1)} %pad_maximum_fusion), channel_id=1, source_target_pairs={{0,1},{1,0},{2,3},{3,2},{4,5},{5,4},{6,7},{7,6},{8,9},{9,8},{10,11... | collective-permute-start | bytes 1720328 | tf_op jit(solution)/shard_map/ppermute | solution.py:35

commit v2 on v1

--- a/solution.py
+++ b/solution.py
@@ -3,6 +3,8 @@
 import jax
 import jax.numpy as jnp
 from jax import lax
+from jax.experimental import pallas as pl
+from jax.experimental.pallas import tpu as pltpu
 from jax.sharding import PartitionSpec as P
 
 AXES = ("blk", "rep")
@@ -14,11 +16,13 @@
     return count.bit_length() - 1
 
 
-def visit_mask(step, rep, blocks, reps):
-    low = (bits_of(reps) + 1) // 2
-    high = bits_of(reps) - low
-    near, far = divmod(rep, 1 << high)
-    return far * (blocks >> high) + step * (1 << low) + near
+def visit_mask(step, rep, reps):
+    width = bits_of(reps)
+    core = rep & 1
+    near = (core << (width - 1)) | (rep >> 1)
+    if width > 1:
+        near ^= core ^ (step & 1)
+    return step * reps + near
 
 
 def fetch(array, masks, blocks, reps):
@@ -35,19 +39,95 @@
     return lax.ppermute(array, AXES, route)
 
 
-def couple(own_y, own_pair, own_sq, visitor, feat):
-    vis_y = visitor[:feat]
-    vis_pair = visitor[feat:]
-    vis_sq = jnp.sum(jnp.square(vis_y.astype(F32)), axis=0)
-    cross = lax.dot_general(own_y, vis_y, (((0,), (0,)), ((), ())), preferred_element_type=F32)
-    kernel = jnp.exp(-0.5 * (own_sq[:, None] + vis_sq[None, :] - 2.0 * cross))
-    coupling = lax.dot_general(
-        own_pair, vis_pair, (((0,), (0,)), ((), ())), preferred_element_type=F32
-    )
-    weight_b = (coupling * kernel).astype(BF16)
-    totals = jnp.sum(weight_b.astype(F32), axis=1)
-    pull = lax.dot_general(vis_y, weight_b, (((1,), (1,)), ((), ())), preferred_element_type=F32)
-    return (totals, pull)
+def couple_kernel(chunk, own_y, own_pair, vis_y, vis_pair, before, after):
+    feat, rows = own_y.shape
+    own = own_y[...]
+    own32 = own.astype(F32)
+    own_half = 0.5 * jnp.sum(own32 * own32, axis=0, keepdims=True)
+    ones = jnp.ones((16, chunk), BF16)
+    pulled = jnp.zeros((feat + 16, rows), F32)
+    for start in range(0, rows, chunk):
+        part_y = vis_y[:, start : start + chunk]
+        turned = part_y.astype(F32).T
+        vis_half = 0.5 * jnp.sum(turned * turned, axis=1, keepdims=True)
+        cross = jnp.dot(turned.astype(BF16), own, preferred_element_type=F32)
+        coupling = lax.dot_general(
+            vis_pair[:, start : start + chunk],
+            own_pair[...],
+            (((0,), (0,)), ((), ())),
+            preferred_element_type=F32,
+        )
+        weight = (coupling * jnp.exp(cross - (own_half + vis_half))).astype(BF16)
+        pulled += jnp.dot(
+            jnp.concatenate([part_y, ones], axis=0), weight, preferred_element_type=F32
+        )
+    after[...] = before[...] + (pulled[:feat] - own32 * pulled[feat : feat + 1])
+
+
+def in_vmem(array):
+    return pltpu.with_memory_space_constraint(array, pltpu.VMEM)
+
+
+def couple(own_y, own_pair, vis_y, vis_pair, drift):
+    rows = own_y.shape[1]
+    chunk = 256 if rows % 256 == 0 else rows
+    return pl.pallas_call(
+        lambda *refs: couple_kernel(chunk, *refs),
+        out_shape=pltpu.VMEM(drift.shape, F32),
+        in_specs=[pl.BlockSpec(memory_space=pltpu.VMEM)] * 5,
+        out_specs=pl.BlockSpec(memory_space=pltpu.VMEM),
+        compiler_params=pltpu.CompilerParams(vmem_limit_bytes=16 << 20),
+        name="couple",
+    )(*map(in_vmem, (own_y, own_pair, vis_y, vis_pair, drift)))
+
+
+def place_kernel(depth, offset, where, table, *refs):
+    w_in, b_in, w_out = refs[-3:]
+    din = w_in.shape[0]
+    half = din // 2
+    base = 2 * (pl.program_id(0) ^ where[0])
+    low = table.at[base + where[1]]
+    high = table.at[base + (1 - where[1])]
+    w_in[:half] = low[:half].astype(F32)
+    w_in[half:] = high[:half].astype(F32)
+    turned = jnp.concatenate(
+        [low[half : half + depth].astype(F32), high[half : half + depth].astype(F32)], axis=0
+    )
+    w_out[...] = turned.T
+    b_in[...] = low[half + depth : half + depth + 16].astype(F32)[:1]
+
+
+def place(table, where, offset, din, feat, reps, earlier):
+    count, height, cols = table.shape
+    hid = cols * reps
+    shapes = (
+        jax.ShapeDtypeStruct((din, hid), F32),
+        jax.ShapeDtypeStruct((1, hid), F32),
+        jax.ShapeDtypeStruct((hid, feat), F32),
+    )
+
+    def column(i, at):
+        return 2 * i + (at[2] ^ offset)
+
+    grid_spec = pltpu.PrefetchScalarGridSpec(
+        num_scalar_prefetch=1,
+        grid=(reps // 2,),
+        in_specs=[pl.BlockSpec(memory_space=pltpu.VMEM)]
+        + [pl.BlockSpec(memory_space=pl.ANY) for _ in earlier],
+        out_specs=[
+            pl.BlockSpec((din, cols), lambda i, at: (0, column(i, at))),
+            pl.BlockSpec((1, cols), lambda i, at: (0, column(i, at))),
+            pl.BlockSpec((cols, feat), lambda i, at: (column(i, at), 0)),
+        ],
+    )
+    return pl.pallas_call(
+        lambda *refs: place_kernel(feat // 2, offset, *refs),
+        out_shape=shapes,
+        grid_spec=grid_spec,
+        input_output_aliases={2 + i: i for i in range(len(earlier))},
+        compiler_params=pltpu.CompilerParams(vmem_limit_bytes=16 << 20),
+        name="place",
+    )(where, in_vmem(table), *earlier)
 
 
 def on_device(points, w_in, b_in, w_out, inv_scale, solves, probes):
@@ -65,21 +145,15 @@
     hidden = jnp.tanh(jnp.dot(points, w_in, preferred_element_type=F32) + b_in).astype(BF16)
     pre = lax.dot_general(w_out, hidden, (((0,), (1,)), ((), ())), preferred_element_type=F32)
     scaled = (pre * inv_scale[:, None]).astype(BF16)
-    own_sq = jnp.sum(jnp.square(scaled.astype(F32)), axis=0)
     own_pair = jnp.concatenate([solves, probes], axis=0)
-    visitor = jnp.concatenate([scaled, probes, solves], axis=0)
-
-    visitors = []
-    for step in range(blocks // reps):
-        masks = [visit_mask(step, r, blocks, reps) for r in range(reps)]
-        visitors.append(fetch(visitor, masks, blocks, reps))
-    totals = jnp.zeros((rows,), F32)
-    pull = jnp.zeros((feat, rows), F32)
-    for vis in visitors:
-        more_totals, more_pull = couple(scaled, own_pair, own_sq, vis, feat)
-        totals = totals + more_totals
-        pull = pull + more_pull
-    drift = pull - scaled.astype(F32) * totals[None, :]
+    pair = jnp.concatenate([probes, solves], axis=0)
+    steps = range(blocks // reps)
+    masks = [[visit_mask(step, r, reps) for r in range(reps)] for step in steps]
+    pairs = [fetch(pair, masks[step], blocks, reps) for step in steps]
+    scaleds = [fetch(scaled, masks[step], blocks, reps) for step in steps]
+    drift = jnp.zeros((feat, rows), F32)
+    for step in steps:
+        drift = couple(scaled, own_pair, scaleds[step], pairs[step], drift)
 
     drift = drift + swap(drift, 0, 1, blocks, reps)
     for bit in range(1, bits_of(reps)):
@@ -125,25 +199,10 @@
     pieces = [part] + [swap(part, h, r, blocks, reps) for h, r in masks[1:]]
     near = jnp.stack(pieces)
     other = swap(near, 0, 1, blocks, reps)
-    table = jnp.stack([near, other])
-    table = table.reshape(2, reps // 2, 2, *part.shape)
-
-    def piece(half, rep):
-        index = (
-            (rep ^ rep_index) & 1,
-            (rep ^ rep_index) >> 1,
-            half ^ side,
-            0,
-            0,
-        )
-        return lax.dynamic_slice(table, index, (1, 1, 1, *part.shape)).reshape(part.shape)
-
-    whole = jnp.concatenate(
-        [jnp.concatenate([piece(h, r) for r in range(reps)], axis=1)[None] for h in range(2)]
-    ).astype(F32)
-    grad_w_in = whole[:, : din // 2].reshape(din, hid)
-    grad_w_out = whole[:, din // 2 : din // 2 + feat // 2].reshape(feat, hid).T
-    grad_b_in = whole[0, din // 2 + feat // 2]
+    where = jnp.stack([rep_index >> 1, side, rep_index & 1])
+    outs = place(near, where, 0, din, feat, reps, ())
+    grad_w_in, grad_b_in, grad_w_out = place(other, where, 1, din, feat, reps, outs)
+    grad_b_in = grad_b_in.reshape(hid)
     return (feat_grad, grad_w_in, grad_b_in, grad_w_out)
 
 

time: 65.5 us -> 63 us (0.962)
  Pallas kernels: 0 us -> 5.79 us
  matrix products: 6.95 us -> 3.44 us
  other arithmetic: 2.49 us -> 0.44 us
  starting transfers between devices: 22.2 us -> 20.8 us
  waiting for transfers between devices: 28.9 us -> 27.9 us
    pallas_call x0 -> x4, Pallas kernels: none -> 5.79 us  [the longest x2 3.17 us: place(): pl.pallas_call(lambda *refs: place_kernel(feat // 2, offset, *refs), out_...]
    ppermute x9, starting transfers between devices: 18.4 us -> 14.1 us  [swap(): return lax.ppermute(array, AXES, route)]
    dot_general x6 -> x0, matrix products: 3.47 us -> none  [the longest x2 1.79 us: couple(): lax.dot_general(own_pair, vis_pair, (((0,), (0,)), ((), ())), preferred_e...]
    ppermute x2 -> x4, starting transfers between devices: 3.78 us -> 6.62 us  [fetch(): return lax.ppermute(array, AXES, route)]
    slice x1 -> x0, local copies, waits for them, and re-layouts: 1.49 us -> none  [on_device(): grad_w_in = whole[:, :din // 2].reshape(din, hid)]
    ppermute x9, waiting for transfers between devices: 21.7 us -> 20.2 us  [swap(): return lax.ppermute(array, AXES, route)]
    slice x2 -> x0, other arithmetic: 1.25 us -> none  [the longest x1 0.67 us: on_device(): grad_w_out = whole[:, din // 2:din // 2 + feat // 2].reshape(feat, hid).T]
    concatenate x0 -> x1, local copies, waits for them, and re-layouts: none -> 0.91 us  [on_device(): pair = jnp.concatenate([probes, solves], axis=0)]
  transfers between devices with their start and end apart: 11 -> 13, of which waited for: 10 -> 9; matrix products, arithmetic and copies ran while one was open for 2% -> 5% of each run, Pallas kernels for 0% -> 5%
where the time goes in v2:
time: 63 us; the launch traced here: 62.8 us
  waiting for transfers between devices  27.9 us (44%)
  starting transfers between devices  20.8 us (33%)
  Pallas kernels  5.79 us (9%)
  local copies, waits for them, and re-layouts  3.68 us (6%)
  matrix products  3.44 us (5%)
  between operations  0.85 us (1%)
    ppermute x9, waiting for transfers between devices, swap(): return lax.ppermute(array, AXES, route)  20.2 us
    ppermute x9, starting transfers between devices, swap(): return lax.ppermute(array, AXES, route)  14.1 us
    ppermute x4, waiting for transfers between devices, fetch(): return lax.ppermute(array, AXES, route)  7.61 us
    ppermute x4, starting transfers between devices, fetch(): return lax.ppermute(array, AXES, route)  6.62 us
    pallas_call x2, Pallas kernels, place(): pl.pallas_call(lambda *refs: place_kernel(feat // 2, offset, *refs), out_...  3.17 us
    pallas_call x2, Pallas kernels, couple(): pl.pallas_call(lambda *refs: couple_kernel(chunk, *refs), out_shape=pltpu...  2.62 us
    dot_general x1, matrix products, on_device(): jnp.dot(points, w_in, preferred_element_type=F32) + b_in  2.2 us
    unnamed x10, local copies, waits for them, and re-layouts  1.82 us
  transfers between devices with their start and end apart: 13, of which 9 were waited for; matrix products, arithmetic and copies ran while one was open for 5% of the time, Pallas kernels for 5%

profile of v2, /device:TPU:0, one launch (start us, length us, event | category | flops | bytes accessed | tf_op | source)
XLA Modules:
  0.0 62.8 jit_solution(10392408382864299985)
XLA Ops:
  0.6 0.0 copy-start
  0.6 1.0 %constant_dynamic-update-slice_fusion.3 = bf16[128,768]{1,0:T(8,128)(2,1)S(1)} fusion(bf16[64,768]{1,0:T(8,128)(2,1)} %param.13), kind=kLoop, calls=%fused_computation.25 | loop fusion | bytes 196608
  1.7 0.9 %constant_dynamic-update-slice_fusion.2 = (bf16[128,768]{1,0:T(8,128)(2,1)S(1)}, bf16[128,768]{1,0:T(8,128)(2,1)S(1)}) fusion(bf16[128,768]{1,0:T(8,128)(2,1)S(1)} %constant_dynamic-update-slice_fusion.3, bf16[64,768]{1,0:T(8,128)(2,1)} %param.12), kind=kLoop, calls=%fused_computation.24 | loop fusion | bytes 294912 | tf_op jit(solution)/shard_map/concatenate | solution.py:149
  2.6 0.0 copy-start.2
  2.6 0.0 copy-start.3
  2.6 0.0 copy-start.1
  2.6 0.8 %collective-permute-start.3 = (bf16[128,768]{1,0:T(8,128)(2,1)S(1)}, bf16[128,768]{1,0:T(8,128)(2,1)S(1)}, u32[]{:S(2)}, u32[]{:S(2)}) collective-permute-start(bf16[128,768]{1,0:T(8,128)(2,1)S(1)} %get-tuple-element.20), channel_id=1, source_target_pairs={{0,0},{13,1},{6,2},{11,3},{4,4},{9,5},{2,6},{15,7},{8,8},{5,9},{14... | collective-permute-start | bytes 589832 | tf_op jit(solution)/shard_map/ppermute | solution.py:30
  3.4 5.1 %collective-permute-start.1 = (bf16[128,768]{1,0:T(8,128)(2,1)S(1)}, bf16[128,768]{1,0:T(8,128)(2,1)S(1)}, u32[]{:S(2)}, u32[]{:S(2)}) collective-permute-start(bf16[128,768]{1,0:T(8,128)(2,1)S(1)} %get-tuple-element.20), channel_id=1, source_target_pairs={{20,0},{25,1},{18,2},{31,3},{16,4},{29,5},{22,6},{27,7},{28,8},{17... | collective-permute-start | bytes 589832 | tf_op jit(solution)/shard_map/ppermute | solution.py:30
  8.5 0.0 copy-done
  8.5 2.2 %tanh_convert_fusion = bf16[768,512]{1,0:T(8,128)(2,1)S(1)} fusion(bf16[768,1024]{1,0:T(8,128)(2,1)S(1)} %copy-done, bf16[1024,512]{1,0:T(8,128)(2,1)} %param.8, f32[512]{0:T(512)} %param.9), kind=kOutput, calls=%fused_computation | convolution fusion | flops 806092800 | bytes 3409920 | tf_op jit(solution)/shard_map/dot_general | solution.py:145
  10.7 0.0 copy-done.2
  10.7 0.0 copy-done.3
  10.7 0.3 fusion.1.refs_0_
  11.1 0.7 %collective-permute-start.2 = (bf16[64,768]{1,0:T(8,128)(2,1)S(1)}, bf16[64,768]{1,0:T(8,128)(2,1)S(1)}, u32[]{:S(2)}, u32[]{:S(2)}) collective-permute-start(bf16[64,768]{1,0:T(8,128)(2,1)S(1)} %fusion.1.refs_0_), channel_id=1, source_target_pairs={{0,0},{13,1},{6,2},{11,3},{4,4},{9,5},{2,6},{15,7},{8,8},{5,9},{14... | collective-permute-start | bytes 294920 | tf_op jit(solution)/shard_map/ppermute | solution.py:30
  11.7 0.1 collective-permute-start
  11.8 0.0 copy-done.1
  11.9 0.0 collective-permute-done.2.refs_2_
  11.9 0.0 collective-permute-done.3.refs_3_
  11.9 1.3 %couple.2.refs_4_ = f32[64,768]{1,0:T(8,128)S(1)} custom-call(bf16[64,768]{1,0:T(8,128)(2,1)S(1)} %fusion.1.refs_0_, bf16[128,768]{1,0:T(8,128)(2,1)S(1)} %constant_dynamic-update-slice_fusion.refs_1_, bf16[64,768]{1,0:T(8,128)(2,1)S(1)} %collective-permute-done.2.refs_2_, bf16[128,768]{1,0:T(8,128)(2,1)S(1)} %collective-permute-done.3.refs_3_, ...), custom_call_target="tpu_custom_call" | custom-call | tf_op jit(solution)/shard_map/couple/pallas_call | solution.py:74
  13.2 7.6 %collective-permute-done.refs_2_ = bf16[64,768]{1,0:T(8,128)(2,1)S(1)} collective-permute-done((bf16[64,768]{1,0:T(8,128)(2,1)S(1)}, bf16[64,768]{1,0:T(8,128)(2,1)S(1)}, u32[]{:S(2)}, u32[]{:S(2)}) %collective-permute-start) | collective-permute-done | bytes 98336 | tf_op jit(solution)/shard_map/ppermute | solution.py:30
  20.8 0.0 collective-permute-done.1.refs_3_
  20.8 1.3 %couple.3 = f32[64,768]{1,0:T(8,128)S(1)} custom-call(bf16[64,768]{1,0:T(8,128)(2,1)S(1)} %fusion.1.refs_0_, bf16[128,768]{1,0:T(8,128)(2,1)S(1)} %constant_dynamic-update-slice_fusion.refs_1_, bf16[64,768]{1,0:T(8,128)(2,1)S(1)} %collective-permute-done.refs_2_, bf16[128,768]{1,0:T(8,128)(2,1)S(1)} %collective-permute-done.1.refs_3_, ...), custom_call_target="tpu_custom_call" | custom-call | tf_op jit(solution)/shard_map/couple/pallas_call | solution.py:74
  22.1 0.5 collective-permute-start.4
  22.7 1.1 %collective-permute-done.4 = f32[64,768]{1,0:T(8,128)S(1)} collective-permute-done((f32[64,768]{1,0:T(8,128)S(1)}, f32[64,768]{1,0:T(8,128)S(1)}, u32[]{:S(2)}, u32[]{:S(2)}) %collective-permute-start.4) | collective-permute-done | bytes 196640 | tf_op jit(solution)/shard_map/ppermute | solution.py:39
  23.8 4.1 %collective-permute-start.5 = (bf16[64,768]{1,0:T(8,128)(2,1)S(1)}, bf16[64,768]{1,0:T(8,128)(2,1)S(1)}, u32[]{:S(2)}, u32[]{:S(2)}) collective-permute-start(bf16[64,768]{1,0:T(8,128)(2,1)S(1)} %add_convert_fusion.2), channel_id=1, source_target_pairs={{0,2},{1,3},{2,0},{3,1},{4,6},{5,7},{6,4},{7,5},{8,10},{9,11},{10,... | collective-permute-start | bytes 294920 | tf_op jit(solution)/shard_map/ppermute | solution.py:39
  27.9 3.1 %collective-permute-done.5 = bf16[64,768]{1,0:T(8,128)(2,1)S(1)} collective-permute-done((bf16[64,768]{1,0:T(8,128)(2,1)S(1)}, bf16[64,768]{1,0:T(8,128)(2,1)S(1)}, u32[]{:S(2)}, u32[]{:S(2)}) %collective-permute-start.5) | collective-permute-done | bytes 98336 | tf_op jit(solution)/shard_map/ppermute | solution.py:39
  31.0 0.1 add_multiply_fusion
  31.1 0.2 fusion.5
  31.3 0.3 fusion.12
  31.6 0.4 convolution_bitcast_fusion
  32.0 0.2 copy.14
  32.2 0.1 fusion.2
  32.3 1.5 %collective-permute-start.6 = (bf16[560,128]{1,0:T(8,128)(2,1)S(1)}, bf16[560,128]{1,0:T(8,128)(2,1)S(1)}, u32[]{:S(2)}, u32[]{:S(2)}) collective-permute-start(bf16[560,128]{1,0:T(8,128)(2,1)S(1)} %dynamic-slice_bitcast_fusion), channel_id=1, source_target_pairs={{0,4},{1,5},{2,6},{3,7},{4,0},{5,1},{6,2},{7,3},{8,12},{9,13},{10,... | collective-permute-start | bytes 430088 | tf_op jit(solution)/shard_map/ppermute | solution.py:39
  33.8 3.8 %collective-permute-done.6 = bf16[560,128]{1,0:T(8,128)(2,1)S(1)} collective-permute-done((bf16[560,128]{1,0:T(8,128)(2,1)S(1)}, bf16[560,128]{1,0:T(8,128)(2,1)S(1)}, u32[]{:S(2)}, u32[]{:S(2)}) %collective-permute-start.6) | collective-permute-done | bytes 143392 | tf_op jit(solution)/shard_map/ppermute | solution.py:39
  37.6 0.8 %collective-permute-start.7 = (bf16[560,128]{1,0:T(8,128)(2,1)S(1)}, bf16[560,128]{1,0:T(8,128)(2,1)S(1)}, u32[]{:S(2)}, u32[]{:S(2)}) collective-permute-start(bf16[560,128]{1,0:T(8,128)(2,1)S(1)} %fusion.3), channel_id=1, source_target_pairs={{0,8},{1,9},{2,10},{3,11},{4,12},{5,13},{6,14},{7,15},{8,0},{9,1},... | collective-permute-start | bytes 430088 | tf_op jit(solution)/shard_map/ppermute | solution.py:39
  38.4 4.4 %collective-permute-done.7 = bf16[560,128]{1,0:T(8,128)(2,1)S(1)} collective-permute-done((bf16[560,128]{1,0:T(8,128)(2,1)S(1)}, bf16[560,128]{1,0:T(8,128)(2,1)S(1)}, u32[]{:S(2)}, u32[]{:S(2)}) %collective-permute-start.7) | collective-permute-done | bytes 143392 | tf_op jit(solution)/shard_map/ppermute | solution.py:39
  42.8 3.6 %collective-permute-start.8 = (bf16[560,128]{1,0:T(8,128)(2,1)S(1)}, bf16[560,128]{1,0:T(8,128)(2,1)S(1)}, u32[]{:S(2)}, u32[]{:S(2)}) collective-permute-start(bf16[560,128]{1,0:T(8,128)(2,1)S(1)} %add_convert_fusion.1), channel_id=1, source_target_pairs={{0,24},{1,25},{2,26},{3,27},{4,28},{5,29},{6,30},{7,31},{8,16},{9,... | collective-permute-start | bytes 430088 | tf_op jit(solution)/shard_map/ppermute | solution.py:39
  46.4 3.4 %collective-permute-done.8 = bf16[560,128]{1,0:T(8,128)(2,1)S(1)} collective-permute-done((bf16[560,128]{1,0:T(8,128)(2,1)S(1)}, bf16[560,128]{1,0:T(8,128)(2,1)S(1)}, u32[]{:S(2)}, u32[]{:S(2)}) %collective-permute-start.8) | collective-permute-done | bytes 143392 | tf_op jit(solution)/shard_map/ppermute | solution.py:39
  49.8 2.6 %collective-permute-start.11 = (bf16[560,128]{1,0:T(8,128)(2,1)S(1)}, bf16[560,128]{1,0:T(8,128)(2,1)S(1)}, u32[]{:S(2)}, u32[]{:S(2)}) collective-permute-start(bf16[560,128]{1,0:T(8,128)(2,1)S(1)} %add_convert_fusion), channel_id=1, source_target_pairs={{0,6},{1,7},{2,4},{3,5},{4,2},{5,3},{6,0},{7,1},{8,14},{9,15},{10,... | collective-permute-start | bytes 430088 | tf_op jit(solution)/shard_map/ppermute | solution.py:39
  52.4 0.4 collective-permute-start.10
  52.8 0.6 collective-permute-start.9
  53.4 2.5 %collective-permute-done.11 = bf16[560,128]{1,0:T(8,128)(2,1)S(1)} collective-permute-done((bf16[560,128]{1,0:T(8,128)(2,1)S(1)}, bf16[560,128]{1,0:T(8,128)(2,1)S(1)}, u32[]{:S(2)}, u32[]{:S(2)}) %collective-permute-start.11) | collective-permute-done | bytes 143392 | tf_op jit(solution)/shard_map/ppermute | solution.py:39
  55.9 1.6 %collective-permute-done.10 = bf16[560,128]{1,0:T(8,128)(2,1)S(1)} collective-permute-done((bf16[560,128]{1,0:T(8,128)(2,1)S(1)}, bf16[560,128]{1,0:T(8,128)(2,1)S(1)}, u32[]{:S(2)}, u32[]{:S(2)}) %collective-permute-start.10) | collective-permute-done | bytes 143392 | tf_op jit(solution)/shard_map/ppermute | solution.py:39
  57.5 0.4 collective-permute-done.9
  57.9 0.1 pad_maximum_fusion.refs_1_
  58.0 0.1 collective-permute-start.12
  58.1 0.1 pad_add_fusion.refs_0_
  58.2 0.7 %constant_dynamic-slice_fusion = f32[64,192]{1,0:T(8,128)} fusion(f32[64,768]{1,0:T(8,128)S(1)} %add_multiply_fusion, s32[]{:T(128)S(6)} %select_n.21), kind=kLoop, calls=%fused_computation.28 | loop fusion | bytes 98308 | tf_op jit(solution)/shard_map/dynamic_slice | solution.py:164
  58.9 1.6 %place.2 = (f32[1024,512]{1,0:T(8,128)}, f32[1,512]{1,0:T(1,128)}, f32[512,64]{1,0:T(8,128)S(1)}) custom-call(s32[3]{0:T(128)S(1)} %pad_add_fusion.refs_0_, bf16[4,560,128]{2,1,0:T(8,128)(2,1)S(1)} %pad_maximum_fusion.refs_1_), custom_call_target="tpu_custom_call" | custom-call | tf_op jit(solution)/shard_map/place/pallas_call | solution.py:123
  60.5 0.0 collective-permute-done.12.refs_1_
  60.5 1.6 %place.3 = (f32[1024,512]{1,0:T(8,128)}, f32[1,512]{1,0:T(1,128)}, f32[512,64]{1,0:T(8,128)S(1)}) custom-call(s32[3]{0:T(128)S(1)} %pad_add_fusion.refs_0_, bf16[4,560,128]{2,1,0:T(8,128)(2,1)S(1)} %collective-permute-done.12.refs_1_, f32[1024,512]{1,0:T(8,128)} %get-tuple-element.10.refs_2_, ...), custom_call_target="tpu_custom_call", output_to_operand_aliasing={{0}: (2, {}), {1}: (3, {}), {2}: (4, {})} | custom-call | tf_op jit(solution)/shard_map/place/pallas_call | solution.py:123
  62.0 0.8 %copy.15 = f32[512,64]{0,1:T(8,128)} copy(f32[512,64]{1,0:T(8,128)S(1)} %get-tuple-element.19) | data formatting | bytes 262144
  (8 shorter events, 0.2 us)
Async XLA Ops:
  0.6 7.9 %copy-start = (bf16[768,1024]{1,0:T(8,128)(2,1)S(1)}, bf16[768,1024]{1,0:T(8,128)(2,1)}, u32[]{:S(2)}) copy-start(bf16[768,1024]{1,0:T(8,128)(2,1)} %param.7) | copy-start | bytes 4718596
  2.6 8.1 %copy-start.2 = (bf16[512,64]{0,1:T(8,128)(2,1)S(1)}, bf16[512,64]{0,1:T(8,128)(2,1)}, u32[]{:S(2)}) copy-start(bf16[512,64]{0,1:T(8,128)(2,1)} %param.10) | copy-start | bytes 196612
  2.6 8.1 %copy-start.3 = (f32[64]{0:T(128)S(1)}, f32[64]{0:T(128)}, u32[]{:S(2)}) copy-start(f32[64]{0:T(128)} %param.11) | copy-start | bytes 772
  2.6 9.2 %copy-start.1 = (bf16[64,768]{1,0:T(8,128)(2,1)S(1)}, bf16[64,768]{1,0:T(8,128)(2,1)}, u32[]{:S(2)}) copy-start(bf16[64,768]{1,0:T(8,128)(2,1)} %param.13) | copy-start | bytes 294916
  2.6 9.3 %collective-permute-start.3 = (bf16[128,768]{1,0:T(8,128)(2,1)S(1)}, bf16[128,768]{1,0:T(8,128)(2,1)S(1)}, u32[]{:S(2)}, u32[]{:S(2)}) collective-permute-start(bf16[128,768]{1,0:T(8,128)(2,1)S(1)} %get-tuple-element.20), channel_id=1, source_target_pairs={{0,0},{13,1},{6,2},{11,3},{4,4},{9,5},{2,6},{15,7},{8,8},{5,9},{14... | collective-permute-start | bytes 589832 | tf_op jit(solution)/shard_map/ppermute | solution.py:30
  3.4 17.4 %collective-permute-start.1 = (bf16[128,768]{1,0:T(8,128)(2,1)S(1)}, bf16[128,768]{1,0:T(8,128)(2,1)S(1)}, u32[]{:S(2)}, u32[]{:S(2)}) collective-permute-start(bf16[128,768]{1,0:T(8,128)(2,1)S(1)} %get-tuple-element.20), channel_id=1, source_target_pairs={{20,0},{25,1},{18,2},{31,3},{16,4},{29,5},{22,6},{27,7},{28,8},{17... | collective-permute-start | bytes 589832 | tf_op jit(solution)/shard_map/ppermute | solution.py:30
  11.1 0.8 %collective-permute-start.2 = (bf16[64,768]{1,0:T(8,128)(2,1)S(1)}, bf16[64,768]{1,0:T(8,128)(2,1)S(1)}, u32[]{:S(2)}, u32[]{:S(2)}) collective-permute-start(bf16[64,768]{1,0:T(8,128)(2,1)S(1)} %fusion.1.refs_0_), channel_id=1, source_target_pairs={{0,0},{13,1},{6,2},{11,3},{4,4},{9,5},{2,6},{15,7},{8,8},{5,9},{14... | collective-permute-start | bytes 294920 | tf_op jit(solution)/shard_map/ppermute | solution.py:30
  11.7 9.1 %collective-permute-start = (bf16[64,768]{1,0:T(8,128)(2,1)S(1)}, bf16[64,768]{1,0:T(8,128)(2,1)S(1)}, u32[]{:S(2)}, u32[]{:S(2)}) collective-permute-start(bf16[64,768]{1,0:T(8,128)(2,1)S(1)} %fusion.1.refs_0_), channel_id=1, source_target_pairs={{20,0},{25,1},{18,2},{31,3},{16,4},{29,5},{22,6},{27,7},{28,8},{17... | collective-permute-start | bytes 294920 | tf_op jit(solution)/shard_map/ppermute | solution.py:30
  22.1 1.6 %collective-permute-start.4 = (f32[64,768]{1,0:T(8,128)S(1)}, f32[64,768]{1,0:T(8,128)S(1)}, u32[]{:S(2)}, u32[]{:S(2)}) collective-permute-start(f32[64,768]{1,0:T(8,128)S(1)} %couple.3), channel_id=1, source_target_pairs={{0,1},{1,0},{2,3},{3,2},{4,5},{5,4},{6,7},{7,6},{8,9},{9,8},{10,11... | collective-permute-start | bytes 589832 | tf_op jit(solution)/shard_map/ppermute | solution.py:39
  23.8 7.2 %collective-permute-start.5 = (bf16[64,768]{1,0:T(8,128)(2,1)S(1)}, bf16[64,768]{1,0:T(8,128)(2,1)S(1)}, u32[]{:S(2)}, u32[]{:S(2)}) collective-permute-start(bf16[64,768]{1,0:T(8,128)(2,1)S(1)} %add_convert_fusion.2), channel_id=1, source_target_pairs={{0,2},{1,3},{2,0},{3,1},{4,6},{5,7},{6,4},{7,5},{8,10},{9,11},{10,... | collective-permute-start | bytes 294920 | tf_op jit(solution)/shard_map/ppermute | solution.py:39
  32.3 5.3 %collective-permute-start.6 = (bf16[560,128]{1,0:T(8,128)(2,1)S(1)}, bf16[560,128]{1,0:T(8,128)(2,1)S(1)}, u32[]{:S(2)}, u32[]{:S(2)}) collective-permute-start(bf16[560,128]{1,0:T(8,128)(2,1)S(1)} %dynamic-slice_bitcast_fusion), channel_id=1, source_target_pairs={{0,4},{1,5},{2,6},{3,7},{4,0},{5,1},{6,2},{7,3},{8,12},{9,13},{10,... | collective-permute-start | bytes 430088 | tf_op jit(solution)/shard_map/ppermute | solution.py:39
  37.6 5.2 %collective-permute-start.7 = (bf16[560,128]{1,0:T(8,128)(2,1)S(1)}, bf16[560,128]{1,0:T(8,128)(2,1)S(1)}, u32[]{:S(2)}, u32[]{:S(2)}) collective-permute-start(bf16[560,128]{1,0:T(8,128)(2,1)S(1)} %fusion.3), channel_id=1, source_target_pairs={{0,8},{1,9},{2,10},{3,11},{4,12},{5,13},{6,14},{7,15},{8,0},{9,1},... | collective-permute-start | bytes 430088 | tf_op jit(solution)/shard_map/ppermute | solution.py:39
  42.8 7.0 %collective-permute-start.8 = (bf16[560,128]{1,0:T(8,128)(2,1)S(1)}, bf16[560,128]{1,0:T(8,128)(2,1)S(1)}, u32[]{:S(2)}, u32[]{:S(2)}) collective-permute-start(bf16[560,128]{1,0:T(8,128)(2,1)S(1)} %add_convert_fusion.1), channel_id=1, source_target_pairs={{0,24},{1,25},{2,26},{3,27},{4,28},{5,29},{6,30},{7,31},{8,16},{9,... | collective-permute-start | bytes 430088 | tf_op jit(solution)/shard_map/ppermute | solution.py:39
  49.8 6.1 %collective-permute-start.11 = (bf16[560,128]{1,0:T(8,128)(2,1)S(1)}, bf16[560,128]{1,0:T(8,128)(2,1)S(1)}, u32[]{:S(2)}, u32[]{:S(2)}) collective-permute-start(bf16[560,128]{1,0:T(8,128)(2,1)S(1)} %add_convert_fusion), channel_id=1, source_target_pairs={{0,6},{1,7},{2,4},{3,5},{4,2},{5,3},{6,0},{7,1},{8,14},{9,15},{10,... | collective-permute-start | bytes 430088 | tf_op jit(solution)/shard_map/ppermute | solution.py:39
  52.4 5.1 %collective-permute-start.10 = (bf16[560,128]{1,0:T(8,128)(2,1)S(1)}, bf16[560,128]{1,0:T(8,128)(2,1)S(1)}, u32[]{:S(2)}, u32[]{:S(2)}) collective-permute-start(bf16[560,128]{1,0:T(8,128)(2,1)S(1)} %add_convert_fusion), channel_id=1, source_target_pairs={{0,2},{1,3},{2,0},{3,1},{4,6},{5,7},{6,4},{7,5},{8,10},{9,11},{10,... | collective-permute-start | bytes 430088 | tf_op jit(solution)/shard_map/ppermute | solution.py:39
  52.8 5.1 %collective-permute-start.9 = (bf16[560,128]{1,0:T(8,128)(2,1)S(1)}, bf16[560,128]{1,0:T(8,128)(2,1)S(1)}, u32[]{:S(2)}, u32[]{:S(2)}) collective-permute-start(bf16[560,128]{1,0:T(8,128)(2,1)S(1)} %add_convert_fusion), channel_id=1, source_target_pairs={{0,4},{1,5},{2,6},{3,7},{4,0},{5,1},{6,2},{7,3},{8,12},{9,13},{10,... | collective-permute-start | bytes 430088 | tf_op jit(solution)/shard_map/ppermute | solution.py:39
  58.0 2.5 %collective-permute-start.12 = (bf16[4,560,128]{2,1,0:T(8,128)(2,1)S(1)}, bf16[4,560,128]{2,1,0:T(8,128)(2,1)S(1)}, u32[]{:S(2)}, u32[]{:S(2)}) collective-permute-start(bf16[4,560,128]{2,1,0:T(8,128)(2,1)S(1)} %pad_maximum_fusion.refs_1_), channel_id=1, source_target_pairs={{0,1},{1,0},{2,3},{3,2},{4,5},{5,4},{6,7},{7,6},{8,9},{9,8},{10,11... | collective-permute-start | bytes 1720328 | tf_op jit(solution)/shard_map/ppermute | solution.py:39

commit v3 on v2

--- a/solution.py
+++ b/solution.py
@@ -6,6 +6,7 @@
 from jax.experimental import pallas as pl
 from jax.experimental.pallas import tpu as pltpu
 from jax.sharding import PartitionSpec as P
+
 
 AXES = ("blk", "rep")
 BF16 = jnp.bfloat16
@@ -30,17 +31,43 @@
     return lax.ppermute(array, AXES, route)
 
 
-def swap(array, blk_mask, rep_mask, blocks, reps):
+def swap(array, blk_masks, rep_mask, blocks, reps):
     route = [
-        (b * reps + r, (b ^ blk_mask) * reps + (r ^ rep_mask))
+        (b * reps + r, (b ^ blk_masks[r & 1]) * reps + (r ^ rep_mask))
         for b in range(blocks)
         for r in range(reps)
     ]
     return lax.ppermute(array, AXES, route)
 
 
+def join_kernel(first, second, joined, sems):
+    count = first.shape[0]
+    copies = [
+        pltpu.make_async_copy(first, joined.at[:count], sems.at[0]),
+        pltpu.make_async_copy(second, joined.at[count:], sems.at[1]),
+    ]
+    for copy in copies:
+        copy.start()
+    for copy in copies:
+        copy.wait()
+
+
+def join(first, second):
+    count, rows = first.shape
+    return pl.pallas_call(
+        join_kernel,
+        out_shape=pltpu.VMEM((2 * count, rows), first.dtype),
+        in_specs=[pl.BlockSpec(memory_space=pl.ANY)] * 2,
+        out_specs=pl.BlockSpec(memory_space=pltpu.VMEM),
+        scratch_shapes=[pltpu.SemaphoreType.DMA((2,))],
+        name="join",
+    )(first, second)
+
+
 def couple_kernel(chunk, own_y, own_pair, vis_y, vis_pair, before, after):
     feat, rows = own_y.shape
+    count = own_pair.shape[0] // 2
+    crossed = jnp.concatenate([own_pair[count:], own_pair[:count]], axis=0)
     own = own_y[...]
     own32 = own.astype(F32)
     own_half = 0.5 * jnp.sum(own32 * own32, axis=0, keepdims=True)
@@ -53,7 +80,7 @@
         cross = jnp.dot(turned.astype(BF16), own, preferred_element_type=F32)
         coupling = lax.dot_general(
             vis_pair[:, start : start + chunk],
-            own_pair[...],
+            crossed,
             (((0,), (0,)), ((), ())),
             preferred_element_type=F32,
         )
@@ -81,49 +108,49 @@
     )(*map(in_vmem, (own_y, own_pair, vis_y, vis_pair, drift)))
 
 
-def place_kernel(depth, offset, where, table, *refs):
-    w_in, b_in, w_out = refs[-3:]
-    din = w_in.shape[0]
-    half = din // 2
-    base = 2 * (pl.program_id(0) ^ where[0])
-    low = table.at[base + where[1]]
-    high = table.at[base + (1 - where[1])]
-    w_in[:half] = low[:half].astype(F32)
-    w_in[half:] = high[:half].astype(F32)
-    turned = jnp.concatenate(
-        [low[half : half + depth].astype(F32), high[half : half + depth].astype(F32)], axis=0
-    )
-    w_out[...] = turned.T
-    b_in[...] = low[half + depth : half + depth + 16].astype(F32)[:1]
-
-
-def place(table, where, offset, din, feat, reps, earlier):
+def place_kernel(where, table, *refs):
+    w_in, b_in, w_out, wide, sems = refs[-5:]
+    rows, depth = w_in.shape[0] // 2, w_out.shape[0] // 2
+    cols = table.shape[2]
+    copies = []
+    for index in range(table.shape[0]):
+        chip, half = divmod(index, 2)
+        wide[index] = table[index].astype(F32)
+        side = where[0] ^ half
+        column = pl.ds(pl.multiple_of((2 * (where[1] ^ chip) + where[2]) * cols, cols), cols)
+        sources = [wide.at[index, :rows], wide.at[index, rows : rows + depth]]
+        targets = [
+            w_in.at[pl.ds(pl.multiple_of(side * rows, rows), rows), column],
+            w_out.at[pl.ds(pl.multiple_of(side * depth, depth), depth), column],
+        ]
+        if half == 0:
+            sources.append(wide.at[index, rows + depth : rows + depth + 1])
+            targets.append(b_in.at[:, column])
+        for source, target in zip(sources, targets):
+            copy = pltpu.make_async_copy(source, target, sems.at[len(copies)])
+            copy.start()
+            copies.append(copy)
+    for copy in copies:
+        copy.wait()
+
+
+def place(table, where, din, feat, hid, earlier):
     count, height, cols = table.shape
-    hid = cols * reps
     shapes = (
         jax.ShapeDtypeStruct((din, hid), F32),
         jax.ShapeDtypeStruct((1, hid), F32),
-        jax.ShapeDtypeStruct((hid, feat), F32),
-    )
-
-    def column(i, at):
-        return 2 * i + (at[2] ^ offset)
-
-    grid_spec = pltpu.PrefetchScalarGridSpec(
-        num_scalar_prefetch=1,
-        grid=(reps // 2,),
-        in_specs=[pl.BlockSpec(memory_space=pltpu.VMEM)]
+        jax.ShapeDtypeStruct((feat, hid), F32),
+    )
+    return pl.pallas_call(
+        place_kernel,
+        out_shape=shapes,
+        in_specs=[pl.BlockSpec(memory_space=pltpu.SMEM), pl.BlockSpec(memory_space=pltpu.VMEM)]
         + [pl.BlockSpec(memory_space=pl.ANY) for _ in earlier],
-        out_specs=[
-            pl.BlockSpec((din, cols), lambda i, at: (0, column(i, at))),
-            pl.BlockSpec((1, cols), lambda i, at: (0, column(i, at))),
-            pl.BlockSpec((cols, feat), lambda i, at: (column(i, at), 0)),
+        out_specs=[pl.BlockSpec(memory_space=pl.ANY)] * 3,
+        scratch_shapes=[
+            pltpu.VMEM((count, height, cols), F32),
+            pltpu.SemaphoreType.DMA((3 * count,)),
         ],
-    )
-    return pl.pallas_call(
-        lambda *refs: place_kernel(feat // 2, offset, *refs),
-        out_shape=shapes,
-        grid_spec=grid_spec,
         input_output_aliases={2 + i: i for i in range(len(earlier))},
         compiler_params=pltpu.CompilerParams(vmem_limit_bytes=16 << 20),
         name="place",
@@ -142,23 +169,29 @@
     quarter = rows // reps
     cols = hid // reps
 
+    pair = join(probes, solves)
     hidden = jnp.tanh(jnp.dot(points, w_in, preferred_element_type=F32) + b_in).astype(BF16)
     pre = lax.dot_general(w_out, hidden, (((0,), (1,)), ((), ())), preferred_element_type=F32)
     scaled = (pre * inv_scale[:, None]).astype(BF16)
-    own_pair = jnp.concatenate([solves, probes], axis=0)
-    pair = jnp.concatenate([probes, solves], axis=0)
     steps = range(blocks // reps)
     masks = [[visit_mask(step, r, reps) for r in range(reps)] for step in steps]
-    pairs = [fetch(pair, masks[step], blocks, reps) for step in steps]
-    scaleds = [fetch(scaled, masks[step], blocks, reps) for step in steps]
+    near, far = masks[0], masks[1:]
+    pairs = [fetch(pair, far[0], blocks, reps)]
+    pairs += [fetch(pair, mask, blocks, reps) for mask in far[1:]]
+    scaleds = [fetch(scaled, far[0], blocks, reps)]
+    scaleds += [fetch(scaled, mask, blocks, reps) for mask in far[1:]]
+    near_scaled = fetch(scaled, near, blocks, reps)
+    near_pair, scaled = lax.optimization_barrier((pair, scaled))
+    near_pair = fetch(near_pair, near, blocks, reps)
     drift = jnp.zeros((feat, rows), F32)
-    for step in steps:
-        drift = couple(scaled, own_pair, scaleds[step], pairs[step], drift)
-
-    drift = drift + swap(drift, 0, 1, blocks, reps)
+    drift = couple(scaled, pair, near_scaled, near_pair, drift)
+    for vis_y, vis_pair in zip(scaleds, pairs):
+        drift = couple(scaled, pair, vis_y, vis_pair, drift)
+
+    drift = drift + swap(drift, (0, 0), 1, blocks, reps)
     for bit in range(1, bits_of(reps)):
         sent = drift.astype(BF16)
-        got = swap(sent, 0, 1 << bit, blocks, reps)
+        got = swap(sent, (0, 0), 1 << bit, blocks, reps)
         drift = sent.astype(F32) + got.astype(F32)
     full_grad = drift * inv_scale[:, None]
     feat_grad = lax.dynamic_slice_in_dim(full_grad, rep_index * quarter, quarter, 1)
@@ -186,22 +219,29 @@
     )
     halves = (halves * norm).astype(BF16)
 
-    side = blk_index % 2
+    same = (0, 0)
+    side = blk_index & 1
+    core = rep_index & 1
     kept = lax.dynamic_index_in_dim(halves, side, 0, keepdims=False)
     sent = lax.dynamic_index_in_dim(halves, 1 - side, 0, keepdims=False)
-    got = swap(sent, 1, 0, blocks, reps)
+    got = swap(sent, (1, 1), 0, blocks, reps)
     part = (kept.astype(F32) + got.astype(F32)).astype(BF16)
     for bit in range(1, bits_of(blocks)):
-        got = swap(part, (2 << bit) - 2, 0, blocks, reps)
+        distance = (2 << bit) - 2
+        got = swap(part, (distance, distance), 0, blocks, reps)
         part = (part.astype(F32) + got.astype(F32)).astype(BF16)
 
-    masks = [(h, r << 1) for r in range(reps // 2) for h in range(2)]
-    pieces = [part] + [swap(part, h, r, blocks, reps) for h, r in masks[1:]]
+    pieces = [part]
+    for index in range(1, reps):
+        chip, half = divmod(index, 2)
+        pieces.append(swap(part, (half, half), chip << 1, blocks, reps))
     near = jnp.stack(pieces)
-    other = swap(near, 0, 1, blocks, reps)
-    where = jnp.stack([rep_index >> 1, side, rep_index & 1])
-    outs = place(near, where, 0, din, feat, reps, ())
-    grad_w_in, grad_b_in, grad_w_out = place(other, where, 1, din, feat, reps, outs)
+    other = swap(near, same, 1, blocks, reps)
+    chip = rep_index >> 1
+    outs = place(near, jnp.stack([side, chip, core]), din, feat, hid, ())
+    outs = place(other, jnp.stack([side, chip, 1 - core]), din, feat, hid, outs)
+    grad_w_in, grad_b_in, grad_w_out = outs
+    grad_w_out = grad_w_out.T
     grad_b_in = grad_b_in.reshape(hid)
     return (feat_grad, grad_w_in, grad_b_in, grad_w_out)
 
@@ -209,6 +249,7 @@
 def solution(mesh):
     in_specs = (P("blk", None), P(), P(), P(), P(), P(None, "blk"), P(None, "blk"))
     out_specs = (P(None, ("blk", "rep")), P(), P(), P())
+
     return jax.shard_map(
         on_device, mesh=mesh, in_specs=in_specs, out_specs=out_specs, check_vma=False
     )

time: 63 us -> 64.5 us (1.024)
  waiting for transfers between devices: 27.9 us -> 31.4 us
  local copies, waits for them, and re-layouts: 3.68 us -> 1.37 us
  Pallas kernels: 5.79 us -> 7 us
  starting transfers between devices: 20.8 us -> 19.7 us
    ppermute x4, waiting for transfers between devices: 7.61 us -> 10.8 us  [fetch(): return lax.ppermute(array, AXES, route)]
    unnamed x10 -> x6, local copies, waits for them, and re-layouts: 1.82 us -> 0.42 us
    pallas_call x2 -> x3, Pallas kernels: 3.17 us -> 4.38 us  [the longest x2 3.3 us: place(): pl.pallas_call(place_kernel, out_shape=shapes, in_specs=[pl.BlockSpec(mem...]
    concatenate x2 -> x0, local copies, waits for them, and re-layouts: 0.91 us -> none  [the longest x1 0.91 us: on_device(): pair = jnp.concatenate([probes, solves], axis=0)]
    ppermute x9, starting transfers between devices: 14.1 us -> 13.2 us  [swap(): return lax.ppermute(array, AXES, route)]
  transfers between devices with their start and end apart: 13 -> 13, of which waited for: 9 -> 9; matrix products, arithmetic and copies ran while one was open for 5% -> 1% of each run, Pallas kernels for 5% -> 5%
where the time goes in v3:
time: 64.5 us; the launch traced here: 64.3 us
  waiting for transfers between devices  31.4 us (49%)
  starting transfers between devices  19.7 us (31%)
  Pallas kernels  7 us (11%)
  matrix products  3.46 us (5%)
  local copies, waits for them, and re-layouts  1.37 us (2%)
  between operations  0.84 us (1%)
    ppermute x9, waiting for transfers between devices, swap(): return lax.ppermute(array, AXES, route)  20.6 us
    ppermute x9, starting transfers between devices, swap(): return lax.ppermute(array, AXES, route)  13.2 us
    ppermute x4, waiting for transfers between devices, fetch(): return lax.ppermute(array, AXES, route)  10.8 us
    ppermute x4, starting transfers between devices, fetch(): return lax.ppermute(array, AXES, route)  6.48 us
    pallas_call x2, Pallas kernels, place(): pl.pallas_call(place_kernel, out_shape=shapes, in_specs=[pl.BlockSpec(mem...  3.3 us
    pallas_call x2, Pallas kernels, couple(): pl.pallas_call(lambda *refs: couple_kernel(chunk, *refs), out_shape=pltpu...  2.62 us
    dot_general x1, matrix products, on_device(): jnp.dot(points, w_in, preferred_element_type=F32) + b_in  2.24 us
  transfers between devices with their start and end apart: 13, of which 9 were waited for; matrix products, arithmetic and copies ran while one was open for 1% of the time, Pallas kernels for 5%

profile of v3, /device:TPU:0, one launch (start us, length us, event | category | flops | bytes accessed | tf_op | source)
XLA Modules:
  0.0 64.3 jit_solution(4372603478636954712)
XLA Ops:
  0.6 0.0 copy-start
  0.6 1.1 %join.1.refs_1_ = bf16[128,768]{1,0:T(8,128)(2,1)S(1)} custom-call(bf16[64,768]{1,0:T(8,128)(2,1)} %first.1, bf16[64,768]{1,0:T(8,128)(2,1)} %second.1), custom_call_target="tpu_custom_call" | custom-call | tf_op jit(solution)/shard_map/join/pallas_call | solution.py:57
  1.7 0.4 copy-done
  2.1 0.0 copy-start.1
  2.1 0.0 copy-start.2
  2.1 2.2 %tanh_convert_fusion = bf16[768,512]{1,0:T(8,128)(2,1)S(1)} fusion(bf16[768,1024]{1,0:T(8,128)(2,1)S(1)} %copy-done, bf16[1024,512]{1,0:T(8,128)(2,1)} %param.8, f32[512]{0:T(512)} %param.9), kind=kOutput, calls=%fused_computation | convolution fusion | flops 806092800 | bytes 3409920 | tf_op jit(solution)/shard_map/dot_general | solution.py:173
  4.4 0.0 copy-done.1
  4.4 0.0 copy-done.2
  4.4 0.3 fusion.1.refs_0_
  4.8 0.7 %collective-permute-start.3 = (bf16[128,768]{1,0:T(8,128)(2,1)S(1)}, bf16[128,768]{1,0:T(8,128)(2,1)S(1)}, u32[]{:S(2)}, u32[]{:S(2)}) collective-permute-start(bf16[128,768]{1,0:T(8,128)(2,1)S(1)} %join.1.refs_1_), channel_id=1, source_target_pairs={{0,0},{13,1},{6,2},{11,3},{4,4},{9,5},{2,6},{15,7},{8,8},{5,9},{14... | collective-permute-start | bytes 589832 | tf_op jit(solution)/shard_map/ppermute | solution.py:31
  5.4 5.1 %collective-permute-start.1 = (bf16[128,768]{1,0:T(8,128)(2,1)S(1)}, bf16[128,768]{1,0:T(8,128)(2,1)S(1)}, u32[]{:S(2)}, u32[]{:S(2)}) collective-permute-start(bf16[128,768]{1,0:T(8,128)(2,1)S(1)} %join.1.refs_1_), channel_id=1, source_target_pairs={{20,0},{25,1},{18,2},{31,3},{16,4},{29,5},{22,6},{27,7},{28,8},{17... | collective-permute-start | bytes 589832 | tf_op jit(solution)/shard_map/ppermute | solution.py:31
  10.5 0.7 %collective-permute-start.2 = (bf16[64,768]{1,0:T(8,128)(2,1)S(1)}, bf16[64,768]{1,0:T(8,128)(2,1)S(1)}, u32[]{:S(2)}, u32[]{:S(2)}) collective-permute-start(bf16[64,768]{1,0:T(8,128)(2,1)S(1)} %fusion.1.refs_0_), channel_id=1, source_target_pairs={{0,0},{13,1},{6,2},{11,3},{4,4},{9,5},{2,6},{15,7},{8,8},{5,9},{14... | collective-permute-start | bytes 294920 | tf_op jit(solution)/shard_map/ppermute | solution.py:31
  11.2 0.1 collective-permute-start
  11.3 0.0 collective-permute-done.2.refs_2_
  11.3 0.0 collective-permute-done.3.refs_3_
  11.3 1.3 %couple.2.refs_4_ = f32[64,768]{1,0:T(8,128)S(1)} custom-call(bf16[64,768]{1,0:T(8,128)(2,1)S(1)} %fusion.1.refs_0_, bf16[128,768]{1,0:T(8,128)(2,1)S(1)} %join.1.refs_1_, bf16[64,768]{1,0:T(8,128)(2,1)S(1)} %collective-permute-done.2.refs_2_, bf16[128,768]{1,0:T(8,128)(2,1)S(1)} %collective-permute-done.3.refs_3_, f32[64,768]{1,0:T(8,128)S(1)} %broadcast_in_dim.4.refs_4_), custom_call_target="tpu_custom_call" | custom-call | tf_op jit(solution)/shard_map/couple/pallas_call | solution.py:101
  12.6 10.8 %collective-permute-done.refs_2_ = bf16[64,768]{1,0:T(8,128)(2,1)S(1)} collective-permute-done((bf16[64,768]{1,0:T(8,128)(2,1)S(1)}, bf16[64,768]{1,0:T(8,128)(2,1)S(1)}, u32[]{:S(2)}, u32[]{:S(2)}) %collective-permute-start) | collective-permute-done | bytes 98336 | tf_op jit(solution)/shard_map/ppermute | solution.py:31
  23.4 0.0 collective-permute-done.1.refs_3_
  23.4 1.3 %couple.3 = f32[64,768]{1,0:T(8,128)S(1)} custom-call(bf16[64,768]{1,0:T(8,128)(2,1)S(1)} %fusion.1.refs_0_, bf16[128,768]{1,0:T(8,128)(2,1)S(1)} %join.1.refs_1_, bf16[64,768]{1,0:T(8,128)(2,1)S(1)} %collective-permute-done.refs_2_, bf16[128,768]{1,0:T(8,128)(2,1)S(1)} %collective-permute-done.1.refs_3_, f32[64,768]{1,0:T(8,128)S(1)} %couple.2.refs_4_), custom_call_target="tpu_custom_call" | custom-call | tf_op jit(solution)/shard_map/couple/pallas_call | solution.py:101
  24.7 0.1 collective-permute-start.4
  24.8 1.4 %collective-permute-done.4 = f32[64,768]{1,0:T(8,128)S(1)} collective-permute-done((f32[64,768]{1,0:T(8,128)S(1)}, f32[64,768]{1,0:T(8,128)S(1)}, u32[]{:S(2)}, u32[]{:S(2)}) %collective-permute-start.4) | collective-permute-done | bytes 196640 | tf_op jit(solution)/shard_map/ppermute | solution.py:40
  26.2 3.7 %collective-permute-start.5 = (bf16[64,768]{1,0:T(8,128)(2,1)S(1)}, bf16[64,768]{1,0:T(8,128)(2,1)S(1)}, u32[]{:S(2)}, u32[]{:S(2)}) collective-permute-start(bf16[64,768]{1,0:T(8,128)(2,1)S(1)} %add_convert_fusion.2), channel_id=1, source_target_pairs={{0,2},{1,3},{2,0},{3,1},{4,6},{5,7},{6,4},{7,5},{8,10},{9,11},{10,... | collective-permute-start | bytes 294920 | tf_op jit(solution)/shard_map/ppermute | solution.py:40
  29.9 3.1 %collective-permute-done.5 = bf16[64,768]{1,0:T(8,128)(2,1)S(1)} collective-permute-done((bf16[64,768]{1,0:T(8,128)(2,1)S(1)}, bf16[64,768]{1,0:T(8,128)(2,1)S(1)}, u32[]{:S(2)}, u32[]{:S(2)}) %collective-permute-start.5) | collective-permute-done | bytes 98336 | tf_op jit(solution)/shard_map/ppermute | solution.py:40
  33.0 0.1 add_multiply_fusion
  33.1 0.2 fusion.5
  33.3 0.3 fusion.12
  33.6 0.4 convolution_bitcast_fusion
  34.0 0.2 copy.14
  34.2 0.1 fusion.2
  34.3 1.5 %collective-permute-start.6 = (bf16[560,128]{1,0:T(8,128)(2,1)S(1)}, bf16[560,128]{1,0:T(8,128)(2,1)S(1)}, u32[]{:S(2)}, u32[]{:S(2)}) collective-permute-start(bf16[560,128]{1,0:T(8,128)(2,1)S(1)} %dynamic-slice_bitcast_fusion), channel_id=1, source_target_pairs={{0,4},{1,5},{2,6},{3,7},{4,0},{5,1},{6,2},{7,3},{8,12},{9,13},{10,... | collective-permute-start | bytes 430088 | tf_op jit(solution)/shard_map/ppermute | solution.py:40
  35.8 3.8 %collective-permute-done.6 = bf16[560,128]{1,0:T(8,128)(2,1)S(1)} collective-permute-done((bf16[560,128]{1,0:T(8,128)(2,1)S(1)}, bf16[560,128]{1,0:T(8,128)(2,1)S(1)}, u32[]{:S(2)}, u32[]{:S(2)}) %collective-permute-start.6) | collective-permute-done | bytes 143392 | tf_op jit(solution)/shard_map/ppermute | solution.py:40
  39.6 0.8 %collective-permute-start.7 = (bf16[560,128]{1,0:T(8,128)(2,1)S(1)}, bf16[560,128]{1,0:T(8,128)(2,1)S(1)}, u32[]{:S(2)}, u32[]{:S(2)}) collective-permute-start(bf16[560,128]{1,0:T(8,128)(2,1)S(1)} %fusion.3), channel_id=1, source_target_pairs={{0,8},{1,9},{2,10},{3,11},{4,12},{5,13},{6,14},{7,15},{8,0},{9,1},... | collective-permute-start | bytes 430088 | tf_op jit(solution)/shard_map/ppermute | solution.py:40
  40.4 4.4 %collective-permute-done.7 = bf16[560,128]{1,0:T(8,128)(2,1)S(1)} collective-permute-done((bf16[560,128]{1,0:T(8,128)(2,1)S(1)}, bf16[560,128]{1,0:T(8,128)(2,1)S(1)}, u32[]{:S(2)}, u32[]{:S(2)}) %collective-permute-start.7) | collective-permute-done | bytes 143392 | tf_op jit(solution)/shard_map/ppermute | solution.py:40
  44.9 3.6 %collective-permute-start.8 = (bf16[560,128]{1,0:T(8,128)(2,1)S(1)}, bf16[560,128]{1,0:T(8,128)(2,1)S(1)}, u32[]{:S(2)}, u32[]{:S(2)}) collective-permute-start(bf16[560,128]{1,0:T(8,128)(2,1)S(1)} %add_convert_fusion.1), channel_id=1, source_target_pairs={{0,24},{1,25},{2,26},{3,27},{4,28},{5,29},{6,30},{7,31},{8,16},{9,... | collective-permute-start | bytes 430088 | tf_op jit(solution)/shard_map/ppermute | solution.py:40
  48.4 3.4 %collective-permute-done.8 = bf16[560,128]{1,0:T(8,128)(2,1)S(1)} collective-permute-done((bf16[560,128]{1,0:T(8,128)(2,1)S(1)}, bf16[560,128]{1,0:T(8,128)(2,1)S(1)}, u32[]{:S(2)}, u32[]{:S(2)}) %collective-permute-start.8) | collective-permute-done | bytes 143392 | tf_op jit(solution)/shard_map/ppermute | solution.py:40
  51.9 2.6 %collective-permute-start.11 = (bf16[560,128]{1,0:T(8,128)(2,1)S(1)}, bf16[560,128]{1,0:T(8,128)(2,1)S(1)}, u32[]{:S(2)}, u32[]{:S(2)}) collective-permute-start(bf16[560,128]{1,0:T(8,128)(2,1)S(1)} %add_convert_fusion), channel_id=1, source_target_pairs={{0,6},{1,7},{2,4},{3,5},{4,2},{5,3},{6,0},{7,1},{8,14},{9,15},{10,... | collective-permute-start | bytes 430088 | tf_op jit(solution)/shard_map/ppermute | solution.py:40
  54.4 0.4 collective-permute-start.10
  54.8 0.6 collective-permute-start.9
  55.4 2.5 %collective-permute-done.11 = bf16[560,128]{1,0:T(8,128)(2,1)S(1)} collective-permute-done((bf16[560,128]{1,0:T(8,128)(2,1)S(1)}, bf16[560,128]{1,0:T(8,128)(2,1)S(1)}, u32[]{:S(2)}, u32[]{:S(2)}) %collective-permute-start.11) | collective-permute-done | bytes 143392 | tf_op jit(solution)/shard_map/ppermute | solution.py:40
  57.9 1.6 %collective-permute-done.10 = bf16[560,128]{1,0:T(8,128)(2,1)S(1)} collective-permute-done((bf16[560,128]{1,0:T(8,128)(2,1)S(1)}, bf16[560,128]{1,0:T(8,128)(2,1)S(1)}, u32[]{:S(2)}, u32[]{:S(2)}) %collective-permute-start.10) | collective-permute-done | bytes 143392 | tf_op jit(solution)/shard_map/ppermute | solution.py:40
  59.5 0.4 collective-permute-done.9
  59.9 0.1 pad_maximum_fusion.table
  60.0 0.1 collective-permute-start.12
  60.1 0.1 pad_add_fusion.2.where
  60.2 0.1 pad_add_fusion.where
  60.3 0.7 %constant_dynamic-slice_fusion = f32[64,192]{1,0:T(8,128)} fusion(f32[64,768]{1,0:T(8,128)S(1)} %add_multiply_fusion, s32[]{:T(128)S(6)} %select_n.14), kind=kLoop, calls=%fused_computation.24 | loop fusion | bytes 98308 | tf_op jit(solution)/shard_map/dynamic_slice | solution.py:197
  61.0 1.6 %place.2 = (f32[1024,512]{1,0:T(8,128)}, f32[1,512]{1,0:T(1,128)}, f32[64,512]{1,0:T(8,128)}) custom-call(s32[3]{0:T(128)S(1)} %pad_add_fusion.2.where, bf16[4,560,128]{2,1,0:T(8,128)(2,1)S(1)} %pad_maximum_fusion.table), custom_call_target="tpu_custom_call" | custom-call | tf_op jit(solution)/shard_map/place/pallas_call | solution.py:144
  62.6 0.0 collective-permute-done.12.table
  62.6 1.7 %place.3 = (f32[1024,512]{1,0:T(8,128)}, f32[1,512]{1,0:T(1,128)}, f32[64,512]{1,0:T(8,128)}) custom-call(s32[3]{0:T(128)S(1)} %pad_add_fusion.where, bf16[4,560,128]{2,1,0:T(8,128)(2,1)S(1)} %collective-permute-done.12.table, f32[1024,512]{1,0:T(8,128)} %get-tuple-element.14.refs_0_, ...), custom_call_target="tpu_custom_call", output_to_operand_aliasing={{0}: (2, {}), {1}: (3, {}), {2}: (4, {})} | custom-call | tf_op jit(solution)/shard_map/place/pallas_call | solution.py:144
  (7 shorter events, 0.2 us)
Async XLA Ops:
  0.6 1.5 %copy-start = (bf16[768,1024]{1,0:T(8,128)(2,1)S(1)}, bf16[768,1024]{1,0:T(8,128)(2,1)}, u32[]{:S(2)}) copy-start(bf16[768,1024]{1,0:T(8,128)(2,1)} %param.7) | copy-start | bytes 4718596
  2.1 2.3 %copy-start.1 = (bf16[512,64]{0,1:T(8,128)(2,1)S(1)}, bf16[512,64]{0,1:T(8,128)(2,1)}, u32[]{:S(2)}) copy-start(bf16[512,64]{0,1:T(8,128)(2,1)} %param.10) | copy-start | bytes 196612
  2.1 2.3 %copy-start.2 = (f32[64]{0:T(128)S(1)}, f32[64]{0:T(128)}, u32[]{:S(2)}) copy-start(f32[64]{0:T(128)} %param.11) | copy-start | bytes 772
  4.8 6.5 %collective-permute-start.3 = (bf16[128,768]{1,0:T(8,128)(2,1)S(1)}, bf16[128,768]{1,0:T(8,128)(2,1)S(1)}, u32[]{:S(2)}, u32[]{:S(2)}) collective-permute-start(bf16[128,768]{1,0:T(8,128)(2,1)S(1)} %join.1.refs_1_), channel_id=1, source_target_pairs={{0,0},{13,1},{6,2},{11,3},{4,4},{9,5},{2,6},{15,7},{8,8},{5,9},{14... | collective-permute-start | bytes 589832 | tf_op jit(solution)/shard_map/ppermute | solution.py:31
  5.4 17.9 %collective-permute-start.1 = (bf16[128,768]{1,0:T(8,128)(2,1)S(1)}, bf16[128,768]{1,0:T(8,128)(2,1)S(1)}, u32[]{:S(2)}, u32[]{:S(2)}) collective-permute-start(bf16[128,768]{1,0:T(8,128)(2,1)S(1)} %join.1.refs_1_), channel_id=1, source_target_pairs={{20,0},{25,1},{18,2},{31,3},{16,4},{29,5},{22,6},{27,7},{28,8},{17... | collective-permute-start | bytes 589832 | tf_op jit(solution)/shard_map/ppermute | solution.py:31
  10.5 0.8 %collective-permute-start.2 = (bf16[64,768]{1,0:T(8,128)(2,1)S(1)}, bf16[64,768]{1,0:T(8,128)(2,1)S(1)}, u32[]{:S(2)}, u32[]{:S(2)}) collective-permute-start(bf16[64,768]{1,0:T(8,128)(2,1)S(1)} %fusion.1.refs_0_), channel_id=1, source_target_pairs={{0,0},{13,1},{6,2},{11,3},{4,4},{9,5},{2,6},{15,7},{8,8},{5,9},{14... | collective-permute-start | bytes 294920 | tf_op jit(solution)/shard_map/ppermute | solution.py:31
  11.2 12.2 %collective-permute-start = (bf16[64,768]{1,0:T(8,128)(2,1)S(1)}, bf16[64,768]{1,0:T(8,128)(2,1)S(1)}, u32[]{:S(2)}, u32[]{:S(2)}) collective-permute-start(bf16[64,768]{1,0:T(8,128)(2,1)S(1)} %fusion.1.refs_0_), channel_id=1, source_target_pairs={{20,0},{25,1},{18,2},{31,3},{16,4},{29,5},{22,6},{27,7},{28,8},{17... | collective-permute-start | bytes 294920 | tf_op jit(solution)/shard_map/ppermute | solution.py:31
  24.7 1.5 %collective-permute-start.4 = (f32[64,768]{1,0:T(8,128)S(1)}, f32[64,768]{1,0:T(8,128)S(1)}, u32[]{:S(2)}, u32[]{:S(2)}) collective-permute-start(f32[64,768]{1,0:T(8,128)S(1)} %couple.3), channel_id=1, source_target_pairs={{0,1},{1,0},{2,3},{3,2},{4,5},{5,4},{6,7},{7,6},{8,9},{9,8},{10,11... | collective-permute-start | bytes 589832 | tf_op jit(solution)/shard_map/ppermute | solution.py:40
  26.2 6.8 %collective-permute-start.5 = (bf16[64,768]{1,0:T(8,128)(2,1)S(1)}, bf16[64,768]{1,0:T(8,128)(2,1)S(1)}, u32[]{:S(2)}, u32[]{:S(2)}) collective-permute-start(bf16[64,768]{1,0:T(8,128)(2,1)S(1)} %add_convert_fusion.2), channel_id=1, source_target_pairs={{0,2},{1,3},{2,0},{3,1},{4,6},{5,7},{6,4},{7,5},{8,10},{9,11},{10,... | collective-permute-start | bytes 294920 | tf_op jit(solution)/shard_map/ppermute | solution.py:40
  34.3 5.3 %collective-permute-start.6 = (bf16[560,128]{1,0:T(8,128)(2,1)S(1)}, bf16[560,128]{1,0:T(8,128)(2,1)S(1)}, u32[]{:S(2)}, u32[]{:S(2)}) collective-permute-start(bf16[560,128]{1,0:T(8,128)(2,1)S(1)} %dynamic-slice_bitcast_fusion), channel_id=1, source_target_pairs={{0,4},{1,5},{2,6},{3,7},{4,0},{5,1},{6,2},{7,3},{8,12},{9,13},{10,... | collective-permute-start | bytes 430088 | tf_op jit(solution)/shard_map/ppermute | solution.py:40
  39.6 5.2 %collective-permute-start.7 = (bf16[560,128]{1,0:T(8,128)(2,1)S(1)}, bf16[560,128]{1,0:T(8,128)(2,1)S(1)}, u32[]{:S(2)}, u32[]{:S(2)}) collective-permute-start(bf16[560,128]{1,0:T(8,128)(2,1)S(1)} %fusion.3), channel_id=1, source_target_pairs={{0,8},{1,9},{2,10},{3,11},{4,12},{5,13},{6,14},{7,15},{8,0},{9,1},... | collective-permute-start | bytes 430088 | tf_op jit(solution)/shard_map/ppermute | solution.py:40
  44.9 7.0 %collective-permute-start.8 = (bf16[560,128]{1,0:T(8,128)(2,1)S(1)}, bf16[560,128]{1,0:T(8,128)(2,1)S(1)}, u32[]{:S(2)}, u32[]{:S(2)}) collective-permute-start(bf16[560,128]{1,0:T(8,128)(2,1)S(1)} %add_convert_fusion.1), channel_id=1, source_target_pairs={{0,24},{1,25},{2,26},{3,27},{4,28},{5,29},{6,30},{7,31},{8,16},{9,... | collective-permute-start | bytes 430088 | tf_op jit(solution)/shard_map/ppermute | solution.py:40
  51.9 6.1 %collective-permute-start.11 = (bf16[560,128]{1,0:T(8,128)(2,1)S(1)}, bf16[560,128]{1,0:T(8,128)(2,1)S(1)}, u32[]{:S(2)}, u32[]{:S(2)}) collective-permute-start(bf16[560,128]{1,0:T(8,128)(2,1)S(1)} %add_convert_fusion), channel_id=1, source_target_pairs={{0,6},{1,7},{2,4},{3,5},{4,2},{5,3},{6,0},{7,1},{8,14},{9,15},{10,... | collective-permute-start | bytes 430088 | tf_op jit(solution)/shard_map/ppermute | solution.py:40
  54.4 5.1 %collective-permute-start.10 = (bf16[560,128]{1,0:T(8,128)(2,1)S(1)}, bf16[560,128]{1,0:T(8,128)(2,1)S(1)}, u32[]{:S(2)}, u32[]{:S(2)}) collective-permute-start(bf16[560,128]{1,0:T(8,128)(2,1)S(1)} %add_convert_fusion), channel_id=1, source_target_pairs={{0,2},{1,3},{2,0},{3,1},{4,6},{5,7},{6,4},{7,5},{8,10},{9,11},{10,... | collective-permute-start | bytes 430088 | tf_op jit(solution)/shard_map/ppermute | solution.py:40
  54.8 5.1 %collective-permute-start.9 = (bf16[560,128]{1,0:T(8,128)(2,1)S(1)}, bf16[560,128]{1,0:T(8,128)(2,1)S(1)}, u32[]{:S(2)}, u32[]{:S(2)}) collective-permute-start(bf16[560,128]{1,0:T(8,128)(2,1)S(1)} %add_convert_fusion), channel_id=1, source_target_pairs={{0,4},{1,5},{2,6},{3,7},{4,0},{5,1},{6,2},{7,3},{8,12},{9,13},{10,... | collective-permute-start | bytes 430088 | tf_op jit(solution)/shard_map/ppermute | solution.py:40
  60.0 2.6 %collective-permute-start.12 = (bf16[4,560,128]{2,1,0:T(8,128)(2,1)S(1)}, bf16[4,560,128]{2,1,0:T(8,128)(2,1)S(1)}, u32[]{:S(2)}, u32[]{:S(2)}) collective-permute-start(bf16[4,560,128]{2,1,0:T(8,128)(2,1)S(1)} %pad_maximum_fusion.table), channel_id=1, source_target_pairs={{0,1},{1,0},{2,3},{3,2},{4,5},{5,4},{6,7},{7,6},{8,9},{9,8},{10,11... | collective-permute-start | bytes 1720328 | tf_op jit(solution)/shard_map/ppermute | solution.py:40

commit v4 on v3

--- a/solution.py
+++ b/solution.py
@@ -108,53 +108,60 @@
     )(*map(in_vmem, (own_y, own_pair, vis_y, vis_pair, drift)))
 
 
-def place_kernel(where, table, *refs):
-    w_in, b_in, w_out, wide, sems = refs[-5:]
+def place_kernel(labels, *refs):
+    tables, (w_in, b_in, w_out, wide, sems) = refs[: len(labels)], refs[-5:]
     rows, depth = w_in.shape[0] // 2, w_out.shape[0] // 2
-    cols = table.shape[2]
+    cols = tables[0].shape[2]
+    own_side = lax.axis_index("blk") & 1
+    own_chip = lax.axis_index("rep") >> 1
+    own_core = lax.axis_index("rep") & 1
     copies = []
-    for index in range(table.shape[0]):
-        chip, half = divmod(index, 2)
-        wide[index] = table[index].astype(F32)
-        side = where[0] ^ half
-        column = pl.ds(pl.multiple_of((2 * (where[1] ^ chip) + where[2]) * cols, cols), cols)
-        sources = [wide.at[index, :rows], wide.at[index, rows : rows + depth]]
-        targets = [
-            w_in.at[pl.ds(pl.multiple_of(side * rows, rows), rows), column],
-            w_out.at[pl.ds(pl.multiple_of(side * depth, depth), depth), column],
-        ]
-        if half == 0:
-            sources.append(wide.at[index, rows + depth : rows + depth + 1])
-            targets.append(b_in.at[:, column])
-        for source, target in zip(sources, targets):
-            copy = pltpu.make_async_copy(source, target, sems.at[len(copies)])
-            copy.start()
-            copies.append(copy)
+    count = 0
+    for table, its_labels in zip(tables, labels):
+        for index, (half, chip, core) in enumerate(its_labels):
+            wide[count] = table[index].astype(F32)
+            side = own_side ^ half
+            column = 2 * (own_chip ^ chip) + (own_core ^ core)
+            column = pl.ds(pl.multiple_of(column * cols, cols), cols)
+            sources = [wide.at[count, :rows], wide.at[count, rows : rows + depth]]
+            targets = [
+                w_in.at[pl.ds(pl.multiple_of(side * rows, rows), rows), column],
+                w_out.at[pl.ds(pl.multiple_of(side * depth, depth), depth), column],
+            ]
+            if half == 0:
+                sources.append(wide.at[count, rows + depth : rows + depth + 1])
+                targets.append(b_in.at[:, column])
+            for source, target in zip(sources, targets):
+                copy = pltpu.make_async_copy(source, target, sems.at[len(copies)])
+                copy.start()
+                copies.append(copy)
+            count += 1
     for copy in copies:
         copy.wait()
 
 
-def place(table, where, din, feat, hid, earlier):
-    count, height, cols = table.shape
+def place(tables, labels, din, feat, hid, earlier):
+    height, cols = tables[0].shape[1:]
+    count = sum(len(its_labels) for its_labels in labels)
     shapes = (
         jax.ShapeDtypeStruct((din, hid), F32),
         jax.ShapeDtypeStruct((1, hid), F32),
         jax.ShapeDtypeStruct((feat, hid), F32),
     )
     return pl.pallas_call(
-        place_kernel,
+        lambda *refs: place_kernel(labels, *refs),
         out_shape=shapes,
-        in_specs=[pl.BlockSpec(memory_space=pltpu.SMEM), pl.BlockSpec(memory_space=pltpu.VMEM)]
+        in_specs=[pl.BlockSpec(memory_space=pltpu.VMEM) for _ in tables]
         + [pl.BlockSpec(memory_space=pl.ANY) for _ in earlier],
         out_specs=[pl.BlockSpec(memory_space=pl.ANY)] * 3,
         scratch_shapes=[
             pltpu.VMEM((count, height, cols), F32),
             pltpu.SemaphoreType.DMA((3 * count,)),
         ],
-        input_output_aliases={2 + i: i for i in range(len(earlier))},
+        input_output_aliases={len(tables) + i: i for i in range(len(earlier))},
         compiler_params=pltpu.CompilerParams(vmem_limit_bytes=16 << 20),
         name="place",
-    )(where, in_vmem(table), *earlier)
+    )(*map(in_vmem, tables), *earlier)
 
 
 def on_device(points, w_in, b_in, w_out, inv_scale, solves, probes):
@@ -178,11 +185,10 @@
     near, far = masks[0], masks[1:]
     pairs = [fetch(pair, far[0], blocks, reps)]
     pairs += [fetch(pair, mask, blocks, reps) for mask in far[1:]]
+    near_pair = fetch(pair, near, blocks, reps)
     scaleds = [fetch(scaled, far[0], blocks, reps)]
     scaleds += [fetch(scaled, mask, blocks, reps) for mask in far[1:]]
     near_scaled = fetch(scaled, near, blocks, reps)
-    near_pair, scaled = lax.optimization_barrier((pair, scaled))
-    near_pair = fetch(near_pair, near, blocks, reps)
     drift = jnp.zeros((feat, rows), F32)
     drift = couple(scaled, pair, near_scaled, near_pair, drift)
     for vis_y, vis_pair in zip(scaleds, pairs):
@@ -221,7 +227,6 @@
 
     same = (0, 0)
     side = blk_index & 1
-    core = rep_index & 1
     kept = lax.dynamic_index_in_dim(halves, side, 0, keepdims=False)
     sent = lax.dynamic_index_in_dim(halves, 1 - side, 0, keepdims=False)
     got = swap(sent, (1, 1), 0, blocks, reps)
@@ -232,14 +237,22 @@
         part = (part.astype(F32) + got.astype(F32)).astype(BF16)
 
     pieces = [part]
+    origins = [(0, 0)]
     for index in range(1, reps):
         chip, half = divmod(index, 2)
         pieces.append(swap(part, (half, half), chip << 1, blocks, reps))
-    near = jnp.stack(pieces)
-    other = swap(near, same, 1, blocks, reps)
-    chip = rep_index >> 1
-    outs = place(near, jnp.stack([side, chip, core]), din, feat, hid, ())
-    outs = place(other, jnp.stack([side, chip, 1 - core]), din, feat, hid, outs)
+        origins.append((half, chip))
+    early, late = jnp.stack(pieces[:2]), jnp.stack(pieces[2:])
+    early_labels, late_labels = (
+        [[(half, chip, core) for half, chip in group] for core in range(2)]
+        for group in (origins[:2], origins[2:])
+    )
+    sizes = (din, feat, hid)
+    early_other = swap(early, same, 1, blocks, reps)
+    outs = place([early, early_other], early_labels, *sizes, ())
+    late_other = swap(late, same, 1, blocks, reps)
+    outs = place([late], late_labels[:1], *sizes, outs)
+    outs = place([late_other], late_labels[1:], *sizes, outs)
     grad_w_in, grad_b_in, grad_w_out = outs
     grad_w_out = grad_w_out.T
     grad_b_in = grad_b_in.reshape(hid)

time: 64.5 us -> 62 us (0.961)
  waiting for transfers between devices: 31.4 us -> 28.8 us
  starting transfers between devices: 19.7 us -> 20.8 us
    ppermute x4, waiting for transfers between devices: 10.8 us -> 7.63 us  [fetch(): return lax.ppermute(array, AXES, route)]
    ppermute x9 -> x10, starting transfers between devices: 13.2 us -> 14.2 us  [swap(): return lax.ppermute(array, AXES, route)]
    ppermute x9 -> x10, waiting for transfers between devices: 20.6 us -> 21.2 us  [swap(): return lax.ppermute(array, AXES, route)]
    pallas_call x2 -> x3, Pallas kernels: 3.3 us -> 2.86 us  [place(): pl.pallas_call(lambda *refs: place_kernel(labels, *refs), out_shape=shape...]
  transfers between devices with their start and end apart: 13 -> 14, of which waited for: 9 -> 9; matrix products, arithmetic and copies ran while one was open for 1% -> 5% of each run, Pallas kernels for 5% -> 5%
where the time goes in v4:
time: 62 us; the launch traced here: 61.8 us
  waiting for transfers between devices  28.8 us (46%)
  starting transfers between devices  20.8 us (34%)
  Pallas kernels  6.55 us (11%)
  matrix products  3.44 us (6%)
  local copies, waits for them, and re-layouts  0.97 us (2%)
  between operations  0.87 us (1%)
    ppermute x10, waiting for transfers between devices, swap(): return lax.ppermute(array, AXES, route)  21.2 us
    ppermute x10, starting transfers between devices, swap(): return lax.ppermute(array, AXES, route)  14.2 us
    ppermute x4, waiting for transfers between devices, fetch(): return lax.ppermute(array, AXES, route)  7.63 us
    ppermute x4, starting transfers between devices, fetch(): return lax.ppermute(array, AXES, route)  6.62 us
    pallas_call x3, Pallas kernels, place(): pl.pallas_call(lambda *refs: place_kernel(labels, *refs), out_shape=shape...  2.86 us
    pallas_call x2, Pallas kernels, couple(): pl.pallas_call(lambda *refs: couple_kernel(chunk, *refs), out_shape=pltpu...  2.62 us
    dot_general x1, matrix products, on_device(): jnp.dot(points, w_in, preferred_element_type=F32) + b_in  2.21 us
  transfers between devices with their start and end apart: 14, of which 9 were waited for; matrix products, arithmetic and copies ran while one was open for 5% of the time, Pallas kernels for 5%

profile of v4, /device:TPU:0, one launch (start us, length us, event | category | flops | bytes accessed | tf_op | source)
XLA Modules:
  0.0 61.8 jit_solution(6356553664525081064)
XLA Ops:
  0.6 0.0 copy-start
  0.6 1.1 %join.1.refs_1_ = bf16[128,768]{1,0:T(8,128)(2,1)S(1)} custom-call(bf16[64,768]{1,0:T(8,128)(2,1)} %first.1, bf16[64,768]{1,0:T(8,128)(2,1)} %second.1), custom_call_target="tpu_custom_call" | custom-call | tf_op jit(solution)/shard_map/join/pallas_call | solution.py:57
  1.7 0.0 copy-start.1
  1.7 0.0 copy-start.2
  1.8 0.8 %collective-permute-start.3 = (bf16[128,768]{1,0:T(8,128)(2,1)S(1)}, bf16[128,768]{1,0:T(8,128)(2,1)S(1)}, u32[]{:S(2)}, u32[]{:S(2)}) collective-permute-start(bf16[128,768]{1,0:T(8,128)(2,1)S(1)} %join.1.refs_1_), channel_id=1, source_target_pairs={{0,0},{13,1},{6,2},{11,3},{4,4},{9,5},{2,6},{15,7},{8,8},{5,9},{14... | collective-permute-start | bytes 589832 | tf_op jit(solution)/shard_map/ppermute | solution.py:31
  2.6 5.1 %collective-permute-start.1 = (bf16[128,768]{1,0:T(8,128)(2,1)S(1)}, bf16[128,768]{1,0:T(8,128)(2,1)S(1)}, u32[]{:S(2)}, u32[]{:S(2)}) collective-permute-start(bf16[128,768]{1,0:T(8,128)(2,1)S(1)} %join.1.refs_1_), channel_id=1, source_target_pairs={{20,0},{25,1},{18,2},{31,3},{16,4},{29,5},{22,6},{27,7},{28,8},{17... | collective-permute-start | bytes 589832 | tf_op jit(solution)/shard_map/ppermute | solution.py:31
  7.6 0.0 copy-done
  7.6 2.2 %tanh_convert_fusion = bf16[768,512]{1,0:T(8,128)(2,1)S(1)} fusion(bf16[768,1024]{1,0:T(8,128)(2,1)S(1)} %copy-done, bf16[1024,512]{1,0:T(8,128)(2,1)} %param.8, f32[512]{0:T(512)} %param.9), kind=kOutput, calls=%fused_computation | convolution fusion | flops 806092800 | bytes 3409920 | tf_op jit(solution)/shard_map/dot_general | solution.py:180
  9.8 0.0 copy-done.1
  9.9 0.0 copy-done.2
  9.9 0.4 fusion.1.refs_0_
  10.2 0.7 %collective-permute-start.2 = (bf16[64,768]{1,0:T(8,128)(2,1)S(1)}, bf16[64,768]{1,0:T(8,128)(2,1)S(1)}, u32[]{:S(2)}, u32[]{:S(2)}) collective-permute-start(bf16[64,768]{1,0:T(8,128)(2,1)S(1)} %fusion.1.refs_0_), channel_id=1, source_target_pairs={{0,0},{13,1},{6,2},{11,3},{4,4},{9,5},{2,6},{15,7},{8,8},{5,9},{14... | collective-permute-start | bytes 294920 | tf_op jit(solution)/shard_map/ppermute | solution.py:31
  10.9 0.1 collective-permute-start
  11.0 0.0 collective-permute-done.2.refs_2_
  11.0 0.0 collective-permute-done.3.refs_3_
  11.0 1.3 %couple.2.refs_4_ = f32[64,768]{1,0:T(8,128)S(1)} custom-call(bf16[64,768]{1,0:T(8,128)(2,1)S(1)} %fusion.1.refs_0_, bf16[128,768]{1,0:T(8,128)(2,1)S(1)} %join.1.refs_1_, bf16[64,768]{1,0:T(8,128)(2,1)S(1)} %collective-permute-done.2.refs_2_, bf16[128,768]{1,0:T(8,128)(2,1)S(1)} %collective-permute-done.3.refs_3_, f32[64,768]{1,0:T(8,128)S(1)} %broadcast_in_dim.4.refs_4_), custom_call_target="tpu_custom_call" | custom-call | tf_op jit(solution)/shard_map/couple/pallas_call | solution.py:101
  12.3 7.6 %collective-permute-done.refs_2_ = bf16[64,768]{1,0:T(8,128)(2,1)S(1)} collective-permute-done((bf16[64,768]{1,0:T(8,128)(2,1)S(1)}, bf16[64,768]{1,0:T(8,128)(2,1)S(1)}, u32[]{:S(2)}, u32[]{:S(2)}) %collective-permute-start) | collective-permute-done | bytes 98336 | tf_op jit(solution)/shard_map/ppermute | solution.py:31
  20.0 0.0 collective-permute-done.1.refs_3_
  20.0 1.3 %couple.3 = f32[64,768]{1,0:T(8,128)S(1)} custom-call(bf16[64,768]{1,0:T(8,128)(2,1)S(1)} %fusion.1.refs_0_, bf16[128,768]{1,0:T(8,128)(2,1)S(1)} %join.1.refs_1_, bf16[64,768]{1,0:T(8,128)(2,1)S(1)} %collective-permute-done.refs_2_, bf16[128,768]{1,0:T(8,128)(2,1)S(1)} %collective-permute-done.1.refs_3_, f32[64,768]{1,0:T(8,128)S(1)} %couple.2.refs_4_), custom_call_target="tpu_custom_call" | custom-call | tf_op jit(solution)/shard_map/couple/pallas_call | solution.py:101
  21.3 0.5 collective-permute-start.4
  21.8 1.1 %collective-permute-done.4 = f32[64,768]{1,0:T(8,128)S(1)} collective-permute-done((f32[64,768]{1,0:T(8,128)S(1)}, f32[64,768]{1,0:T(8,128)S(1)}, u32[]{:S(2)}, u32[]{:S(2)}) %collective-permute-start.4) | collective-permute-done | bytes 196640 | tf_op jit(solution)/shard_map/ppermute | solution.py:40
  22.9 4.1 %collective-permute-start.5 = (bf16[64,768]{1,0:T(8,128)(2,1)S(1)}, bf16[64,768]{1,0:T(8,128)(2,1)S(1)}, u32[]{:S(2)}, u32[]{:S(2)}) collective-permute-start(bf16[64,768]{1,0:T(8,128)(2,1)S(1)} %add_convert_fusion.2), channel_id=1, source_target_pairs={{0,2},{1,3},{2,0},{3,1},{4,6},{5,7},{6,4},{7,5},{8,10},{9,11},{10,... | collective-permute-start | bytes 294920 | tf_op jit(solution)/shard_map/ppermute | solution.py:40
  27.0 3.1 %collective-permute-done.5 = bf16[64,768]{1,0:T(8,128)(2,1)S(1)} collective-permute-done((bf16[64,768]{1,0:T(8,128)(2,1)S(1)}, bf16[64,768]{1,0:T(8,128)(2,1)S(1)}, u32[]{:S(2)}, u32[]{:S(2)}) %collective-permute-start.5) | collective-permute-done | bytes 98336 | tf_op jit(solution)/shard_map/ppermute | solution.py:40
  30.1 0.1 add_multiply_fusion
  30.2 0.3 fusion.12
  30.5 0.2 fusion.5
  30.7 0.4 convolution_bitcast_fusion
  31.1 0.2 copy.17
  31.3 0.1 fusion.2
  31.4 1.5 %collective-permute-start.6 = (bf16[560,128]{1,0:T(8,128)(2,1)S(1)}, bf16[560,128]{1,0:T(8,128)(2,1)S(1)}, u32[]{:S(2)}, u32[]{:S(2)}) collective-permute-start(bf16[560,128]{1,0:T(8,128)(2,1)S(1)} %dynamic-slice_bitcast_fusion), channel_id=1, source_target_pairs={{0,4},{1,5},{2,6},{3,7},{4,0},{5,1},{6,2},{7,3},{8,12},{9,13},{10,... | collective-permute-start | bytes 430088 | tf_op jit(solution)/shard_map/ppermute | solution.py:40
  32.9 3.8 %collective-permute-done.6 = bf16[560,128]{1,0:T(8,128)(2,1)S(1)} collective-permute-done((bf16[560,128]{1,0:T(8,128)(2,1)S(1)}, bf16[560,128]{1,0:T(8,128)(2,1)S(1)}, u32[]{:S(2)}, u32[]{:S(2)}) %collective-permute-start.6) | collective-permute-done | bytes 143392 | tf_op jit(solution)/shard_map/ppermute | solution.py:40
  36.8 0.8 %collective-permute-start.7 = (bf16[560,128]{1,0:T(8,128)(2,1)S(1)}, bf16[560,128]{1,0:T(8,128)(2,1)S(1)}, u32[]{:S(2)}, u32[]{:S(2)}) collective-permute-start(bf16[560,128]{1,0:T(8,128)(2,1)S(1)} %fusion.3), channel_id=1, source_target_pairs={{0,8},{1,9},{2,10},{3,11},{4,12},{5,13},{6,14},{7,15},{8,0},{9,1},... | collective-permute-start | bytes 430088 | tf_op jit(solution)/shard_map/ppermute | solution.py:40
  37.5 4.4 %collective-permute-done.7 = bf16[560,128]{1,0:T(8,128)(2,1)S(1)} collective-permute-done((bf16[560,128]{1,0:T(8,128)(2,1)S(1)}, bf16[560,128]{1,0:T(8,128)(2,1)S(1)}, u32[]{:S(2)}, u32[]{:S(2)}) %collective-permute-start.7) | collective-permute-done | bytes 143392 | tf_op jit(solution)/shard_map/ppermute | solution.py:40
  42.0 3.6 %collective-permute-start.8 = (bf16[560,128]{1,0:T(8,128)(2,1)S(1)}, bf16[560,128]{1,0:T(8,128)(2,1)S(1)}, u32[]{:S(2)}, u32[]{:S(2)}) collective-permute-start(bf16[560,128]{1,0:T(8,128)(2,1)S(1)} %add_convert_fusion.1), channel_id=1, source_target_pairs={{0,24},{1,25},{2,26},{3,27},{4,28},{5,29},{6,30},{7,31},{8,16},{9,... | collective-permute-start | bytes 430088 | tf_op jit(solution)/shard_map/ppermute | solution.py:40
  45.6 3.4 %collective-permute-done.8 = bf16[560,128]{1,0:T(8,128)(2,1)S(1)} collective-permute-done((bf16[560,128]{1,0:T(8,128)(2,1)S(1)}, bf16[560,128]{1,0:T(8,128)(2,1)S(1)}, u32[]{:S(2)}, u32[]{:S(2)}) %collective-permute-start.8) | collective-permute-done | bytes 143392 | tf_op jit(solution)/shard_map/ppermute | solution.py:40
  49.0 1.5 %collective-permute-start.12 = (bf16[560,128]{1,0:T(8,128)(2,1)S(1)}, bf16[560,128]{1,0:T(8,128)(2,1)S(1)}, u32[]{:S(2)}, u32[]{:S(2)}) collective-permute-start(bf16[560,128]{1,0:T(8,128)(2,1)S(1)} %add_convert_fusion), channel_id=1, source_target_pairs={{0,4},{1,5},{2,6},{3,7},{4,0},{5,1},{6,2},{7,3},{8,12},{9,13},{10,... | collective-permute-start | bytes 430088 | tf_op jit(solution)/shard_map/ppermute | solution.py:40
  50.5 1.6 %collective-permute-start.9 = (bf16[560,128]{1,0:T(8,128)(2,1)S(1)}, bf16[560,128]{1,0:T(8,128)(2,1)S(1)}, u32[]{:S(2)}, u32[]{:S(2)}) collective-permute-start(bf16[560,128]{1,0:T(8,128)(2,1)S(1)} %add_convert_fusion), channel_id=1, source_target_pairs={{0,2},{1,3},{2,0},{3,1},{4,6},{5,7},{6,4},{7,5},{8,10},{9,11},{10,... | collective-permute-start | bytes 430088 | tf_op jit(solution)/shard_map/ppermute | solution.py:40
  52.1 0.4 collective-permute-start.10
  52.5 1.6 %collective-permute-done.12 = bf16[560,128]{1,0:T(8,128)(2,1)S(1)} collective-permute-done((bf16[560,128]{1,0:T(8,128)(2,1)S(1)}, bf16[560,128]{1,0:T(8,128)(2,1)S(1)}, u32[]{:S(2)}, u32[]{:S(2)}) %collective-permute-start.12) | collective-permute-done | bytes 143392 | tf_op jit(solution)/shard_map/ppermute | solution.py:40
  54.2 0.1 collective-permute-start.13
  54.3 1.3 %collective-permute-done.9 = bf16[560,128]{1,0:T(8,128)(2,1)S(1)} collective-permute-done((bf16[560,128]{1,0:T(8,128)(2,1)S(1)}, bf16[560,128]{1,0:T(8,128)(2,1)S(1)}, u32[]{:S(2)}, u32[]{:S(2)}) %collective-permute-start.9) | collective-permute-done | bytes 143392 | tf_op jit(solution)/shard_map/ppermute | solution.py:40
  55.6 2.5 %collective-permute-done.10 = bf16[560,128]{1,0:T(8,128)(2,1)S(1)} collective-permute-done((bf16[560,128]{1,0:T(8,128)(2,1)S(1)}, bf16[560,128]{1,0:T(8,128)(2,1)S(1)}, u32[]{:S(2)}, u32[]{:S(2)}) %collective-permute-start.10) | collective-permute-done | bytes 143392 | tf_op jit(solution)/shard_map/ppermute | solution.py:40
  58.1 0.1 collective-permute-start.11
  58.2 0.7 %constant_dynamic-slice_fusion = f32[64,192]{1,0:T(8,128)} fusion(f32[64,768]{1,0:T(8,128)S(1)} %add_multiply_fusion, s32[]{:T(128)S(6)} %select_n.14), kind=kLoop, calls=%fused_computation.25 | loop fusion | bytes 98308 | tf_op jit(solution)/shard_map/dynamic_slice | solution.py:203
  58.9 0.0 collective-permute-done.13.refs_1_
  59.0 1.1 %place.3 = (f32[1024,512]{1,0:T(8,128)}, f32[1,512]{1,0:T(1,128)}, f32[64,512]{1,0:T(8,128)}) custom-call(bf16[2,560,128]{2,1,0:T(8,128)(2,1)S(1)} %pad_maximum_fusion.1.refs_0_, bf16[2,560,128]{2,1,0:T(8,128)(2,1)S(1)} %collective-permute-done.13.refs_1_), custom_call_target="tpu_custom_call" | custom-call | tf_op jit(solution)/shard_map/place/pallas_call | solution.py:151
  60.1 0.9 %place.4 = (f32[1024,512]{1,0:T(8,128)}, f32[1,512]{1,0:T(1,128)}, f32[64,512]{1,0:T(8,128)}) custom-call(bf16[2,560,128]{2,1,0:T(8,128)(2,1)S(1)} %pad_maximum_fusion.refs_0_, f32[1024,512]{1,0:T(8,128)} %get-tuple-element.13.refs_1_, f32[1,512]{1,0:T(1,128)} %get-tuple-element.14.refs_2_, ...), custom_call_target="tpu_custom_call", output_to_operand_aliasing={{0}: (1, {}), {1}: (2, {}), {2}: (3, {})} | custom-call | tf_op jit(solution)/shard_map/place/pallas_call | solution.py:151
  61.0 0.0 collective-permute-done.11.refs_0_
  61.0 0.9 %place.5 = (f32[1024,512]{1,0:T(8,128)}, f32[1,512]{1,0:T(1,128)}, f32[64,512]{1,0:T(8,128)}) custom-call(bf16[2,560,128]{2,1,0:T(8,128)(2,1)S(1)} %collective-permute-done.11.refs_0_, f32[1024,512]{1,0:T(8,128)} %get-tuple-element.16.refs_1_, f32[1,512]{1,0:T(1,128)} %get-tuple-element.17.refs_2_, ...), custom_call_target="tpu_custom_call", output_to_operand_aliasing={{0}: (1, {}), {1}: (2, {}), {2}: (3, {})} | custom-call | tf_op jit(solution)/shard_map/place/pallas_call | solution.py:151
  (9 shorter events, 0.2 us)
Async XLA Ops:
  0.6 7.0 %copy-start = (bf16[768,1024]{1,0:T(8,128)(2,1)S(1)}, bf16[768,1024]{1,0:T(8,128)(2,1)}, u32[]{:S(2)}) copy-start(bf16[768,1024]{1,0:T(8,128)(2,1)} %param.7) | copy-start | bytes 4718596
  1.7 8.1 %copy-start.1 = (bf16[512,64]{0,1:T(8,128)(2,1)S(1)}, bf16[512,64]{0,1:T(8,128)(2,1)}, u32[]{:S(2)}) copy-start(bf16[512,64]{0,1:T(8,128)(2,1)} %param.10) | copy-start | bytes 196612
  1.7 8.1 %copy-start.2 = (f32[64]{0:T(128)S(1)}, f32[64]{0:T(128)}, u32[]{:S(2)}) copy-start(f32[64]{0:T(128)} %param.11) | copy-start | bytes 772
  1.8 9.2 %collective-permute-start.3 = (bf16[128,768]{1,0:T(8,128)(2,1)S(1)}, bf16[128,768]{1,0:T(8,128)(2,1)S(1)}, u32[]{:S(2)}, u32[]{:S(2)}) collective-permute-start(bf16[128,768]{1,0:T(8,128)(2,1)S(1)} %join.1.refs_1_), channel_id=1, source_target_pairs={{0,0},{13,1},{6,2},{11,3},{4,4},{9,5},{2,6},{15,7},{8,8},{5,9},{14... | collective-permute-start | bytes 589832 | tf_op jit(solution)/shard_map/ppermute | solution.py:31
  2.6 17.4 %collective-permute-start.1 = (bf16[128,768]{1,0:T(8,128)(2,1)S(1)}, bf16[128,768]{1,0:T(8,128)(2,1)S(1)}, u32[]{:S(2)}, u32[]{:S(2)}) collective-permute-start(bf16[128,768]{1,0:T(8,128)(2,1)S(1)} %join.1.refs_1_), channel_id=1, source_target_pairs={{20,0},{25,1},{18,2},{31,3},{16,4},{29,5},{22,6},{27,7},{28,8},{17... | collective-permute-start | bytes 589832 | tf_op jit(solution)/shard_map/ppermute | solution.py:31
  10.2 0.8 %collective-permute-start.2 = (bf16[64,768]{1,0:T(8,128)(2,1)S(1)}, bf16[64,768]{1,0:T(8,128)(2,1)S(1)}, u32[]{:S(2)}, u32[]{:S(2)}) collective-permute-start(bf16[64,768]{1,0:T(8,128)(2,1)S(1)} %fusion.1.refs_0_), channel_id=1, source_target_pairs={{0,0},{13,1},{6,2},{11,3},{4,4},{9,5},{2,6},{15,7},{8,8},{5,9},{14... | collective-permute-start | bytes 294920 | tf_op jit(solution)/shard_map/ppermute | solution.py:31
  10.9 9.1 %collective-permute-start = (bf16[64,768]{1,0:T(8,128)(2,1)S(1)}, bf16[64,768]{1,0:T(8,128)(2,1)S(1)}, u32[]{:S(2)}, u32[]{:S(2)}) collective-permute-start(bf16[64,768]{1,0:T(8,128)(2,1)S(1)} %fusion.1.refs_0_), channel_id=1, source_target_pairs={{20,0},{25,1},{18,2},{31,3},{16,4},{29,5},{22,6},{27,7},{28,8},{17... | collective-permute-start | bytes 294920 | tf_op jit(solution)/shard_map/ppermute | solution.py:31
  21.3 1.6 %collective-permute-start.4 = (f32[64,768]{1,0:T(8,128)S(1)}, f32[64,768]{1,0:T(8,128)S(1)}, u32[]{:S(2)}, u32[]{:S(2)}) collective-permute-start(f32[64,768]{1,0:T(8,128)S(1)} %couple.3), channel_id=1, source_target_pairs={{0,1},{1,0},{2,3},{3,2},{4,5},{5,4},{6,7},{7,6},{8,9},{9,8},{10,11... | collective-permute-start | bytes 589832 | tf_op jit(solution)/shard_map/ppermute | solution.py:40
  22.9 7.2 %collective-permute-start.5 = (bf16[64,768]{1,0:T(8,128)(2,1)S(1)}, bf16[64,768]{1,0:T(8,128)(2,1)S(1)}, u32[]{:S(2)}, u32[]{:S(2)}) collective-permute-start(bf16[64,768]{1,0:T(8,128)(2,1)S(1)} %add_convert_fusion.2), channel_id=1, source_target_pairs={{0,2},{1,3},{2,0},{3,1},{4,6},{5,7},{6,4},{7,5},{8,10},{9,11},{10,... | collective-permute-start | bytes 294920 | tf_op jit(solution)/shard_map/ppermute | solution.py:40
  31.4 5.3 %collective-permute-start.6 = (bf16[560,128]{1,0:T(8,128)(2,1)S(1)}, bf16[560,128]{1,0:T(8,128)(2,1)S(1)}, u32[]{:S(2)}, u32[]{:S(2)}) collective-permute-start(bf16[560,128]{1,0:T(8,128)(2,1)S(1)} %dynamic-slice_bitcast_fusion), channel_id=1, source_target_pairs={{0,4},{1,5},{2,6},{3,7},{4,0},{5,1},{6,2},{7,3},{8,12},{9,13},{10,... | collective-permute-start | bytes 430088 | tf_op jit(solution)/shard_map/ppermute | solution.py:40
  36.8 5.2 %collective-permute-start.7 = (bf16[560,128]{1,0:T(8,128)(2,1)S(1)}, bf16[560,128]{1,0:T(8,128)(2,1)S(1)}, u32[]{:S(2)}, u32[]{:S(2)}) collective-permute-start(bf16[560,128]{1,0:T(8,128)(2,1)S(1)} %fusion.3), channel_id=1, source_target_pairs={{0,8},{1,9},{2,10},{3,11},{4,12},{5,13},{6,14},{7,15},{8,0},{9,1},... | collective-permute-start | bytes 430088 | tf_op jit(solution)/shard_map/ppermute | solution.py:40
  42.0 7.0 %collective-permute-start.8 = (bf16[560,128]{1,0:T(8,128)(2,1)S(1)}, bf16[560,128]{1,0:T(8,128)(2,1)S(1)}, u32[]{:S(2)}, u32[]{:S(2)}) collective-permute-start(bf16[560,128]{1,0:T(8,128)(2,1)S(1)} %add_convert_fusion.1), channel_id=1, source_target_pairs={{0,24},{1,25},{2,26},{3,27},{4,28},{5,29},{6,30},{7,31},{8,16},{9,... | collective-permute-start | bytes 430088 | tf_op jit(solution)/shard_map/ppermute | solution.py:40
  49.0 5.2 %collective-permute-start.12 = (bf16[560,128]{1,0:T(8,128)(2,1)S(1)}, bf16[560,128]{1,0:T(8,128)(2,1)S(1)}, u32[]{:S(2)}, u32[]{:S(2)}) collective-permute-start(bf16[560,128]{1,0:T(8,128)(2,1)S(1)} %add_convert_fusion), channel_id=1, source_target_pairs={{0,4},{1,5},{2,6},{3,7},{4,0},{5,1},{6,2},{7,3},{8,12},{9,13},{10,... | collective-permute-start | bytes 430088 | tf_op jit(solution)/shard_map/ppermute | solution.py:40
  50.5 5.1 %collective-permute-start.9 = (bf16[560,128]{1,0:T(8,128)(2,1)S(1)}, bf16[560,128]{1,0:T(8,128)(2,1)S(1)}, u32[]{:S(2)}, u32[]{:S(2)}) collective-permute-start(bf16[560,128]{1,0:T(8,128)(2,1)S(1)} %add_convert_fusion), channel_id=1, source_target_pairs={{0,2},{1,3},{2,0},{3,1},{4,6},{5,7},{6,4},{7,5},{8,10},{9,11},{10,... | collective-permute-start | bytes 430088 | tf_op jit(solution)/shard_map/ppermute | solution.py:40
  52.1 6.0 %collective-permute-start.10 = (bf16[560,128]{1,0:T(8,128)(2,1)S(1)}, bf16[560,128]{1,0:T(8,128)(2,1)S(1)}, u32[]{:S(2)}, u32[]{:S(2)}) collective-permute-start(bf16[560,128]{1,0:T(8,128)(2,1)S(1)} %add_convert_fusion), channel_id=1, source_target_pairs={{0,6},{1,7},{2,4},{3,5},{4,2},{5,3},{6,0},{7,1},{8,14},{9,15},{10,... | collective-permute-start | bytes 430088 | tf_op jit(solution)/shard_map/ppermute | solution.py:40
  54.2 4.8 %collective-permute-start.13 = (bf16[2,560,128]{2,1,0:T(8,128)(2,1)S(1)}, bf16[2,560,128]{2,1,0:T(8,128)(2,1)S(1)}, u32[]{:S(2)}, u32[]{:S(2)}) collective-permute-start(bf16[2,560,128]{2,1,0:T(8,128)(2,1)S(1)} %pad_maximum_fusion.1.refs_0_), channel_id=1, source_target_pairs={{0,1},{1,0},{2,3},{3,2},{4,5},{5,4},{6,7},{7,6},{8,9},{9,8},{10,11... | collective-permute-start | bytes 860168 | tf_op jit(solution)/shard_map/ppermute | solution.py:40
  58.1 2.8 %collective-permute-start.11 = (bf16[2,560,128]{2,1,0:T(8,128)(2,1)S(1)}, bf16[2,560,128]{2,1,0:T(8,128)(2,1)S(1)}, u32[]{:S(2)}, u32[]{:S(2)}) collective-permute-start(bf16[2,560,128]{2,1,0:T(8,128)(2,1)S(1)} %pad_maximum_fusion.refs_0_), channel_id=1, source_target_pairs={{0,1},{1,0},{2,3},{3,2},{4,5},{5,4},{6,7},{7,6},{8,9},{9,8},{10,11... | collective-permute-start | bytes 860168 | tf_op jit(solution)/shard_map/ppermute | solution.py:40

commit v5 on v4

--- a/solution.py
+++ b/solution.py
@@ -64,31 +64,42 @@
     )(first, second)
 
 
+def exponent_rows(vectors, first):
+    wide = vectors.astype(F32)
+    left = -0.5 * jnp.sum(wide * wide, axis=0, keepdims=True)
+    parts = []
+    for _ in range(3):
+        part = left.astype(BF16).astype(F32)
+        parts.append(part)
+        left = left - part
+    ones = [jnp.ones_like(left)] * 3
+    rows = parts + ones if first else ones + parts
+    rows.append(jnp.zeros((10, vectors.shape[1]), F32))
+    return jnp.concatenate([vectors, jnp.concatenate(rows, axis=0).astype(BF16)], axis=0)
+
+
 def couple_kernel(chunk, own_y, own_pair, vis_y, vis_pair, before, after):
     feat, rows = own_y.shape
     count = own_pair.shape[0] // 2
     crossed = jnp.concatenate([own_pair[count:], own_pair[:count]], axis=0)
     own = own_y[...]
-    own32 = own.astype(F32)
-    own_half = 0.5 * jnp.sum(own32 * own32, axis=0, keepdims=True)
+    own_rows = exponent_rows(own, True)
     ones = jnp.ones((16, chunk), BF16)
     pulled = jnp.zeros((feat + 16, rows), F32)
+    over_rows = (((0,), (0,)), ((), ()))
     for start in range(0, rows, chunk):
         part_y = vis_y[:, start : start + chunk]
-        turned = part_y.astype(F32).T
-        vis_half = 0.5 * jnp.sum(turned * turned, axis=1, keepdims=True)
-        cross = jnp.dot(turned.astype(BF16), own, preferred_element_type=F32)
         coupling = lax.dot_general(
-            vis_pair[:, start : start + chunk],
-            crossed,
-            (((0,), (0,)), ((), ())),
-            preferred_element_type=F32,
+            vis_pair[:, start : start + chunk], crossed, over_rows, preferred_element_type=F32
         )
-        weight = (coupling * jnp.exp(cross - (own_half + vis_half))).astype(BF16)
+        exponent = lax.dot_general(
+            exponent_rows(part_y, False), own_rows, over_rows, preferred_element_type=F32
+        )
+        weight = (coupling * jnp.exp(exponent)).astype(BF16)
         pulled += jnp.dot(
             jnp.concatenate([part_y, ones], axis=0), weight, preferred_element_type=F32
         )
-    after[...] = before[...] + (pulled[:feat] - own32 * pulled[feat : feat + 1])
+    after[...] = before[...] + (pulled[:feat] - own.astype(F32) * pulled[feat : feat + 1])
 
 
 def in_vmem(array):
@@ -97,13 +108,13 @@
 
 def couple(own_y, own_pair, vis_y, vis_pair, drift):
     rows = own_y.shape[1]
-    chunk = 256 if rows % 256 == 0 else rows
+    chunk = 256 if rows > 1024 and rows % 256 == 0 else rows
     return pl.pallas_call(
         lambda *refs: couple_kernel(chunk, *refs),
         out_shape=pltpu.VMEM(drift.shape, F32),
         in_specs=[pl.BlockSpec(memory_space=pltpu.VMEM)] * 5,
         out_specs=pl.BlockSpec(memory_space=pltpu.VMEM),
-        compiler_params=pltpu.CompilerParams(vmem_limit_bytes=16 << 20),
+        compiler_params=pltpu.CompilerParams(vmem_limit_bytes=24 << 20),
         name="couple",
     )(*map(in_vmem, (own_y, own_pair, vis_y, vis_pair, drift)))
 

time: 62 us -> 61.8 us (level)
  no operation moved by 1% of the time
where the time goes in v5:
time: 61.8 us; the launch traced here: 61.6 us
  waiting for transfers between devices  29.3 us (47%)
  starting transfers between devices  20.6 us (33%)
  Pallas kernels  6 us (10%)
  matrix products  3.43 us (6%)
  local copies, waits for them, and re-layouts  0.97 us (2%)
  between operations  0.87 us (1%)
    ppermute x10, waiting for transfers between devices, swap(): return lax.ppermute(array, AXES, route)  21.4 us
    ppermute x10, starting transfers between devices, swap(): return lax.ppermute(array, AXES, route)  14 us
    ppermute x4, waiting for transfers between devices, fetch(): return lax.ppermute(array, AXES, route)  7.91 us
    ppermute x4, starting transfers between devices, fetch(): return lax.ppermute(array, AXES, route)  6.62 us
    pallas_call x3, Pallas kernels, place(): pl.pallas_call(lambda *refs: place_kernel(labels, *refs), out_shape=shape...  2.86 us
    dot_general x1, matrix products, on_device(): jnp.dot(points, w_in, preferred_element_type=F32) + b_in  2.21 us
    pallas_call x2, Pallas kernels, couple(): pl.pallas_call(lambda *refs: couple_kernel(chunk, *refs), out_shape=pltpu...  2.06 us
  transfers between devices with their start and end apart: 14, of which 9 were waited for; matrix products, arithmetic and copies ran while one was open for 5% of the time, Pallas kernels for 5%

profile of v5, /device:TPU:0, one launch (start us, length us, event | category | flops | bytes accessed | tf_op | source)
XLA Modules:
  0.0 61.6 jit_solution(3179610904234430840)
XLA Ops:
  0.6 0.0 copy-start
  0.6 1.1 %join.1.refs_1_ = bf16[128,768]{1,0:T(8,128)(2,1)S(1)} custom-call(bf16[64,768]{1,0:T(8,128)(2,1)} %first.1, bf16[64,768]{1,0:T(8,128)(2,1)} %second.1), custom_call_target="tpu_custom_call" | custom-call | tf_op jit(solution)/shard_map/join/pallas_call | solution.py:57
  1.7 0.0 copy-start.1
  1.7 0.0 copy-start.2
  1.8 0.8 %collective-permute-start.3 = (bf16[128,768]{1,0:T(8,128)(2,1)S(1)}, bf16[128,768]{1,0:T(8,128)(2,1)S(1)}, u32[]{:S(2)}, u32[]{:S(2)}) collective-permute-start(bf16[128,768]{1,0:T(8,128)(2,1)S(1)} %join.1.refs_1_), channel_id=1, source_target_pairs={{0,0},{13,1},{6,2},{11,3},{4,4},{9,5},{2,6},{15,7},{8,8},{5,9},{14... | collective-permute-start | bytes 589832 | tf_op jit(solution)/shard_map/ppermute | solution.py:31
  2.6 5.1 %collective-permute-start.1 = (bf16[128,768]{1,0:T(8,128)(2,1)S(1)}, bf16[128,768]{1,0:T(8,128)(2,1)S(1)}, u32[]{:S(2)}, u32[]{:S(2)}) collective-permute-start(bf16[128,768]{1,0:T(8,128)(2,1)S(1)} %join.1.refs_1_), channel_id=1, source_target_pairs={{20,0},{25,1},{18,2},{31,3},{16,4},{29,5},{22,6},{27,7},{28,8},{17... | collective-permute-start | bytes 589832 | tf_op jit(solution)/shard_map/ppermute | solution.py:31
  7.6 0.0 copy-done
  7.6 2.2 %tanh_convert_fusion = bf16[768,512]{1,0:T(8,128)(2,1)S(1)} fusion(bf16[768,1024]{1,0:T(8,128)(2,1)S(1)} %copy-done, bf16[1024,512]{1,0:T(8,128)(2,1)} %param.8, f32[512]{0:T(512)} %param.9), kind=kOutput, calls=%fused_computation | convolution fusion | flops 806092800 | bytes 3409920 | tf_op jit(solution)/shard_map/dot_general | solution.py:191
  9.8 0.0 copy-done.1
  9.9 0.0 copy-done.2
  9.9 0.4 fusion.1.refs_0_
  10.2 0.7 %collective-permute-start.2 = (bf16[64,768]{1,0:T(8,128)(2,1)S(1)}, bf16[64,768]{1,0:T(8,128)(2,1)S(1)}, u32[]{:S(2)}, u32[]{:S(2)}) collective-permute-start(bf16[64,768]{1,0:T(8,128)(2,1)S(1)} %fusion.1.refs_0_), channel_id=1, source_target_pairs={{0,0},{13,1},{6,2},{11,3},{4,4},{9,5},{2,6},{15,7},{8,8},{5,9},{14... | collective-permute-start | bytes 294920 | tf_op jit(solution)/shard_map/ppermute | solution.py:31
  10.9 0.1 collective-permute-start
  11.0 0.0 collective-permute-done.2.refs_2_
  11.0 0.0 collective-permute-done.3.refs_3_
  11.0 1.0 %couple.2.refs_4_ = f32[64,768]{1,0:T(8,128)S(1)} custom-call(bf16[64,768]{1,0:T(8,128)(2,1)S(1)} %fusion.1.refs_0_, bf16[128,768]{1,0:T(8,128)(2,1)S(1)} %join.1.refs_1_, bf16[64,768]{1,0:T(8,128)(2,1)S(1)} %collective-permute-done.2.refs_2_, bf16[128,768]{1,0:T(8,128)(2,1)S(1)} %collective-permute-done.3.refs_3_, f32[64,768]{1,0:T(8,128)S(1)} %broadcast_in_dim.4.refs_4_), custom_call_target="tpu_custom_call" | custom-call | tf_op jit(solution)/shard_map/couple/pallas_call | solution.py:112
  12.1 7.9 %collective-permute-done.refs_2_ = bf16[64,768]{1,0:T(8,128)(2,1)S(1)} collective-permute-done((bf16[64,768]{1,0:T(8,128)(2,1)S(1)}, bf16[64,768]{1,0:T(8,128)(2,1)S(1)}, u32[]{:S(2)}, u32[]{:S(2)}) %collective-permute-start) | collective-permute-done | bytes 98336 | tf_op jit(solution)/shard_map/ppermute | solution.py:31
  20.0 0.0 collective-permute-done.1.refs_3_
  20.0 1.0 %couple.3 = f32[64,768]{1,0:T(8,128)S(1)} custom-call(bf16[64,768]{1,0:T(8,128)(2,1)S(1)} %fusion.1.refs_0_, bf16[128,768]{1,0:T(8,128)(2,1)S(1)} %join.1.refs_1_, bf16[64,768]{1,0:T(8,128)(2,1)S(1)} %collective-permute-done.refs_2_, bf16[128,768]{1,0:T(8,128)(2,1)S(1)} %collective-permute-done.1.refs_3_, f32[64,768]{1,0:T(8,128)S(1)} %couple.2.refs_4_), custom_call_target="tpu_custom_call" | custom-call | tf_op jit(solution)/shard_map/couple/pallas_call | solution.py:112
  21.0 0.3 collective-permute-start.4
  21.3 1.3 %collective-permute-done.4 = f32[64,768]{1,0:T(8,128)S(1)} collective-permute-done((f32[64,768]{1,0:T(8,128)S(1)}, f32[64,768]{1,0:T(8,128)S(1)}, u32[]{:S(2)}, u32[]{:S(2)}) %collective-permute-start.4) | collective-permute-done | bytes 196640 | tf_op jit(solution)/shard_map/ppermute | solution.py:40
  22.5 4.2 %collective-permute-start.5 = (bf16[64,768]{1,0:T(8,128)(2,1)S(1)}, bf16[64,768]{1,0:T(8,128)(2,1)S(1)}, u32[]{:S(2)}, u32[]{:S(2)}) collective-permute-start(bf16[64,768]{1,0:T(8,128)(2,1)S(1)} %add_convert_fusion.2), channel_id=1, source_target_pairs={{0,2},{1,3},{2,0},{3,1},{4,6},{5,7},{6,4},{7,5},{8,10},{9,11},{10,... | collective-permute-start | bytes 294920 | tf_op jit(solution)/shard_map/ppermute | solution.py:40
  26.8 3.1 %collective-permute-done.5 = bf16[64,768]{1,0:T(8,128)(2,1)S(1)} collective-permute-done((bf16[64,768]{1,0:T(8,128)(2,1)S(1)}, bf16[64,768]{1,0:T(8,128)(2,1)S(1)}, u32[]{:S(2)}, u32[]{:S(2)}) %collective-permute-start.5) | collective-permute-done | bytes 98336 | tf_op jit(solution)/shard_map/ppermute | solution.py:40
  29.9 0.1 add_multiply_fusion
  29.9 0.3 fusion.12
  30.3 0.2 fusion.5
  30.4 0.4 convolution_bitcast_fusion
  30.8 0.2 copy.17
  31.0 0.1 fusion.2
  31.1 1.5 %collective-permute-start.6 = (bf16[560,128]{1,0:T(8,128)(2,1)S(1)}, bf16[560,128]{1,0:T(8,128)(2,1)S(1)}, u32[]{:S(2)}, u32[]{:S(2)}) collective-permute-start(bf16[560,128]{1,0:T(8,128)(2,1)S(1)} %dynamic-slice_bitcast_fusion), channel_id=1, source_target_pairs={{0,4},{1,5},{2,6},{3,7},{4,0},{5,1},{6,2},{7,3},{8,12},{9,13},{10,... | collective-permute-start | bytes 430088 | tf_op jit(solution)/shard_map/ppermute | solution.py:40
  32.7 3.8 %collective-permute-done.6 = bf16[560,128]{1,0:T(8,128)(2,1)S(1)} collective-permute-done((bf16[560,128]{1,0:T(8,128)(2,1)S(1)}, bf16[560,128]{1,0:T(8,128)(2,1)S(1)}, u32[]{:S(2)}, u32[]{:S(2)}) %collective-permute-start.6) | collective-permute-done | bytes 143392 | tf_op jit(solution)/shard_map/ppermute | solution.py:40
  36.5 0.8 %collective-permute-start.7 = (bf16[560,128]{1,0:T(8,128)(2,1)S(1)}, bf16[560,128]{1,0:T(8,128)(2,1)S(1)}, u32[]{:S(2)}, u32[]{:S(2)}) collective-permute-start(bf16[560,128]{1,0:T(8,128)(2,1)S(1)} %fusion.3), channel_id=1, source_target_pairs={{0,8},{1,9},{2,10},{3,11},{4,12},{5,13},{6,14},{7,15},{8,0},{9,1},... | collective-permute-start | bytes 430088 | tf_op jit(solution)/shard_map/ppermute | solution.py:40
  37.3 4.4 %collective-permute-done.7 = bf16[560,128]{1,0:T(8,128)(2,1)S(1)} collective-permute-done((bf16[560,128]{1,0:T(8,128)(2,1)S(1)}, bf16[560,128]{1,0:T(8,128)(2,1)S(1)}, u32[]{:S(2)}, u32[]{:S(2)}) %collective-permute-start.7) | collective-permute-done | bytes 143392 | tf_op jit(solution)/shard_map/ppermute | solution.py:40
  41.7 3.6 %collective-permute-start.8 = (bf16[560,128]{1,0:T(8,128)(2,1)S(1)}, bf16[560,128]{1,0:T(8,128)(2,1)S(1)}, u32[]{:S(2)}, u32[]{:S(2)}) collective-permute-start(bf16[560,128]{1,0:T(8,128)(2,1)S(1)} %add_convert_fusion.1), channel_id=1, source_target_pairs={{0,24},{1,25},{2,26},{3,27},{4,28},{5,29},{6,30},{7,31},{8,16},{9,... | collective-permute-start | bytes 430088 | tf_op jit(solution)/shard_map/ppermute | solution.py:40
  45.3 3.4 %collective-permute-done.8 = bf16[560,128]{1,0:T(8,128)(2,1)S(1)} collective-permute-done((bf16[560,128]{1,0:T(8,128)(2,1)S(1)}, bf16[560,128]{1,0:T(8,128)(2,1)S(1)}, u32[]{:S(2)}, u32[]{:S(2)}) %collective-permute-start.8) | collective-permute-done | bytes 143392 | tf_op jit(solution)/shard_map/ppermute | solution.py:40
  48.7 1.5 %collective-permute-start.12 = (bf16[560,128]{1,0:T(8,128)(2,1)S(1)}, bf16[560,128]{1,0:T(8,128)(2,1)S(1)}, u32[]{:S(2)}, u32[]{:S(2)}) collective-permute-start(bf16[560,128]{1,0:T(8,128)(2,1)S(1)} %add_convert_fusion), channel_id=1, source_target_pairs={{0,4},{1,5},{2,6},{3,7},{4,0},{5,1},{6,2},{7,3},{8,12},{9,13},{10,... | collective-permute-start | bytes 430088 | tf_op jit(solution)/shard_map/ppermute | solution.py:40
  50.2 1.6 %collective-permute-start.9 = (bf16[560,128]{1,0:T(8,128)(2,1)S(1)}, bf16[560,128]{1,0:T(8,128)(2,1)S(1)}, u32[]{:S(2)}, u32[]{:S(2)}) collective-permute-start(bf16[560,128]{1,0:T(8,128)(2,1)S(1)} %add_convert_fusion), channel_id=1, source_target_pairs={{0,2},{1,3},{2,0},{3,1},{4,6},{5,7},{6,4},{7,5},{8,10},{9,11},{10,... | collective-permute-start | bytes 430088 | tf_op jit(solution)/shard_map/ppermute | solution.py:40
  51.8 0.4 collective-permute-start.10
  52.3 1.6 %collective-permute-done.12 = bf16[560,128]{1,0:T(8,128)(2,1)S(1)} collective-permute-done((bf16[560,128]{1,0:T(8,128)(2,1)S(1)}, bf16[560,128]{1,0:T(8,128)(2,1)S(1)}, u32[]{:S(2)}, u32[]{:S(2)}) %collective-permute-start.12) | collective-permute-done | bytes 143392 | tf_op jit(solution)/shard_map/ppermute | solution.py:40
  53.9 0.1 collective-permute-start.13
  54.0 1.3 %collective-permute-done.9 = bf16[560,128]{1,0:T(8,128)(2,1)S(1)} collective-permute-done((bf16[560,128]{1,0:T(8,128)(2,1)S(1)}, bf16[560,128]{1,0:T(8,128)(2,1)S(1)}, u32[]{:S(2)}, u32[]{:S(2)}) %collective-permute-start.9) | collective-permute-done | bytes 143392 | tf_op jit(solution)/shard_map/ppermute | solution.py:40
  55.3 2.5 %collective-permute-done.10 = bf16[560,128]{1,0:T(8,128)(2,1)S(1)} collective-permute-done((bf16[560,128]{1,0:T(8,128)(2,1)S(1)}, bf16[560,128]{1,0:T(8,128)(2,1)S(1)}, u32[]{:S(2)}, u32[]{:S(2)}) %collective-permute-start.10) | collective-permute-done | bytes 143392 | tf_op jit(solution)/shard_map/ppermute | solution.py:40
  57.9 0.1 collective-permute-start.11
  57.9 0.7 %constant_dynamic-slice_fusion = f32[64,192]{1,0:T(8,128)} fusion(f32[64,768]{1,0:T(8,128)S(1)} %add_multiply_fusion, s32[]{:T(128)S(6)} %select_n.14), kind=kLoop, calls=%fused_computation.25 | loop fusion | bytes 98308 | tf_op jit(solution)/shard_map/dynamic_slice | solution.py:214
  58.7 0.0 collective-permute-done.13.refs_1_
  58.7 1.1 %place.3 = (f32[1024,512]{1,0:T(8,128)}, f32[1,512]{1,0:T(1,128)}, f32[64,512]{1,0:T(8,128)}) custom-call(bf16[2,560,128]{2,1,0:T(8,128)(2,1)S(1)} %pad_maximum_fusion.1.refs_0_, bf16[2,560,128]{2,1,0:T(8,128)(2,1)S(1)} %collective-permute-done.13.refs_1_), custom_call_target="tpu_custom_call" | custom-call | tf_op jit(solution)/shard_map/place/pallas_call | solution.py:162
  59.8 0.9 %place.4 = (f32[1024,512]{1,0:T(8,128)}, f32[1,512]{1,0:T(1,128)}, f32[64,512]{1,0:T(8,128)}) custom-call(bf16[2,560,128]{2,1,0:T(8,128)(2,1)S(1)} %pad_maximum_fusion.refs_0_, f32[1024,512]{1,0:T(8,128)} %get-tuple-element.13.refs_1_, f32[1,512]{1,0:T(1,128)} %get-tuple-element.14.refs_2_, ...), custom_call_target="tpu_custom_call", output_to_operand_aliasing={{0}: (1, {}), {1}: (2, {}), {2}: (3, {})} | custom-call | tf_op jit(solution)/shard_map/place/pallas_call | solution.py:162
  60.7 0.0 collective-permute-done.11.refs_0_
  60.7 0.9 %place.5 = (f32[1024,512]{1,0:T(8,128)}, f32[1,512]{1,0:T(1,128)}, f32[64,512]{1,0:T(8,128)}) custom-call(bf16[2,560,128]{2,1,0:T(8,128)(2,1)S(1)} %collective-permute-done.11.refs_0_, f32[1024,512]{1,0:T(8,128)} %get-tuple-element.16.refs_1_, f32[1,512]{1,0:T(1,128)} %get-tuple-element.17.refs_2_, ...), custom_call_target="tpu_custom_call", output_to_operand_aliasing={{0}: (1, {}), {1}: (2, {}), {2}: (3, {})} | custom-call | tf_op jit(solution)/shard_map/place/pallas_call | solution.py:162
  (9 shorter events, 0.2 us)
Async XLA Ops:
  0.6 7.0 %copy-start = (bf16[768,1024]{1,0:T(8,128)(2,1)S(1)}, bf16[768,1024]{1,0:T(8,128)(2,1)}, u32[]{:S(2)}) copy-start(bf16[768,1024]{1,0:T(8,128)(2,1)} %param.7) | copy-start | bytes 4718596
  1.7 8.1 %copy-start.1 = (bf16[512,64]{0,1:T(8,128)(2,1)S(1)}, bf16[512,64]{0,1:T(8,128)(2,1)}, u32[]{:S(2)}) copy-start(bf16[512,64]{0,1:T(8,128)(2,1)} %param.10) | copy-start | bytes 196612
  1.7 8.1 %copy-start.2 = (f32[64]{0:T(128)S(1)}, f32[64]{0:T(128)}, u32[]{:S(2)}) copy-start(f32[64]{0:T(128)} %param.11) | copy-start | bytes 772
  1.8 9.2 %collective-permute-start.3 = (bf16[128,768]{1,0:T(8,128)(2,1)S(1)}, bf16[128,768]{1,0:T(8,128)(2,1)S(1)}, u32[]{:S(2)}, u32[]{:S(2)}) collective-permute-start(bf16[128,768]{1,0:T(8,128)(2,1)S(1)} %join.1.refs_1_), channel_id=1, source_target_pairs={{0,0},{13,1},{6,2},{11,3},{4,4},{9,5},{2,6},{15,7},{8,8},{5,9},{14... | collective-permute-start | bytes 589832 | tf_op jit(solution)/shard_map/ppermute | solution.py:31
  2.6 17.4 %collective-permute-start.1 = (bf16[128,768]{1,0:T(8,128)(2,1)S(1)}, bf16[128,768]{1,0:T(8,128)(2,1)S(1)}, u32[]{:S(2)}, u32[]{:S(2)}) collective-permute-start(bf16[128,768]{1,0:T(8,128)(2,1)S(1)} %join.1.refs_1_), channel_id=1, source_target_pairs={{20,0},{25,1},{18,2},{31,3},{16,4},{29,5},{22,6},{27,7},{28,8},{17... | collective-permute-start | bytes 589832 | tf_op jit(solution)/shard_map/ppermute | solution.py:31
  10.2 0.8 %collective-permute-start.2 = (bf16[64,768]{1,0:T(8,128)(2,1)S(1)}, bf16[64,768]{1,0:T(8,128)(2,1)S(1)}, u32[]{:S(2)}, u32[]{:S(2)}) collective-permute-start(bf16[64,768]{1,0:T(8,128)(2,1)S(1)} %fusion.1.refs_0_), channel_id=1, source_target_pairs={{0,0},{13,1},{6,2},{11,3},{4,4},{9,5},{2,6},{15,7},{8,8},{5,9},{14... | collective-permute-start | bytes 294920 | tf_op jit(solution)/shard_map/ppermute | solution.py:31
  10.9 9.1 %collective-permute-start = (bf16[64,768]{1,0:T(8,128)(2,1)S(1)}, bf16[64,768]{1,0:T(8,128)(2,1)S(1)}, u32[]{:S(2)}, u32[]{:S(2)}) collective-permute-start(bf16[64,768]{1,0:T(8,128)(2,1)S(1)} %fusion.1.refs_0_), channel_id=1, source_target_pairs={{20,0},{25,1},{18,2},{31,3},{16,4},{29,5},{22,6},{27,7},{28,8},{17... | collective-permute-start | bytes 294920 | tf_op jit(solution)/shard_map/ppermute | solution.py:31
  21.0 1.5 %collective-permute-start.4 = (f32[64,768]{1,0:T(8,128)S(1)}, f32[64,768]{1,0:T(8,128)S(1)}, u32[]{:S(2)}, u32[]{:S(2)}) collective-permute-start(f32[64,768]{1,0:T(8,128)S(1)} %couple.3), channel_id=1, source_target_pairs={{0,1},{1,0},{2,3},{3,2},{4,5},{5,4},{6,7},{7,6},{8,9},{9,8},{10,11... | collective-permute-start | bytes 589832 | tf_op jit(solution)/shard_map/ppermute | solution.py:40
  22.5 7.3 %collective-permute-start.5 = (bf16[64,768]{1,0:T(8,128)(2,1)S(1)}, bf16[64,768]{1,0:T(8,128)(2,1)S(1)}, u32[]{:S(2)}, u32[]{:S(2)}) collective-permute-start(bf16[64,768]{1,0:T(8,128)(2,1)S(1)} %add_convert_fusion.2), channel_id=1, source_target_pairs={{0,2},{1,3},{2,0},{3,1},{4,6},{5,7},{6,4},{7,5},{8,10},{9,11},{10,... | collective-permute-start | bytes 294920 | tf_op jit(solution)/shard_map/ppermute | solution.py:40
  31.1 5.3 %collective-permute-start.6 = (bf16[560,128]{1,0:T(8,128)(2,1)S(1)}, bf16[560,128]{1,0:T(8,128)(2,1)S(1)}, u32[]{:S(2)}, u32[]{:S(2)}) collective-permute-start(bf16[560,128]{1,0:T(8,128)(2,1)S(1)} %dynamic-slice_bitcast_fusion), channel_id=1, source_target_pairs={{0,4},{1,5},{2,6},{3,7},{4,0},{5,1},{6,2},{7,3},{8,12},{9,13},{10,... | collective-permute-start | bytes 430088 | tf_op jit(solution)/shard_map/ppermute | solution.py:40
  36.5 5.2 %collective-permute-start.7 = (bf16[560,128]{1,0:T(8,128)(2,1)S(1)}, bf16[560,128]{1,0:T(8,128)(2,1)S(1)}, u32[]{:S(2)}, u32[]{:S(2)}) collective-permute-start(bf16[560,128]{1,0:T(8,128)(2,1)S(1)} %fusion.3), channel_id=1, source_target_pairs={{0,8},{1,9},{2,10},{3,11},{4,12},{5,13},{6,14},{7,15},{8,0},{9,1},... | collective-permute-start | bytes 430088 | tf_op jit(solution)/shard_map/ppermute | solution.py:40
  41.7 7.0 %collective-permute-start.8 = (bf16[560,128]{1,0:T(8,128)(2,1)S(1)}, bf16[560,128]{1,0:T(8,128)(2,1)S(1)}, u32[]{:S(2)}, u32[]{:S(2)}) collective-permute-start(bf16[560,128]{1,0:T(8,128)(2,1)S(1)} %add_convert_fusion.1), channel_id=1, source_target_pairs={{0,24},{1,25},{2,26},{3,27},{4,28},{5,29},{6,30},{7,31},{8,16},{9,... | collective-permute-start | bytes 430088 | tf_op jit(solution)/shard_map/ppermute | solution.py:40
  48.7 5.2 %collective-permute-start.12 = (bf16[560,128]{1,0:T(8,128)(2,1)S(1)}, bf16[560,128]{1,0:T(8,128)(2,1)S(1)}, u32[]{:S(2)}, u32[]{:S(2)}) collective-permute-start(bf16[560,128]{1,0:T(8,128)(2,1)S(1)} %add_convert_fusion), channel_id=1, source_target_pairs={{0,4},{1,5},{2,6},{3,7},{4,0},{5,1},{6,2},{7,3},{8,12},{9,13},{10,... | collective-permute-start | bytes 430088 | tf_op jit(solution)/shard_map/ppermute | solution.py:40
  50.2 5.1 %collective-permute-start.9 = (bf16[560,128]{1,0:T(8,128)(2,1)S(1)}, bf16[560,128]{1,0:T(8,128)(2,1)S(1)}, u32[]{:S(2)}, u32[]{:S(2)}) collective-permute-start(bf16[560,128]{1,0:T(8,128)(2,1)S(1)} %add_convert_fusion), channel_id=1, source_target_pairs={{0,2},{1,3},{2,0},{3,1},{4,6},{5,7},{6,4},{7,5},{8,10},{9,11},{10,... | collective-permute-start | bytes 430088 | tf_op jit(solution)/shard_map/ppermute | solution.py:40
  51.8 6.0 %collective-permute-start.10 = (bf16[560,128]{1,0:T(8,128)(2,1)S(1)}, bf16[560,128]{1,0:T(8,128)(2,1)S(1)}, u32[]{:S(2)}, u32[]{:S(2)}) collective-permute-start(bf16[560,128]{1,0:T(8,128)(2,1)S(1)} %add_convert_fusion), channel_id=1, source_target_pairs={{0,6},{1,7},{2,4},{3,5},{4,2},{5,3},{6,0},{7,1},{8,14},{9,15},{10,... | collective-permute-start | bytes 430088 | tf_op jit(solution)/shard_map/ppermute | solution.py:40
  53.9 4.8 %collective-permute-start.13 = (bf16[2,560,128]{2,1,0:T(8,128)(2,1)S(1)}, bf16[2,560,128]{2,1,0:T(8,128)(2,1)S(1)}, u32[]{:S(2)}, u32[]{:S(2)}) collective-permute-start(bf16[2,560,128]{2,1,0:T(8,128)(2,1)S(1)} %pad_maximum_fusion.1.refs_0_), channel_id=1, source_target_pairs={{0,1},{1,0},{2,3},{3,2},{4,5},{5,4},{6,7},{7,6},{8,9},{9,8},{10,11... | collective-permute-start | bytes 860168 | tf_op jit(solution)/shard_map/ppermute | solution.py:40
  57.9 2.8 %collective-permute-start.11 = (bf16[2,560,128]{2,1,0:T(8,128)(2,1)S(1)}, bf16[2,560,128]{2,1,0:T(8,128)(2,1)S(1)}, u32[]{:S(2)}, u32[]{:S(2)}) collective-permute-start(bf16[2,560,128]{2,1,0:T(8,128)(2,1)S(1)} %pad_maximum_fusion.refs_0_), channel_id=1, source_target_pairs={{0,1},{1,0},{2,3},{3,2},{4,5},{5,4},{6,7},{7,6},{8,9},{9,8},{10,11... | collective-permute-start | bytes 860168 | tf_op jit(solution)/shard_map/ppermute | solution.py:40

commit v6 on v5

--- a/solution.py
+++ b/solution.py
@@ -253,17 +253,21 @@
         chip, half = divmod(index, 2)
         pieces.append(swap(part, (half, half), chip << 1, blocks, reps))
         origins.append((half, chip))
-    early, late = jnp.stack(pieces[:2]), jnp.stack(pieces[2:])
-    early_labels, late_labels = (
+    sizes = (din, feat, hid)
+    groups = (pieces[:1], pieces[1:-1], pieces[-1:])
+    labels = [
         [[(half, chip, core) for half, chip in group] for core in range(2)]
-        for group in (origins[:2], origins[2:])
-    )
-    sizes = (din, feat, hid)
-    early_other = swap(early, same, 1, blocks, reps)
-    outs = place([early, early_other], early_labels, *sizes, ())
-    late_other = swap(late, same, 1, blocks, reps)
-    outs = place([late], late_labels[:1], *sizes, outs)
-    outs = place([late_other], late_labels[1:], *sizes, outs)
+        for group in (origins[:1], origins[1:-1], origins[-1:])
+    ]
+    tables = [jnp.stack(group) for group in groups]
+    others = []
+    for table in tables:
+        others.append(swap(table, same, 1, blocks, reps))
+    outs = place([tables[0], others[0]], labels[0], *sizes, ())
+    outs = place(
+        [tables[1], others[1], tables[2]], [*labels[1], labels[2][0]], *sizes, outs
+    )
+    outs = place([others[2]], labels[2][1:], *sizes, outs)
     grad_w_in, grad_b_in, grad_w_out = outs
     grad_w_out = grad_w_out.T
     grad_b_in = grad_b_in.reshape(hid)

time: 61.8 us -> 66.3 us (1.073)
  waiting for transfers between devices: 29.3 us -> 32.5 us
  starting transfers between devices: 20.6 us -> 22 us
    ppermute x10 -> x11, waiting for transfers between devices: 21.4 us -> 24.6 us  [swap(): return lax.ppermute(array, AXES, route)]
    ppermute x10 -> x11, starting transfers between devices: 14 us -> 15.4 us  [swap(): return lax.ppermute(array, AXES, route)]
  transfers between devices with their start and end apart: 14 -> 15, of which waited for: 9 -> 9; matrix products, arithmetic and copies ran while one was open for 5% -> 5% of each run, Pallas kernels for 5% -> 5%
where the time goes in v6:
time: 66.3 us; the launch traced here: 66.1 us
  waiting for transfers between devices  32.5 us (49%)
  starting transfers between devices  22 us (33%)
  Pallas kernels  6 us (9%)
  matrix products  3.43 us (5%)
  local copies, waits for them, and re-layouts  0.97 us (1%)
  between operations  0.86 us (1%)
    ppermute x11, waiting for transfers between devices, swap(): return lax.ppermute(array, AXES, route)  24.6 us
    ppermute x11, starting transfers between devices, swap(): return lax.ppermute(array, AXES, route)  15.4 us
    ppermute x4, waiting for transfers between devices, fetch(): return lax.ppermute(array, AXES, route)  7.91 us
    ppermute x4, starting transfers between devices, fetch(): return lax.ppermute(array, AXES, route)  6.62 us
    pallas_call x3, Pallas kernels, place(): pl.pallas_call(lambda *refs: place_kernel(labels, *refs), out_shape=shape...  2.86 us
    dot_general x1, matrix products, on_device(): jnp.dot(points, w_in, preferred_element_type=F32) + b_in  2.21 us
    pallas_call x2, Pallas kernels, couple(): pl.pallas_call(lambda *refs: couple_kernel(chunk, *refs), out_shape=pltpu...  2.06 us
  transfers between devices with their start and end apart: 15, of which 9 were waited for; matrix products, arithmetic and copies ran while one was open for 5% of the time, Pallas kernels for 5%

profile of v6, /device:TPU:0, one launch (start us, length us, event | category | flops | bytes accessed | tf_op | source)
XLA Modules:
  0.0 66.1 jit_solution(9092374193522487545)
XLA Ops:
  0.6 0.0 copy-start
  0.6 1.1 %join.1.refs_1_ = bf16[128,768]{1,0:T(8,128)(2,1)S(1)} custom-call(bf16[64,768]{1,0:T(8,128)(2,1)} %first.1, bf16[64,768]{1,0:T(8,128)(2,1)} %second.1), custom_call_target="tpu_custom_call" | custom-call | tf_op jit(solution)/shard_map/join/pallas_call | solution.py:57
  1.7 0.0 copy-start.1
  1.7 0.0 copy-start.2
  1.8 0.8 %collective-permute-start.3 = (bf16[128,768]{1,0:T(8,128)(2,1)S(1)}, bf16[128,768]{1,0:T(8,128)(2,1)S(1)}, u32[]{:S(2)}, u32[]{:S(2)}) collective-permute-start(bf16[128,768]{1,0:T(8,128)(2,1)S(1)} %join.1.refs_1_), channel_id=1, source_target_pairs={{0,0},{13,1},{6,2},{11,3},{4,4},{9,5},{2,6},{15,7},{8,8},{5,9},{14... | collective-permute-start | bytes 589832 | tf_op jit(solution)/shard_map/ppermute | solution.py:31
  2.6 5.1 %collective-permute-start.1 = (bf16[128,768]{1,0:T(8,128)(2,1)S(1)}, bf16[128,768]{1,0:T(8,128)(2,1)S(1)}, u32[]{:S(2)}, u32[]{:S(2)}) collective-permute-start(bf16[128,768]{1,0:T(8,128)(2,1)S(1)} %join.1.refs_1_), channel_id=1, source_target_pairs={{20,0},{25,1},{18,2},{31,3},{16,4},{29,5},{22,6},{27,7},{28,8},{17... | collective-permute-start | bytes 589832 | tf_op jit(solution)/shard_map/ppermute | solution.py:31
  7.6 0.0 copy-done
  7.6 2.2 %tanh_convert_fusion = bf16[768,512]{1,0:T(8,128)(2,1)S(1)} fusion(bf16[768,1024]{1,0:T(8,128)(2,1)S(1)} %copy-done, bf16[1024,512]{1,0:T(8,128)(2,1)} %param.8, f32[512]{0:T(512)} %param.9), kind=kOutput, calls=%fused_computation | convolution fusion | flops 806092800 | bytes 3409920 | tf_op jit(solution)/shard_map/dot_general | solution.py:191
  9.8 0.0 copy-done.1
  9.9 0.0 copy-done.2
  9.9 0.4 fusion.1.refs_0_
  10.2 0.7 %collective-permute-start.2 = (bf16[64,768]{1,0:T(8,128)(2,1)S(1)}, bf16[64,768]{1,0:T(8,128)(2,1)S(1)}, u32[]{:S(2)}, u32[]{:S(2)}) collective-permute-start(bf16[64,768]{1,0:T(8,128)(2,1)S(1)} %fusion.1.refs_0_), channel_id=1, source_target_pairs={{0,0},{13,1},{6,2},{11,3},{4,4},{9,5},{2,6},{15,7},{8,8},{5,9},{14... | collective-permute-start | bytes 294920 | tf_op jit(solution)/shard_map/ppermute | solution.py:31
  10.9 0.1 collective-permute-start
  11.0 0.0 collective-permute-done.2.refs_2_
  11.0 0.0 collective-permute-done.3.refs_3_
  11.0 1.0 %couple.2.refs_4_ = f32[64,768]{1,0:T(8,128)S(1)} custom-call(bf16[64,768]{1,0:T(8,128)(2,1)S(1)} %fusion.1.refs_0_, bf16[128,768]{1,0:T(8,128)(2,1)S(1)} %join.1.refs_1_, bf16[64,768]{1,0:T(8,128)(2,1)S(1)} %collective-permute-done.2.refs_2_, bf16[128,768]{1,0:T(8,128)(2,1)S(1)} %collective-permute-done.3.refs_3_, f32[64,768]{1,0:T(8,128)S(1)} %broadcast_in_dim.4.refs_4_), custom_call_target="tpu_custom_call" | custom-call | tf_op jit(solution)/shard_map/couple/pallas_call | solution.py:112
  12.1 7.9 %collective-permute-done.refs_2_ = bf16[64,768]{1,0:T(8,128)(2,1)S(1)} collective-permute-done((bf16[64,768]{1,0:T(8,128)(2,1)S(1)}, bf16[64,768]{1,0:T(8,128)(2,1)S(1)}, u32[]{:S(2)}, u32[]{:S(2)}) %collective-permute-start) | collective-permute-done | bytes 98336 | tf_op jit(solution)/shard_map/ppermute | solution.py:31
  20.0 0.0 collective-permute-done.1.refs_3_
  20.0 1.0 %couple.3 = f32[64,768]{1,0:T(8,128)S(1)} custom-call(bf16[64,768]{1,0:T(8,128)(2,1)S(1)} %fusion.1.refs_0_, bf16[128,768]{1,0:T(8,128)(2,1)S(1)} %join.1.refs_1_, bf16[64,768]{1,0:T(8,128)(2,1)S(1)} %collective-permute-done.refs_2_, bf16[128,768]{1,0:T(8,128)(2,1)S(1)} %collective-permute-done.1.refs_3_, f32[64,768]{1,0:T(8,128)S(1)} %couple.2.refs_4_), custom_call_target="tpu_custom_call" | custom-call | tf_op jit(solution)/shard_map/couple/pallas_call | solution.py:112
  21.0 0.3 collective-permute-start.4
  21.3 1.3 %collective-permute-done.4 = f32[64,768]{1,0:T(8,128)S(1)} collective-permute-done((f32[64,768]{1,0:T(8,128)S(1)}, f32[64,768]{1,0:T(8,128)S(1)}, u32[]{:S(2)}, u32[]{:S(2)}) %collective-permute-start.4) | collective-permute-done | bytes 196640 | tf_op jit(solution)/shard_map/ppermute | solution.py:40
  22.5 4.2 %collective-permute-start.5 = (bf16[64,768]{1,0:T(8,128)(2,1)S(1)}, bf16[64,768]{1,0:T(8,128)(2,1)S(1)}, u32[]{:S(2)}, u32[]{:S(2)}) collective-permute-start(bf16[64,768]{1,0:T(8,128)(2,1)S(1)} %add_convert_fusion.2), channel_id=1, source_target_pairs={{0,2},{1,3},{2,0},{3,1},{4,6},{5,7},{6,4},{7,5},{8,10},{9,11},{10,... | collective-permute-start | bytes 294920 | tf_op jit(solution)/shard_map/ppermute | solution.py:40
  26.8 3.1 %collective-permute-done.5 = bf16[64,768]{1,0:T(8,128)(2,1)S(1)} collective-permute-done((bf16[64,768]{1,0:T(8,128)(2,1)S(1)}, bf16[64,768]{1,0:T(8,128)(2,1)S(1)}, u32[]{:S(2)}, u32[]{:S(2)}) %collective-permute-start.5) | collective-permute-done | bytes 98336 | tf_op jit(solution)/shard_map/ppermute | solution.py:40
  29.9 0.1 add_multiply_fusion
  29.9 0.3 fusion.12
  30.3 0.2 fusion.5
  30.4 0.4 convolution_bitcast_fusion
  30.8 0.2 copy.17
  31.0 0.1 fusion.2
  31.1 1.5 %collective-permute-start.6 = (bf16[560,128]{1,0:T(8,128)(2,1)S(1)}, bf16[560,128]{1,0:T(8,128)(2,1)S(1)}, u32[]{:S(2)}, u32[]{:S(2)}) collective-permute-start(bf16[560,128]{1,0:T(8,128)(2,1)S(1)} %dynamic-slice_bitcast_fusion), channel_id=1, source_target_pairs={{0,4},{1,5},{2,6},{3,7},{4,0},{5,1},{6,2},{7,3},{8,12},{9,13},{10,... | collective-permute-start | bytes 430088 | tf_op jit(solution)/shard_map/ppermute | solution.py:40
  32.7 3.8 %collective-permute-done.6 = bf16[560,128]{1,0:T(8,128)(2,1)S(1)} collective-permute-done((bf16[560,128]{1,0:T(8,128)(2,1)S(1)}, bf16[560,128]{1,0:T(8,128)(2,1)S(1)}, u32[]{:S(2)}, u32[]{:S(2)}) %collective-permute-start.6) | collective-permute-done | bytes 143392 | tf_op jit(solution)/shard_map/ppermute | solution.py:40
  36.5 0.8 %collective-permute-start.7 = (bf16[560,128]{1,0:T(8,128)(2,1)S(1)}, bf16[560,128]{1,0:T(8,128)(2,1)S(1)}, u32[]{:S(2)}, u32[]{:S(2)}) collective-permute-start(bf16[560,128]{1,0:T(8,128)(2,1)S(1)} %fusion.3), channel_id=1, source_target_pairs={{0,8},{1,9},{2,10},{3,11},{4,12},{5,13},{6,14},{7,15},{8,0},{9,1},... | collective-permute-start | bytes 430088 | tf_op jit(solution)/shard_map/ppermute | solution.py:40
  37.3 4.4 %collective-permute-done.7 = bf16[560,128]{1,0:T(8,128)(2,1)S(1)} collective-permute-done((bf16[560,128]{1,0:T(8,128)(2,1)S(1)}, bf16[560,128]{1,0:T(8,128)(2,1)S(1)}, u32[]{:S(2)}, u32[]{:S(2)}) %collective-permute-start.7) | collective-permute-done | bytes 143392 | tf_op jit(solution)/shard_map/ppermute | solution.py:40
  41.7 3.6 %collective-permute-start.8 = (bf16[560,128]{1,0:T(8,128)(2,1)S(1)}, bf16[560,128]{1,0:T(8,128)(2,1)S(1)}, u32[]{:S(2)}, u32[]{:S(2)}) collective-permute-start(bf16[560,128]{1,0:T(8,128)(2,1)S(1)} %add_convert_fusion.1), channel_id=1, source_target_pairs={{0,24},{1,25},{2,26},{3,27},{4,28},{5,29},{6,30},{7,31},{8,16},{9,... | collective-permute-start | bytes 430088 | tf_op jit(solution)/shard_map/ppermute | solution.py:40
  45.3 3.4 %collective-permute-done.8 = bf16[560,128]{1,0:T(8,128)(2,1)S(1)} collective-permute-done((bf16[560,128]{1,0:T(8,128)(2,1)S(1)}, bf16[560,128]{1,0:T(8,128)(2,1)S(1)}, u32[]{:S(2)}, u32[]{:S(2)}) %collective-permute-start.8) | collective-permute-done | bytes 143392 | tf_op jit(solution)/shard_map/ppermute | solution.py:40
  48.7 1.5 %collective-permute-start.11 = (bf16[560,128]{1,0:T(8,128)(2,1)S(1)}, bf16[560,128]{1,0:T(8,128)(2,1)S(1)}, u32[]{:S(2)}, u32[]{:S(2)}) collective-permute-start(bf16[560,128]{1,0:T(8,128)(2,1)S(1)} %add_convert_fusion), channel_id=1, source_target_pairs={{0,4},{1,5},{2,6},{3,7},{4,0},{5,1},{6,2},{7,3},{8,12},{9,13},{10,... | collective-permute-start | bytes 430088 | tf_op jit(solution)/shard_map/ppermute | solution.py:40
  50.2 1.6 %collective-permute-start.12 = (bf16[560,128]{1,0:T(8,128)(2,1)S(1)}, bf16[560,128]{1,0:T(8,128)(2,1)S(1)}, u32[]{:S(2)}, u32[]{:S(2)}) collective-permute-start(bf16[560,128]{1,0:T(8,128)(2,1)S(1)} %add_convert_fusion), channel_id=1, source_target_pairs={{0,2},{1,3},{2,0},{3,1},{4,6},{5,7},{6,4},{7,5},{8,10},{9,11},{10,... | collective-permute-start | bytes 430088 | tf_op jit(solution)/shard_map/ppermute | solution.py:40
  51.8 2.0 %collective-permute-done.11 = bf16[560,128]{1,0:T(8,128)(2,1)S(1)} collective-permute-done((bf16[560,128]{1,0:T(8,128)(2,1)S(1)}, bf16[560,128]{1,0:T(8,128)(2,1)S(1)}, u32[]{:S(2)}, u32[]{:S(2)}) %collective-permute-start.11) | collective-permute-done | bytes 143392 | tf_op jit(solution)/shard_map/ppermute | solution.py:40
  53.9 1.4 %collective-permute-done.12 = bf16[560,128]{1,0:T(8,128)(2,1)S(1)} collective-permute-done((bf16[560,128]{1,0:T(8,128)(2,1)S(1)}, bf16[560,128]{1,0:T(8,128)(2,1)S(1)}, u32[]{:S(2)}, u32[]{:S(2)}) %collective-permute-start.12) | collective-permute-done | bytes 143392 | tf_op jit(solution)/shard_map/ppermute | solution.py:40
  55.3 0.1 collective-permute-start.13
  55.4 1.7 %collective-permute-start.9 = (bf16[560,128]{1,0:T(8,128)(2,1)S(1)}, bf16[560,128]{1,0:T(8,128)(2,1)S(1)}, u32[]{:S(2)}, u32[]{:S(2)}) collective-permute-start(bf16[560,128]{1,0:T(8,128)(2,1)S(1)} %add_convert_fusion), channel_id=1, source_target_pairs={{0,6},{1,7},{2,4},{3,5},{4,2},{5,3},{6,0},{7,1},{8,14},{9,15},{10,... | collective-permute-start | bytes 430088 | tf_op jit(solution)/shard_map/ppermute | solution.py:40
  57.1 0.2 collective-permute-start.14
  57.3 5.2 %collective-permute-done.9 = bf16[560,128]{1,0:T(8,128)(2,1)S(1)} collective-permute-done((bf16[560,128]{1,0:T(8,128)(2,1)S(1)}, bf16[560,128]{1,0:T(8,128)(2,1)S(1)}, u32[]{:S(2)}, u32[]{:S(2)}) %collective-permute-start.9) | collective-permute-done | bytes 143392 | tf_op jit(solution)/shard_map/ppermute | solution.py:40
  62.5 0.0 collective-permute-start.10
  62.5 0.7 %constant_dynamic-slice_fusion = f32[64,192]{1,0:T(8,128)} fusion(f32[64,768]{1,0:T(8,128)S(1)} %add_multiply_fusion, s32[]{:T(128)S(6)} %select_n.14), kind=kLoop, calls=%fused_computation.24 | loop fusion | bytes 98308 | tf_op jit(solution)/shard_map/dynamic_slice | solution.py:214
  63.2 0.0 collective-permute-done.14.refs_1_
  63.2 0.9 %place.3 = (f32[1024,512]{1,0:T(8,128)}, f32[1,512]{1,0:T(1,128)}, f32[64,512]{1,0:T(8,128)}) custom-call(bf16[1,560,128]{2,1,0:T(8,128)(2,1)S(1)} %bitcast.24, bf16[1,560,128]{2,1,0:T(8,128)(2,1)S(1)} %collective-permute-done.14.refs_1_), custom_call_target="tpu_custom_call" | custom-call | tf_op jit(solution)/shard_map/place/pallas_call | solution.py:162
  64.1 0.0 collective-permute-done.13.refs_1_
  64.1 1.2 %place.4 = (f32[1024,512]{1,0:T(8,128)}, f32[1,512]{1,0:T(1,128)}, f32[64,512]{1,0:T(8,128)}) custom-call(bf16[2,560,128]{2,1,0:T(8,128)(2,1)S(1)} %pad_maximum_fusion.refs_0_, bf16[2,560,128]{2,1,0:T(8,128)(2,1)S(1)} %collective-permute-done.13.refs_1_, ...), custom_call_target="tpu_custom_call", output_to_operand_aliasing={{0}: (3, {}), {1}: (4, {}), {2}: (5, {})} | custom-call | tf_op jit(solution)/shard_map/place/pallas_call | solution.py:162
  65.3 0.0 collective-permute-done.10.refs_0_
  65.4 0.8 %place.5 = (f32[1024,512]{1,0:T(8,128)}, f32[1,512]{1,0:T(1,128)}, f32[64,512]{1,0:T(8,128)}) custom-call(bf16[1,560,128]{2,1,0:T(8,128)(2,1)S(1)} %collective-permute-done.10.refs_0_, f32[1024,512]{1,0:T(8,128)} %get-tuple-element.16.refs_1_, f32[1,512]{1,0:T(1,128)} %get-tuple-element.17.refs_2_, ...), custom_call_target="tpu_custom_call", output_to_operand_aliasing={{0}: (1, {}), {1}: (2, {}), {2}: (3, {})} | custom-call | tf_op jit(solution)/shard_map/place/pallas_call | solution.py:162
  (8 shorter events, 0.2 us)
Async XLA Ops:
  0.6 7.0 %copy-start = (bf16[768,1024]{1,0:T(8,128)(2,1)S(1)}, bf16[768,1024]{1,0:T(8,128)(2,1)}, u32[]{:S(2)}) copy-start(bf16[768,1024]{1,0:T(8,128)(2,1)} %param.7) | copy-start | bytes 4718596
  1.7 8.1 %copy-start.1 = (bf16[512,64]{0,1:T(8,128)(2,1)S(1)}, bf16[512,64]{0,1:T(8,128)(2,1)}, u32[]{:S(2)}) copy-start(bf16[512,64]{0,1:T(8,128)(2,1)} %param.10) | copy-start | bytes 196612
  1.7 8.1 %copy-start.2 = (f32[64]{0:T(128)S(1)}, f32[64]{0:T(128)}, u32[]{:S(2)}) copy-start(f32[64]{0:T(128)} %param.11) | copy-start | bytes 772
  1.8 9.2 %collective-permute-start.3 = (bf16[128,768]{1,0:T(8,128)(2,1)S(1)}, bf16[128,768]{1,0:T(8,128)(2,1)S(1)}, u32[]{:S(2)}, u32[]{:S(2)}) collective-permute-start(bf16[128,768]{1,0:T(8,128)(2,1)S(1)} %join.1.refs_1_), channel_id=1, source_target_pairs={{0,0},{13,1},{6,2},{11,3},{4,4},{9,5},{2,6},{15,7},{8,8},{5,9},{14... | collective-permute-start | bytes 589832 | tf_op jit(solution)/shard_map/ppermute | solution.py:31
  2.6 17.4 %collective-permute-start.1 = (bf16[128,768]{1,0:T(8,128)(2,1)S(1)}, bf16[128,768]{1,0:T(8,128)(2,1)S(1)}, u32[]{:S(2)}, u32[]{:S(2)}) collective-permute-start(bf16[128,768]{1,0:T(8,128)(2,1)S(1)} %join.1.refs_1_), channel_id=1, source_target_pairs={{20,0},{25,1},{18,2},{31,3},{16,4},{29,5},{22,6},{27,7},{28,8},{17... | collective-permute-start | bytes 589832 | tf_op jit(solution)/shard_map/ppermute | solution.py:31
  10.2 0.8 %collective-permute-start.2 = (bf16[64,768]{1,0:T(8,128)(2,1)S(1)}, bf16[64,768]{1,0:T(8,128)(2,1)S(1)}, u32[]{:S(2)}, u32[]{:S(2)}) collective-permute-start(bf16[64,768]{1,0:T(8,128)(2,1)S(1)} %fusion.1.refs_0_), channel_id=1, source_target_pairs={{0,0},{13,1},{6,2},{11,3},{4,4},{9,5},{2,6},{15,7},{8,8},{5,9},{14... | collective-permute-start | bytes 294920 | tf_op jit(solution)/shard_map/ppermute | solution.py:31
  10.9 9.1 %collective-permute-start = (bf16[64,768]{1,0:T(8,128)(2,1)S(1)}, bf16[64,768]{1,0:T(8,128)(2,1)S(1)}, u32[]{:S(2)}, u32[]{:S(2)}) collective-permute-start(bf16[64,768]{1,0:T(8,128)(2,1)S(1)} %fusion.1.refs_0_), channel_id=1, source_target_pairs={{20,0},{25,1},{18,2},{31,3},{16,4},{29,5},{22,6},{27,7},{28,8},{17... | collective-permute-start | bytes 294920 | tf_op jit(solution)/shard_map/ppermute | solution.py:31
  21.0 1.5 %collective-permute-start.4 = (f32[64,768]{1,0:T(8,128)S(1)}, f32[64,768]{1,0:T(8,128)S(1)}, u32[]{:S(2)}, u32[]{:S(2)}) collective-permute-start(f32[64,768]{1,0:T(8,128)S(1)} %couple.3), channel_id=1, source_target_pairs={{0,1},{1,0},{2,3},{3,2},{4,5},{5,4},{6,7},{7,6},{8,9},{9,8},{10,11... | collective-permute-start | bytes 589832 | tf_op jit(solution)/shard_map/ppermute | solution.py:40
  22.5 7.3 %collective-permute-start.5 = (bf16[64,768]{1,0:T(8,128)(2,1)S(1)}, bf16[64,768]{1,0:T(8,128)(2,1)S(1)}, u32[]{:S(2)}, u32[]{:S(2)}) collective-permute-start(bf16[64,768]{1,0:T(8,128)(2,1)S(1)} %add_convert_fusion.2), channel_id=1, source_target_pairs={{0,2},{1,3},{2,0},{3,1},{4,6},{5,7},{6,4},{7,5},{8,10},{9,11},{10,... | collective-permute-start | bytes 294920 | tf_op jit(solution)/shard_map/ppermute | solution.py:40
  31.1 5.3 %collective-permute-start.6 = (bf16[560,128]{1,0:T(8,128)(2,1)S(1)}, bf16[560,128]{1,0:T(8,128)(2,1)S(1)}, u32[]{:S(2)}, u32[]{:S(2)}) collective-permute-start(bf16[560,128]{1,0:T(8,128)(2,1)S(1)} %dynamic-slice_bitcast_fusion), channel_id=1, source_target_pairs={{0,4},{1,5},{2,6},{3,7},{4,0},{5,1},{6,2},{7,3},{8,12},{9,13},{10,... | collective-permute-start | bytes 430088 | tf_op jit(solution)/shard_map/ppermute | solution.py:40
  36.5 5.2 %collective-permute-start.7 = (bf16[560,128]{1,0:T(8,128)(2,1)S(1)}, bf16[560,128]{1,0:T(8,128)(2,1)S(1)}, u32[]{:S(2)}, u32[]{:S(2)}) collective-permute-start(bf16[560,128]{1,0:T(8,128)(2,1)S(1)} %fusion.3), channel_id=1, source_target_pairs={{0,8},{1,9},{2,10},{3,11},{4,12},{5,13},{6,14},{7,15},{8,0},{9,1},... | collective-permute-start | bytes 430088 | tf_op jit(solution)/shard_map/ppermute | solution.py:40
  41.7 7.0 %collective-permute-start.8 = (bf16[560,128]{1,0:T(8,128)(2,1)S(1)}, bf16[560,128]{1,0:T(8,128)(2,1)S(1)}, u32[]{:S(2)}, u32[]{:S(2)}) collective-permute-start(bf16[560,128]{1,0:T(8,128)(2,1)S(1)} %add_convert_fusion.1), channel_id=1, source_target_pairs={{0,24},{1,25},{2,26},{3,27},{4,28},{5,29},{6,30},{7,31},{8,16},{9,... | collective-permute-start | bytes 430088 | tf_op jit(solution)/shard_map/ppermute | solution.py:40
  48.7 5.2 %collective-permute-start.11 = (bf16[560,128]{1,0:T(8,128)(2,1)S(1)}, bf16[560,128]{1,0:T(8,128)(2,1)S(1)}, u32[]{:S(2)}, u32[]{:S(2)}) collective-permute-start(bf16[560,128]{1,0:T(8,128)(2,1)S(1)} %add_convert_fusion), channel_id=1, source_target_pairs={{0,4},{1,5},{2,6},{3,7},{4,0},{5,1},{6,2},{7,3},{8,12},{9,13},{10,... | collective-permute-start | bytes 430088 | tf_op jit(solution)/shard_map/ppermute | solution.py:40
  50.2 5.1 %collective-permute-start.12 = (bf16[560,128]{1,0:T(8,128)(2,1)S(1)}, bf16[560,128]{1,0:T(8,128)(2,1)S(1)}, u32[]{:S(2)}, u32[]{:S(2)}) collective-permute-start(bf16[560,128]{1,0:T(8,128)(2,1)S(1)} %add_convert_fusion), channel_id=1, source_target_pairs={{0,2},{1,3},{2,0},{3,1},{4,6},{5,7},{6,4},{7,5},{8,10},{9,11},{10,... | collective-permute-start | bytes 430088 | tf_op jit(solution)/shard_map/ppermute | solution.py:40
  55.3 8.7 %collective-permute-start.13 = (bf16[2,560,128]{2,1,0:T(8,128)(2,1)S(1)}, bf16[2,560,128]{2,1,0:T(8,128)(2,1)S(1)}, u32[]{:S(2)}, u32[]{:S(2)}) collective-permute-start(bf16[2,560,128]{2,1,0:T(8,128)(2,1)S(1)} %pad_maximum_fusion.refs_0_), channel_id=1, source_target_pairs={{0,1},{1,0},{2,3},{3,2},{4,5},{5,4},{6,7},{7,6},{8,9},{9,8},{10,11... | collective-permute-start | bytes 860168 | tf_op jit(solution)/shard_map/ppermute | solution.py:40
  55.4 7.1 %collective-permute-start.9 = (bf16[560,128]{1,0:T(8,128)(2,1)S(1)}, bf16[560,128]{1,0:T(8,128)(2,1)S(1)}, u32[]{:S(2)}, u32[]{:S(2)}) collective-permute-start(bf16[560,128]{1,0:T(8,128)(2,1)S(1)} %add_convert_fusion), channel_id=1, source_target_pairs={{0,6},{1,7},{2,4},{3,5},{4,2},{5,3},{6,0},{7,1},{8,14},{9,15},{10,... | collective-permute-start | bytes 430088 | tf_op jit(solution)/shard_map/ppermute | solution.py:40
  57.1 6.1 %collective-permute-start.14 = (bf16[1,560,128]{2,1,0:T(8,128)(2,1)S(1)}, bf16[1,560,128]{2,1,0:T(8,128)(2,1)S(1)}, u32[]{:S(2)}, u32[]{:S(2)}) collective-permute-start(bf16[1,560,128]{2,1,0:T(8,128)(2,1)S(1)} %bitcast.23), channel_id=1, source_target_pairs={{0,1},{1,0},{2,3},{3,2},{4,5},{5,4},{6,7},{7,6},{8,9},{9,8},{10,11... | collective-permute-start | bytes 430088 | tf_op jit(solution)/shard_map/ppermute | solution.py:40
  62.5 2.9 %collective-permute-start.10 = (bf16[1,560,128]{2,1,0:T(8,128)(2,1)S(1)}, bf16[1,560,128]{2,1,0:T(8,128)(2,1)S(1)}, u32[]{:S(2)}, u32[]{:S(2)}) collective-permute-start(bf16[1,560,128]{2,1,0:T(8,128)(2,1)S(1)} %bitcast.25), channel_id=1, source_target_pairs={{0,1},{1,0},{2,3},{3,2},{4,5},{5,4},{6,7},{7,6},{8,9},{9,8},{10,11... | collective-permute-start | bytes 430088 | tf_op jit(solution)/shard_map/ppermute | solution.py:40

commit v7 on v6

--- a/solution.py
+++ b/solution.py
@@ -205,7 +205,8 @@
     for vis_y, vis_pair in zip(scaleds, pairs):
         drift = couple(scaled, pair, vis_y, vis_pair, drift)
 
-    drift = drift + swap(drift, (0, 0), 1, blocks, reps)
+    sent = drift.astype(BF16)
+    drift = sent.astype(F32) + swap(sent, (0, 0), 1, blocks, reps).astype(F32)
     for bit in range(1, bits_of(reps)):
         sent = drift.astype(BF16)
         got = swap(sent, (0, 0), 1 << bit, blocks, reps)
@@ -223,24 +224,26 @@
     hid32 = own_hidden.astype(F32)
     pre_grad = back * (1.0 - hid32 * hid32)
     norm = 1.0 / math.sqrt(npts)
-    term_w_in = lax.dot_general(
-        points, pre_grad.astype(BF16), (((0,), (0,)), ((), ())), preferred_element_type=F32
-    )
+    pre_b16 = pre_grad.astype(BF16)
     term_b_in = jnp.sum(pre_grad, axis=0)
-    term_w_out = lax.dot_general(
-        grad_b16, own_hidden, (((1,), (0,)), ((), ())), preferred_element_type=F32
-    )
-    bias = jnp.broadcast_to(term_b_in[None, None], (2, 16, cols))
-    halves = jnp.concatenate(
-        [term_w_in.reshape(2, din // 2, cols), term_w_out.reshape(2, feat // 2, cols), bias], axis=1
-    )
-    halves = (halves * norm).astype(BF16)
+    bias = jnp.broadcast_to(term_b_in[None], (16, cols))
+
+    def half_of_rows(which):
+        own_points = lax.dynamic_slice_in_dim(points, which * (din // 2), din // 2, 1)
+        own_grad = lax.dynamic_slice_in_dim(grad_b16, which * (feat // 2), feat // 2, 0)
+        term_w_in = lax.dot_general(
+            own_points, pre_b16, (((0,), (0,)), ((), ())), preferred_element_type=F32
+        )
+        term_w_out = lax.dot_general(
+            own_grad, own_hidden, (((1,), (0,)), ((), ())), preferred_element_type=F32
+        )
+        return (jnp.concatenate([term_w_in, term_w_out, bias], axis=0) * norm).astype(BF16)
 
     same = (0, 0)
     side = blk_index & 1
-    kept = lax.dynamic_index_in_dim(halves, side, 0, keepdims=False)
-    sent = lax.dynamic_index_in_dim(halves, 1 - side, 0, keepdims=False)
-    got = swap(sent, (1, 1), 0, blocks, reps)
+    given = half_of_rows(1 - side)
+    got = swap(given, (1, 1), 0, blocks, reps)
+    kept = half_of_rows(side)
     part = (kept.astype(F32) + got.astype(F32)).astype(BF16)
     for bit in range(1, bits_of(blocks)):
         distance = (2 << bit) - 2

time: 66.3 us -> 66 us (level)
  transfers between devices with their start and end apart: 15 -> 15, of which waited for: 9 -> 9; matrix products, arithmetic and copies ran while one was open for 5% -> 6% of each run, Pallas kernels for 5% -> 5%
where the time goes in v7:
time: 66 us; the launch traced here: 65.8 us
  waiting for transfers between devices  31.9 us (48%)
  starting transfers between devices  21.9 us (33%)
  Pallas kernels  6 us (9%)
  matrix products  4.01 us (6%)
  between operations  0.85 us (1%)
  local copies, waits for them, and re-layouts  0.76 us (1%)
    ppermute x11, waiting for transfers between devices, swap(): return lax.ppermute(array, AXES, route)  24 us
    ppermute x11, starting transfers between devices, swap(): return lax.ppermute(array, AXES, route)  15.3 us
    ppermute x4, waiting for transfers between devices, fetch(): return lax.ppermute(array, AXES, route)  7.91 us
    ppermute x4, starting transfers between devices, fetch(): return lax.ppermute(array, AXES, route)  6.62 us
    pallas_call x3, Pallas kernels, place(): pl.pallas_call(lambda *refs: place_kernel(labels, *refs), out_shape=shape...  2.86 us
    dot_general x1, matrix products, on_device(): jnp.dot(points, w_in, preferred_element_type=F32) + b_in  2.21 us
    pallas_call x2, Pallas kernels, couple(): pl.pallas_call(lambda *refs: couple_kernel(chunk, *refs), out_shape=pltpu...  2.07 us
  transfers between devices with their start and end apart: 15, of which 9 were waited for; matrix products, arithmetic and copies ran while one was open for 6% of the time, Pallas kernels for 5%

profile of v7, /device:TPU:0, one launch (start us, length us, event | category | flops | bytes accessed | tf_op | source)
XLA Modules:
  0.0 65.8 jit_solution(4287252942244342463)
XLA Ops:
  0.6 0.0 copy-start
  0.6 1.1 %join.1.refs_1_ = bf16[128,768]{1,0:T(8,128)(2,1)S(1)} custom-call(bf16[64,768]{1,0:T(8,128)(2,1)} %first.1, bf16[64,768]{1,0:T(8,128)(2,1)} %second.1), custom_call_target="tpu_custom_call" | custom-call | tf_op jit(solution)/shard_map/join/pallas_call | solution.py:57
  1.7 0.0 copy-start.1
  1.7 0.0 copy-start.2
  1.8 0.8 %collective-permute-start.3 = (bf16[128,768]{1,0:T(8,128)(2,1)S(1)}, bf16[128,768]{1,0:T(8,128)(2,1)S(1)}, u32[]{:S(2)}, u32[]{:S(2)}) collective-permute-start(bf16[128,768]{1,0:T(8,128)(2,1)S(1)} %join.1.refs_1_), channel_id=1, source_target_pairs={{0,0},{13,1},{6,2},{11,3},{4,4},{9,5},{2,6},{15,7},{8,8},{5,9},{14... | collective-permute-start | bytes 589832 | tf_op jit(solution)/shard_map/ppermute | solution.py:31
  2.6 5.1 %collective-permute-start.1 = (bf16[128,768]{1,0:T(8,128)(2,1)S(1)}, bf16[128,768]{1,0:T(8,128)(2,1)S(1)}, u32[]{:S(2)}, u32[]{:S(2)}) collective-permute-start(bf16[128,768]{1,0:T(8,128)(2,1)S(1)} %join.1.refs_1_), channel_id=1, source_target_pairs={{20,0},{25,1},{18,2},{31,3},{16,4},{29,5},{22,6},{27,7},{28,8},{17... | collective-permute-start | bytes 589832 | tf_op jit(solution)/shard_map/ppermute | solution.py:31
  7.6 0.0 copy-done
  7.6 2.2 %tanh_convert_fusion = bf16[768,512]{1,0:T(8,128)(2,1)S(1)} fusion(bf16[768,1024]{1,0:T(8,128)(2,1)S(1)} %copy-done, bf16[1024,512]{1,0:T(8,128)(2,1)} %param.8, f32[512]{0:T(512)} %param.9), kind=kOutput, calls=%fused_computation | convolution fusion | flops 806092800 | bytes 3409920 | tf_op jit(solution)/shard_map/dot_general | solution.py:191
  9.8 0.0 copy-done.1
  9.9 0.0 copy-done.2
  9.9 0.4 fusion.1.refs_0_
  10.2 0.7 %collective-permute-start.2 = (bf16[64,768]{1,0:T(8,128)(2,1)S(1)}, bf16[64,768]{1,0:T(8,128)(2,1)S(1)}, u32[]{:S(2)}, u32[]{:S(2)}) collective-permute-start(bf16[64,768]{1,0:T(8,128)(2,1)S(1)} %fusion.1.refs_0_), channel_id=1, source_target_pairs={{0,0},{13,1},{6,2},{11,3},{4,4},{9,5},{2,6},{15,7},{8,8},{5,9},{14... | collective-permute-start | bytes 294920 | tf_op jit(solution)/shard_map/ppermute | solution.py:31
  10.9 0.1 collective-permute-start
  11.0 0.0 collective-permute-done.2.refs_2_
  11.0 0.0 collective-permute-done.3.refs_3_
  11.0 1.0 %couple.2.refs_4_ = f32[64,768]{1,0:T(8,128)S(1)} custom-call(bf16[64,768]{1,0:T(8,128)(2,1)S(1)} %fusion.1.refs_0_, bf16[128,768]{1,0:T(8,128)(2,1)S(1)} %join.1.refs_1_, bf16[64,768]{1,0:T(8,128)(2,1)S(1)} %collective-permute-done.2.refs_2_, bf16[128,768]{1,0:T(8,128)(2,1)S(1)} %collective-permute-done.3.refs_3_, f32[64,768]{1,0:T(8,128)S(1)} %broadcast_in_dim.4.refs_4_), custom_call_target="tpu_custom_call" | custom-call | tf_op jit(solution)/shard_map/couple/pallas_call | solution.py:112
  12.1 7.9 %collective-permute-done.refs_2_ = bf16[64,768]{1,0:T(8,128)(2,1)S(1)} collective-permute-done((bf16[64,768]{1,0:T(8,128)(2,1)S(1)}, bf16[64,768]{1,0:T(8,128)(2,1)S(1)}, u32[]{:S(2)}, u32[]{:S(2)}) %collective-permute-start) | collective-permute-done | bytes 98336 | tf_op jit(solution)/shard_map/ppermute | solution.py:31
  20.0 0.0 collective-permute-done.1.refs_3_
  20.0 1.0 %couple.3 = f32[64,768]{1,0:T(8,128)S(1)} custom-call(bf16[64,768]{1,0:T(8,128)(2,1)S(1)} %fusion.1.refs_0_, bf16[128,768]{1,0:T(8,128)(2,1)S(1)} %join.1.refs_1_, bf16[64,768]{1,0:T(8,128)(2,1)S(1)} %collective-permute-done.refs_2_, bf16[128,768]{1,0:T(8,128)(2,1)S(1)} %collective-permute-done.1.refs_3_, f32[64,768]{1,0:T(8,128)S(1)} %couple.2.refs_4_), custom_call_target="tpu_custom_call" | custom-call | tf_op jit(solution)/shard_map/couple/pallas_call | solution.py:112
  21.0 0.3 collective-permute-start.4
  21.3 1.1 %collective-permute-done.4 = bf16[64,768]{1,0:T(8,128)(2,1)S(1)} collective-permute-done((bf16[64,768]{1,0:T(8,128)(2,1)S(1)}, bf16[64,768]{1,0:T(8,128)(2,1)S(1)}, u32[]{:S(2)}, u32[]{:S(2)}) %collective-permute-start.4) | collective-permute-done | bytes 98336 | tf_op jit(solution)/shard_map/ppermute | solution.py:40
  22.4 4.2 %collective-permute-start.5 = (bf16[64,768]{1,0:T(8,128)(2,1)S(1)}, bf16[64,768]{1,0:T(8,128)(2,1)S(1)}, u32[]{:S(2)}, u32[]{:S(2)}) collective-permute-start(bf16[64,768]{1,0:T(8,128)(2,1)S(1)} %add_convert_fusion.3), channel_id=1, source_target_pairs={{0,2},{1,3},{2,0},{3,1},{4,6},{5,7},{6,4},{7,5},{8,10},{9,11},{10,... | collective-permute-start | bytes 294920 | tf_op jit(solution)/shard_map/ppermute | solution.py:40
  26.6 3.1 %collective-permute-done.5 = bf16[64,768]{1,0:T(8,128)(2,1)S(1)} collective-permute-done((bf16[64,768]{1,0:T(8,128)(2,1)S(1)}, bf16[64,768]{1,0:T(8,128)(2,1)S(1)}, u32[]{:S(2)}, u32[]{:S(2)}) %collective-permute-start.5) | collective-permute-done | bytes 98336 | tf_op jit(solution)/shard_map/ppermute | solution.py:40
  29.8 0.1 fusion.24
  29.9 0.3 fusion.25
  30.2 0.2 fusion.10
  30.3 0.4 fusion.2
  30.8 1.5 %collective-permute-start.6 = (bf16[560,128]{1,0:T(8,128)(2,1)S(1)}, bf16[560,128]{1,0:T(8,128)(2,1)S(1)}, u32[]{:S(2)}, u32[]{:S(2)}) collective-permute-start(bf16[560,128]{1,0:T(8,128)(2,1)S(1)} %fusion.9), channel_id=1, source_target_pairs={{0,4},{1,5},{2,6},{3,7},{4,0},{5,1},{6,2},{7,3},{8,12},{9,13},{10,... | collective-permute-start | bytes 430088 | tf_op jit(solution)/shard_map/ppermute | solution.py:40
  32.3 0.4 fusion.4
  32.7 0.2 fusion.12
  32.9 3.2 %collective-permute-done.6 = bf16[560,128]{1,0:T(8,128)(2,1)S(1)} collective-permute-done((bf16[560,128]{1,0:T(8,128)(2,1)S(1)}, bf16[560,128]{1,0:T(8,128)(2,1)S(1)}, u32[]{:S(2)}, u32[]{:S(2)}) %collective-permute-start.6) | collective-permute-done | bytes 143392 | tf_op jit(solution)/shard_map/ppermute | solution.py:40
  36.1 0.8 %collective-permute-start.7 = (bf16[560,128]{1,0:T(8,128)(2,1)S(1)}, bf16[560,128]{1,0:T(8,128)(2,1)S(1)}, u32[]{:S(2)}, u32[]{:S(2)}) collective-permute-start(bf16[560,128]{1,0:T(8,128)(2,1)S(1)} %add_convert_fusion.2), channel_id=1, source_target_pairs={{0,8},{1,9},{2,10},{3,11},{4,12},{5,13},{6,14},{7,15},{8,0},{9,1},... | collective-permute-start | bytes 430088 | tf_op jit(solution)/shard_map/ppermute | solution.py:40
  36.9 4.4 %collective-permute-done.7 = bf16[560,128]{1,0:T(8,128)(2,1)S(1)} collective-permute-done((bf16[560,128]{1,0:T(8,128)(2,1)S(1)}, bf16[560,128]{1,0:T(8,128)(2,1)S(1)}, u32[]{:S(2)}, u32[]{:S(2)}) %collective-permute-start.7) | collective-permute-done | bytes 143392 | tf_op jit(solution)/shard_map/ppermute | solution.py:40
  41.3 3.6 %collective-permute-start.8 = (bf16[560,128]{1,0:T(8,128)(2,1)S(1)}, bf16[560,128]{1,0:T(8,128)(2,1)S(1)}, u32[]{:S(2)}, u32[]{:S(2)}) collective-permute-start(bf16[560,128]{1,0:T(8,128)(2,1)S(1)} %add_convert_fusion.1), channel_id=1, source_target_pairs={{0,24},{1,25},{2,26},{3,27},{4,28},{5,29},{6,30},{7,31},{8,16},{9,... | collective-permute-start | bytes 430088 | tf_op jit(solution)/shard_map/ppermute | solution.py:40
  44.9 3.4 %collective-permute-done.8 = bf16[560,128]{1,0:T(8,128)(2,1)S(1)} collective-permute-done((bf16[560,128]{1,0:T(8,128)(2,1)S(1)}, bf16[560,128]{1,0:T(8,128)(2,1)S(1)}, u32[]{:S(2)}, u32[]{:S(2)}) %collective-permute-start.8) | collective-permute-done | bytes 143392 | tf_op jit(solution)/shard_map/ppermute | solution.py:40
  48.4 1.5 %collective-permute-start.11 = (bf16[560,128]{1,0:T(8,128)(2,1)S(1)}, bf16[560,128]{1,0:T(8,128)(2,1)S(1)}, u32[]{:S(2)}, u32[]{:S(2)}) collective-permute-start(bf16[560,128]{1,0:T(8,128)(2,1)S(1)} %add_convert_fusion), channel_id=1, source_target_pairs={{0,4},{1,5},{2,6},{3,7},{4,0},{5,1},{6,2},{7,3},{8,12},{9,13},{10,... | collective-permute-start | bytes 430088 | tf_op jit(solution)/shard_map/ppermute | solution.py:40
  49.9 1.6 %collective-permute-start.12 = (bf16[560,128]{1,0:T(8,128)(2,1)S(1)}, bf16[560,128]{1,0:T(8,128)(2,1)S(1)}, u32[]{:S(2)}, u32[]{:S(2)}) collective-permute-start(bf16[560,128]{1,0:T(8,128)(2,1)S(1)} %add_convert_fusion), channel_id=1, source_target_pairs={{0,2},{1,3},{2,0},{3,1},{4,6},{5,7},{6,4},{7,5},{8,10},{9,11},{10,... | collective-permute-start | bytes 430088 | tf_op jit(solution)/shard_map/ppermute | solution.py:40
  51.5 2.1 %collective-permute-done.11 = bf16[560,128]{1,0:T(8,128)(2,1)S(1)} collective-permute-done((bf16[560,128]{1,0:T(8,128)(2,1)S(1)}, bf16[560,128]{1,0:T(8,128)(2,1)S(1)}, u32[]{:S(2)}, u32[]{:S(2)}) %collective-permute-start.11) | collective-permute-done | bytes 143392 | tf_op jit(solution)/shard_map/ppermute | solution.py:40
  53.5 1.4 %collective-permute-done.12 = bf16[560,128]{1,0:T(8,128)(2,1)S(1)} collective-permute-done((bf16[560,128]{1,0:T(8,128)(2,1)S(1)}, bf16[560,128]{1,0:T(8,128)(2,1)S(1)}, u32[]{:S(2)}, u32[]{:S(2)}) %collective-permute-start.12) | collective-permute-done | bytes 143392 | tf_op jit(solution)/shard_map/ppermute | solution.py:40
  55.0 0.1 collective-permute-start.13
  55.1 1.7 %collective-permute-start.9 = (bf16[560,128]{1,0:T(8,128)(2,1)S(1)}, bf16[560,128]{1,0:T(8,128)(2,1)S(1)}, u32[]{:S(2)}, u32[]{:S(2)}) collective-permute-start(bf16[560,128]{1,0:T(8,128)(2,1)S(1)} %add_convert_fusion), channel_id=1, source_target_pairs={{0,6},{1,7},{2,4},{3,5},{4,2},{5,3},{6,0},{7,1},{8,14},{9,15},{10,... | collective-permute-start | bytes 430088 | tf_op jit(solution)/shard_map/ppermute | solution.py:40
  56.8 0.2 collective-permute-start.14
  56.9 5.2 %collective-permute-done.9 = bf16[560,128]{1,0:T(8,128)(2,1)S(1)} collective-permute-done((bf16[560,128]{1,0:T(8,128)(2,1)S(1)}, bf16[560,128]{1,0:T(8,128)(2,1)S(1)}, u32[]{:S(2)}, u32[]{:S(2)}) %collective-permute-start.9) | collective-permute-done | bytes 143392 | tf_op jit(solution)/shard_map/ppermute | solution.py:40
  62.1 0.0 collective-permute-start.10
  62.1 0.7 %constant_dynamic-slice_fusion = f32[64,192]{1,0:T(8,128)} fusion(f32[64,768]{1,0:T(8,128)S(1)} %get-tuple-element.23, s32[]{:T(128)S(6)} %select_n.19), kind=kLoop, calls=%fused_computation.35 | loop fusion | bytes 98308 | tf_op jit(solution)/shard_map/dynamic_slice | solution.py:215
  62.9 0.0 collective-permute-done.14.refs_1_
  62.9 0.9 %place.3 = (f32[1024,512]{1,0:T(8,128)}, f32[1,512]{1,0:T(1,128)}, f32[64,512]{1,0:T(8,128)}) custom-call(bf16[1,560,128]{2,1,0:T(8,128)(2,1)S(1)} %bitcast.16, bf16[1,560,128]{2,1,0:T(8,128)(2,1)S(1)} %collective-permute-done.14.refs_1_), custom_call_target="tpu_custom_call" | custom-call | tf_op jit(solution)/shard_map/place/pallas_call | solution.py:162
  63.7 0.0 collective-permute-done.13.refs_1_
  63.8 1.2 %place.4 = (f32[1024,512]{1,0:T(8,128)}, f32[1,512]{1,0:T(1,128)}, f32[64,512]{1,0:T(8,128)}) custom-call(bf16[2,560,128]{2,1,0:T(8,128)(2,1)S(1)} %pad_maximum_fusion.2.refs_0_, bf16[2,560,128]{2,1,0:T(8,128)(2,1)S(1)} %collective-permute-done.13.refs_1_, ...), custom_call_target="tpu_custom_call", output_to_operand_aliasing={{0}: (3, {}), {1}: (4, {}), {2}: (5, {})} | custom-call | tf_op jit(solution)/shard_map/place/pallas_call | solution.py:162
  65.0 0.0 collective-permute-done.10.refs_0_
  65.0 0.8 %place.5 = (f32[1024,512]{1,0:T(8,128)}, f32[1,512]{1,0:T(1,128)}, f32[64,512]{1,0:T(8,128)}) custom-call(bf16[1,560,128]{2,1,0:T(8,128)(2,1)S(1)} %collective-permute-done.10.refs_0_, f32[1024,512]{1,0:T(8,128)} %get-tuple-element.16.refs_1_, f32[1,512]{1,0:T(1,128)} %get-tuple-element.17.refs_2_, ...), custom_call_target="tpu_custom_call", output_to_operand_aliasing={{0}: (1, {}), {1}: (2, {}), {2}: (3, {})} | custom-call | tf_op jit(solution)/shard_map/place/pallas_call | solution.py:162
  (9 shorter events, 0.2 us)
Async XLA Ops:
  0.6 7.0 %copy-start = (bf16[768,1024]{1,0:T(8,128)(2,1)S(1)}, bf16[768,1024]{1,0:T(8,128)(2,1)}, u32[]{:S(2)}) copy-start(bf16[768,1024]{1,0:T(8,128)(2,1)} %param.7) | copy-start | bytes 4718596
  1.7 8.1 %copy-start.1 = (bf16[512,64]{0,1:T(8,128)(2,1)S(1)}, bf16[512,64]{0,1:T(8,128)(2,1)}, u32[]{:S(2)}) copy-start(bf16[512,64]{0,1:T(8,128)(2,1)} %param.10) | copy-start | bytes 196612
  1.7 8.1 %copy-start.2 = (f32[64]{0:T(128)S(1)}, f32[64]{0:T(128)}, u32[]{:S(2)}) copy-start(f32[64]{0:T(128)} %param.11) | copy-start | bytes 772
  1.8 9.2 %collective-permute-start.3 = (bf16[128,768]{1,0:T(8,128)(2,1)S(1)}, bf16[128,768]{1,0:T(8,128)(2,1)S(1)}, u32[]{:S(2)}, u32[]{:S(2)}) collective-permute-start(bf16[128,768]{1,0:T(8,128)(2,1)S(1)} %join.1.refs_1_), channel_id=1, source_target_pairs={{0,0},{13,1},{6,2},{11,3},{4,4},{9,5},{2,6},{15,7},{8,8},{5,9},{14... | collective-permute-start | bytes 589832 | tf_op jit(solution)/shard_map/ppermute | solution.py:31
  2.6 17.4 %collective-permute-start.1 = (bf16[128,768]{1,0:T(8,128)(2,1)S(1)}, bf16[128,768]{1,0:T(8,128)(2,1)S(1)}, u32[]{:S(2)}, u32[]{:S(2)}) collective-permute-start(bf16[128,768]{1,0:T(8,128)(2,1)S(1)} %join.1.refs_1_), channel_id=1, source_target_pairs={{20,0},{25,1},{18,2},{31,3},{16,4},{29,5},{22,6},{27,7},{28,8},{17... | collective-permute-start | bytes 589832 | tf_op jit(solution)/shard_map/ppermute | solution.py:31
  10.2 0.8 %collective-permute-start.2 = (bf16[64,768]{1,0:T(8,128)(2,1)S(1)}, bf16[64,768]{1,0:T(8,128)(2,1)S(1)}, u32[]{:S(2)}, u32[]{:S(2)}) collective-permute-start(bf16[64,768]{1,0:T(8,128)(2,1)S(1)} %fusion.1.refs_0_), channel_id=1, source_target_pairs={{0,0},{13,1},{6,2},{11,3},{4,4},{9,5},{2,6},{15,7},{8,8},{5,9},{14... | collective-permute-start | bytes 294920 | tf_op jit(solution)/shard_map/ppermute | solution.py:31
  10.9 9.1 %collective-permute-start = (bf16[64,768]{1,0:T(8,128)(2,1)S(1)}, bf16[64,768]{1,0:T(8,128)(2,1)S(1)}, u32[]{:S(2)}, u32[]{:S(2)}) collective-permute-start(bf16[64,768]{1,0:T(8,128)(2,1)S(1)} %fusion.1.refs_0_), channel_id=1, source_target_pairs={{20,0},{25,1},{18,2},{31,3},{16,4},{29,5},{22,6},{27,7},{28,8},{17... | collective-permute-start | bytes 294920 | tf_op jit(solution)/shard_map/ppermute | solution.py:31
  21.0 1.4 %collective-permute-start.4 = (bf16[64,768]{1,0:T(8,128)(2,1)S(1)}, bf16[64,768]{1,0:T(8,128)(2,1)S(1)}, u32[]{:S(2)}, u32[]{:S(2)}) collective-permute-start(bf16[64,768]{1,0:T(8,128)(2,1)S(1)} %convert_element_type.71), channel_id=1, source_target_pairs={{0,1},{1,0},{2,3},{3,2},{4,5},{5,4},{6,7},{7,6},{8,9},{9,8},{10,11... | collective-permute-start | bytes 294920 | tf_op jit(solution)/shard_map/ppermute | solution.py:40
  22.4 7.3 %collective-permute-start.5 = (bf16[64,768]{1,0:T(8,128)(2,1)S(1)}, bf16[64,768]{1,0:T(8,128)(2,1)S(1)}, u32[]{:S(2)}, u32[]{:S(2)}) collective-permute-start(bf16[64,768]{1,0:T(8,128)(2,1)S(1)} %add_convert_fusion.3), channel_id=1, source_target_pairs={{0,2},{1,3},{2,0},{3,1},{4,6},{5,7},{6,4},{7,5},{8,10},{9,11},{10,... | collective-permute-start | bytes 294920 | tf_op jit(solution)/shard_map/ppermute | solution.py:40
  30.8 5.3 %collective-permute-start.6 = (bf16[560,128]{1,0:T(8,128)(2,1)S(1)}, bf16[560,128]{1,0:T(8,128)(2,1)S(1)}, u32[]{:S(2)}, u32[]{:S(2)}) collective-permute-start(bf16[560,128]{1,0:T(8,128)(2,1)S(1)} %fusion.9), channel_id=1, source_target_pairs={{0,4},{1,5},{2,6},{3,7},{4,0},{5,1},{6,2},{7,3},{8,12},{9,13},{10,... | collective-permute-start | bytes 430088 | tf_op jit(solution)/shard_map/ppermute | solution.py:40
  36.1 5.2 %collective-permute-start.7 = (bf16[560,128]{1,0:T(8,128)(2,1)S(1)}, bf16[560,128]{1,0:T(8,128)(2,1)S(1)}, u32[]{:S(2)}, u32[]{:S(2)}) collective-permute-start(bf16[560,128]{1,0:T(8,128)(2,1)S(1)} %add_convert_fusion.2), channel_id=1, source_target_pairs={{0,8},{1,9},{2,10},{3,11},{4,12},{5,13},{6,14},{7,15},{8,0},{9,1},... | collective-permute-start | bytes 430088 | tf_op jit(solution)/shard_map/ppermute | solution.py:40
  41.3 7.0 %collective-permute-start.8 = (bf16[560,128]{1,0:T(8,128)(2,1)S(1)}, bf16[560,128]{1,0:T(8,128)(2,1)S(1)}, u32[]{:S(2)}, u32[]{:S(2)}) collective-permute-start(bf16[560,128]{1,0:T(8,128)(2,1)S(1)} %add_convert_fusion.1), channel_id=1, source_target_pairs={{0,24},{1,25},{2,26},{3,27},{4,28},{5,29},{6,30},{7,31},{8,16},{9,... | collective-permute-start | bytes 430088 | tf_op jit(solution)/shard_map/ppermute | solution.py:40
  48.4 5.2 %collective-permute-start.11 = (bf16[560,128]{1,0:T(8,128)(2,1)S(1)}, bf16[560,128]{1,0:T(8,128)(2,1)S(1)}, u32[]{:S(2)}, u32[]{:S(2)}) collective-permute-start(bf16[560,128]{1,0:T(8,128)(2,1)S(1)} %add_convert_fusion), channel_id=1, source_target_pairs={{0,4},{1,5},{2,6},{3,7},{4,0},{5,1},{6,2},{7,3},{8,12},{9,13},{10,... | collective-permute-start | bytes 430088 | tf_op jit(solution)/shard_map/ppermute | solution.py:40
  49.9 5.1 %collective-permute-start.12 = (bf16[560,128]{1,0:T(8,128)(2,1)S(1)}, bf16[560,128]{1,0:T(8,128)(2,1)S(1)}, u32[]{:S(2)}, u32[]{:S(2)}) collective-permute-start(bf16[560,128]{1,0:T(8,128)(2,1)S(1)} %add_convert_fusion), channel_id=1, source_target_pairs={{0,2},{1,3},{2,0},{3,1},{4,6},{5,7},{6,4},{7,5},{8,10},{9,11},{10,... | collective-permute-start | bytes 430088 | tf_op jit(solution)/shard_map/ppermute | solution.py:40
  55.0 8.7 %collective-permute-start.13 = (bf16[2,560,128]{2,1,0:T(8,128)(2,1)S(1)}, bf16[2,560,128]{2,1,0:T(8,128)(2,1)S(1)}, u32[]{:S(2)}, u32[]{:S(2)}) collective-permute-start(bf16[2,560,128]{2,1,0:T(8,128)(2,1)S(1)} %pad_maximum_fusion.2.refs_0_), channel_id=1, source_target_pairs={{0,1},{1,0},{2,3},{3,2},{4,5},{5,4},{6,7},{7,6},{8,9},{9,8},{10,11... | collective-permute-start | bytes 860168 | tf_op jit(solution)/shard_map/ppermute | solution.py:40
  55.1 7.1 %collective-permute-start.9 = (bf16[560,128]{1,0:T(8,128)(2,1)S(1)}, bf16[560,128]{1,0:T(8,128)(2,1)S(1)}, u32[]{:S(2)}, u32[]{:S(2)}) collective-permute-start(bf16[560,128]{1,0:T(8,128)(2,1)S(1)} %add_convert_fusion), channel_id=1, source_target_pairs={{0,6},{1,7},{2,4},{3,5},{4,2},{5,3},{6,0},{7,1},{8,14},{9,15},{10,... | collective-permute-start | bytes 430088 | tf_op jit(solution)/shard_map/ppermute | solution.py:40
  56.8 6.1 %collective-permute-start.14 = (bf16[1,560,128]{2,1,0:T(8,128)(2,1)S(1)}, bf16[1,560,128]{2,1,0:T(8,128)(2,1)S(1)}, u32[]{:S(2)}, u32[]{:S(2)}) collective-permute-start(bf16[1,560,128]{2,1,0:T(8,128)(2,1)S(1)} %bitcast.15), channel_id=1, source_target_pairs={{0,1},{1,0},{2,3},{3,2},{4,5},{5,4},{6,7},{7,6},{8,9},{9,8},{10,11... | collective-permute-start | bytes 430088 | tf_op jit(solution)/shard_map/ppermute | solution.py:40
  62.1 2.9 %collective-permute-start.10 = (bf16[1,560,128]{2,1,0:T(8,128)(2,1)S(1)}, bf16[1,560,128]{2,1,0:T(8,128)(2,1)S(1)}, u32[]{:S(2)}, u32[]{:S(2)}) collective-permute-start(bf16[1,560,128]{2,1,0:T(8,128)(2,1)S(1)} %bitcast.17), channel_id=1, source_target_pairs={{0,1},{1,0},{2,3},{3,2},{4,5},{5,4},{6,7},{7,6},{8,9},{9,8},{10,11... | collective-permute-start | bytes 430088 | tf_op jit(solution)/shard_map/ppermute | solution.py:40
